TPU v7x, 512 devices: a whole 4x4x16 slice. The times are simulated.
512 devices in a mesh: wide: 32 (over z, y_hi), narrow: 16 (over x, y_lo, core).
Axes of the slice: x: 4, y: 4 (y_hi: 2, y_lo: 2; y = y_hi * 2 + y_lo), z: 16, core: 2. Of those that a mesh axis runs over, the one named last changes fastest.
Arguments:
- embed: bfloat16 [393216, 1024], P(('wide', 'narrow')), may hold values from -6 to 6
- dest: int32 [393216], P(('wide', 'narrow')), may hold values from 0 to 15, as said below
- means: bfloat16 [4096, 1024], P('narrow'), may hold values from -3 to 3
- variances: bfloat16 [4096, 1024], P('narrow'), may hold values from 0.5 to 2
Outputs:
- new_means: float32 [4096, 1024], P('narrow')
- new_variances: float32 [4096, 1024], P('narrow')
Inputs may be any that keep to these rules, and one draw needn't show every extreme that they name: `dest`: among the rows of one device, each group number appears exactly 768 / 16 times.
All inputs are finite; a program needn't handle non-finite values.
Results may differ from a plain program's by a relative error of at most 0.00045.
The roundings to bfloat16 on the way count: a program that leaves them out, or rounds other values in their place, can miss the bound.
Values may be sent and summed in bfloat16 or wider, within the bound.
No kernel may reach another device: no remote copies, remote signals or barrier semaphores. Data moves between devices by JAX's collectives and lax.ppermute only.
A program may use at most 64 MiB of HBM per device.

v0:
```python
import jax
import jax.numpy as jnp
from jax import lax
from jax.sharding import PartitionSpec as P

SINK = 3


def score_rows(rows, mean_block, var_block):
    prec = 1.0 / var_block.astype(jnp.float32)
    mean_wide = mean_block.astype(jnp.float32)
    quad = (-0.5 * prec).astype(jnp.bfloat16)
    linear = (mean_wide * prec).astype(jnp.bfloat16)
    offset = -0.5 * jnp.sum(
        jnp.log(var_block.astype(jnp.float32)) + mean_wide * mean_wide * prec, axis=1
    )
    squared = (rows.astype(jnp.float32) * rows.astype(jnp.float32)).astype(jnp.bfloat16)
    stacked = jnp.concatenate([squared, rows], axis=1)
    weights = jnp.concatenate([quad, linear], axis=1)
    raw = lax.dot_general(
        stacked, weights, (((1,), (1,)), ((), ())), preferred_element_type=jnp.float32
    )
    scale = rows.shape[1] ** (-0.5)
    return scale * (raw + offset[None, :])


def finish(total, first, second):
    new_mean = first / total[:, None]
    new_var = second / total[:, None] - new_mean * new_mean + 0.01
    return (new_mean, new_var)


def on_device(embed, dest, means, variances):
    rows_dev, width = embed.shape
    groups = lax.axis_size("narrow")
    block = rows_dev // groups
    comp = means.shape[0]
    order = jnp.argsort(dest, stable=True)
    ordered = embed[order].reshape(groups, block, width)
    arrived = lax.all_to_all(ordered, "narrow", split_axis=0, concat_axis=0, tiled=True).reshape(
        rows_dev, width
    )
    score = score_rows(arrived, means, variances)
    resp = jax.nn.softmax(score, axis=1)
    target = jnp.float32(rows_dev * lax.axis_size("wide") / comp)
    for step in range(SINK):
        mass = lax.psum(jnp.sum(resp, axis=0), "wide")
        scaled = resp * (target / mass)[None, :]
        resp = scaled / jnp.sum(scaled, axis=1, keepdims=True)
    values = arrived.astype(jnp.float32)
    first = lax.dot_general(
        resp,
        values,
        (((0,), (0,)), ((), ())),
        precision=lax.Precision.HIGHEST,
        preferred_element_type=jnp.float32,
    )
    second = lax.dot_general(
        resp,
        values * values,
        (((0,), (0,)), ((), ())),
        precision=lax.Precision.HIGHEST,
        preferred_element_type=jnp.float32,
    )
    total = jnp.sum(resp, axis=0)
    total, first, second = lax.psum((total, first, second), "wide")
    new_mean, new_var = finish(total, first, second)
    return (new_mean, new_var)


def solution(mesh):
    return jax.shard_map(
        on_device,
        mesh=mesh,
        in_specs=(
            P(("wide", "narrow"), None),
            P(("wide", "narrow")),
            P("narrow", None),
            P("narrow", None),
        ),
        out_specs=(P("narrow", None), P("narrow", None)),
        check_vma=False,
    )
```

profile of v0, /device:TPU:24, one launch (start us, length us, event | category | flops | bytes accessed | tf_op | source)
XLA Modules:
  0.0 604.0 jit_solution(7852464779374893760)
XLA Ops:
  7.2 0.0 copy-start
  7.2 5.2 sort.17
  12.4 0.0 copy-done
  12.4 3.6 gather_fusion
  16.0 5.8 all-to-all-start
  21.7 0.0 all-reduce.3.cloned.1.call-start
  21.8 2.6 fusion.13
  24.4 18.6 %all-to-all-done = bf16[16,48,1024]{2,1,0:T(8,128)(2,1)S(1)} async-done(((bf16[16,48,1024]{2,1,0:T(8,128)(2,1)}), bf16[16,48,1024]{2,1,0:T(8,128)(2,1)S(1)}, u32[]{:S(2)}, u32[]{:S(2)}) %all-to-all-start) | async-done | bytes 1572896 | tf_op jit(solution)/shard_map/all_to_all | solution.py:40
  43.0 0.5 fusion.5
  43.4 0.7 copy-done.1
  44.1 0.2 copy-done.3
  44.4 0.4 copy-done.4
  44.7 2.4 fusion.27
  47.2 0.1 fusion.20
  47.3 0.2 fusion.22
  47.5 80.0 %psum.42 = f32[256]{0:T(256)S(1)} all-reduce(f32[256]{0:T(256)S(1)} %fusion.22), channel_id=1, replica_groups=mesh['wide'=32,'narrow'=16] {'wide'}, use_global_device_ids=true, to_apply=%region_5.6 | all-reduce | flops 256 | bytes 2048 | tf_op jit(solution)/shard_map/psum | solution.py:47
  127.6 0.2 multiply_reduce_fusion.2
  127.7 0.3 fusion.26
  128.0 76.4 %psum.43 = f32[256]{0:T(256)S(1)} all-reduce(f32[256]{0:T(256)S(1)} %get-tuple-element.10), channel_id=1, replica_groups=mesh['wide'=32,'narrow'=16] {'wide'}, use_global_device_ids=true, to_apply=%region_8.9 | all-reduce | flops 256 | bytes 2048 | tf_op jit(solution)/shard_map/psum | solution.py:47
  204.4 0.1 multiply_reduce_fusion.1
  204.5 0.2 fusion.25
  204.8 72.0 %psum.44 = f32[256]{0:T(256)S(1)} all-reduce(f32[256]{0:T(256)S(1)} %get-tuple-element.8), channel_id=1, replica_groups=mesh['wide'=32,'narrow'=16] {'wide'}, use_global_device_ids=true, to_apply=%region_11.12 | all-reduce | flops 256 | bytes 2048 | tf_op jit(solution)/shard_map/psum | solution.py:47
  276.8 0.1 multiply_reduce_fusion
  276.9 0.0 copy-start.2
  276.9 5.4 fusion.4
  282.3 0.0 copy-done.2
  282.3 2.5 fusion.24
  284.8 0.0 all-reduce.3.cloned.1.call-update
  284.8 0.2 fusion.23
  285.0 75.8 %psum.46 = f32[256]{0:T(256)S(1)} all-reduce(f32[256]{0:T(256)S(1)} %fusion.23), channel_id=1, replica_groups=mesh['wide'=32,'narrow'=16] {'wide'}, use_global_device_ids=true, to_apply=%region_15.16 | all-reduce | flops 256 | bytes 2048 | tf_op jit(solution)/shard_map/psum | solution.py:66
  360.8 233.0 %all-reduce.3.cloned.1.call-done = (f32[256,1024]{1,0:T(8,128)}, f32[256,1024]{1,0:T(8,128)}) async-done(((f32[256,1024]{1,0:T(8,128)}, f32[256,1024]{1,0:T(8,128)}), (f32[256,1024]{1,0:T(8,128)}, f32[256,1024]{1,0:T(8,128)})) %all-reduce.3.cloned.1.call-update) | async-done | bytes 2097168 | tf_op jit(solution)/shard_map/psum | solution.py:66
  593.8 3.3 subtract_add_fusion
  (10 shorter events, 0.0 us)
Async XLA Ops:
  7.2 5.2 copy-start
  16.0 27.0 %all-to-all-start = ((bf16[16,48,1024]{2,1,0:T(8,128)(2,1)}), bf16[16,48,1024]{2,1,0:T(8,128)(2,1)S(1)}, u32[]{:S(2)}, u32[]{:S(2)}) async-start(bf16[16,48,1024]{2,1,0:T(8,128)(2,1)} %bitcast.7), calls=%async_computation | async-start | bytes 3145728 | tf_op jit(solution)/shard_map/all_to_all | solution.py:40
  21.7 572.1 %all-reduce.3.cloned.1.call-start = ((), (), s32[]{:S(2)}) async-start(), calls=%async_computation.1 | async-start | bytes 4194304 | tf_op jit(solution)/shard_map/psum | solution.py:66
  43.0 1.2 copy-start.1
  43.0 1.4 copy-start.3
  43.0 1.8 copy-start.4
  276.9 5.4 copy-start.2
Sparse Core Ops, SparseCore 0:
  284.9 308.8 all-reduce.2
where the time goes:
time: 607 us; the launch traced here: 604 us
  blocking collectives  304 us (50%)
  waiting for transfers between devices  252 us (42%)
  between operations  14.1 us (2%)
  other arithmetic  13.1 us (2%)
  matrix products  10.3 us (2%)
    psum x1, waiting for transfers between devices, on_device(): total, first, second = lax.psum((total, first, second), 'wide')  233 us
    psum x3, blocking collectives, on_device(): mass = lax.psum(jnp.sum(resp, axis=0), 'wide')  228 us
    psum x1, blocking collectives, on_device(): total, first, second = lax.psum((total, first, second), 'wide')  75.8 us
    all_to_all x1, waiting for transfers between devices, on_device(): lax.all_to_all(ordered, 'narrow', split_axis=0, concat_axis=0, tiled=True)  18.6 us
  transfers between devices with their start and end apart: 2, of which 2 were waited for; matrix products, arithmetic and copies ran while one was open for 0% of the time, Pallas kernels for 0%

commit v1 on v0

--- a/solution.py
+++ b/solution.py
@@ -4,6 +4,7 @@
 from jax.sharding import PartitionSpec as P
 
 SINK = 3
+PAD = 128
 
 
 def score_rows(rows, mean_block, var_block):
@@ -24,17 +25,35 @@
     return scale * (raw + offset[None, :])
 
 
-def finish(total, first, second):
-    new_mean = first / total[:, None]
-    new_var = second / total[:, None] - new_mean * new_mean + 0.01
-    return (new_mean, new_var)
+def sum_small(part, members):
+    block = part.reshape(1, -1, 128)
+    sent = jnp.broadcast_to(block, (members,) + block.shape[1:])
+    got = lax.all_to_all(sent, "wide", split_axis=0, concat_axis=0, tiled=True)
+    return jnp.sum(got, axis=0).reshape(part.shape)
+
+
+def with_total(values, total):
+    high = lax.reduce_precision(total, 5, 10)
+    low = total - high
+    lane = lax.broadcasted_iota(jnp.int32, (values.shape[0], PAD), 1)
+    tail = jnp.where(lane < PAD // 2, high[:, None], low[:, None])
+    return jnp.concatenate([values, tail], axis=1).astype(jnp.float16)
+
+
+def split_total(payload):
+    moments = payload.shape[1] - PAD
+    return payload[:, :moments], payload[:, moments] + payload[:, moments + PAD // 2]
 
 
 def on_device(embed, dest, means, variances):
     rows_dev, width = embed.shape
     groups = lax.axis_size("narrow")
+    members = lax.axis_size("wide")
     block = rows_dev // groups
     comp = means.shape[0]
+    deep = members // 2
+    pairs = [[2 * z, 2 * z + 1] for z in range(deep)]
+    lines = [[2 * z + y for z in range(deep)] for y in range(2)]
     order = jnp.argsort(dest, stable=True)
     ordered = embed[order].reshape(groups, block, width)
     arrived = lax.all_to_all(ordered, "narrow", split_axis=0, concat_axis=0, tiled=True).reshape(
@@ -42,30 +61,44 @@
     )
     score = score_rows(arrived, means, variances)
     resp = jax.nn.softmax(score, axis=1)
-    target = jnp.float32(rows_dev * lax.axis_size("wide") / comp)
+    target = jnp.float32(rows_dev * members / comp)
     for step in range(SINK):
-        mass = lax.psum(jnp.sum(resp, axis=0), "wide")
+        mass = sum_small(jnp.sum(resp, axis=0), members)
         scaled = resp * (target / mass)[None, :]
         resp = scaled / jnp.sum(scaled, axis=1, keepdims=True)
     values = arrived.astype(jnp.float32)
-    first = lax.dot_general(
+    both = jnp.concatenate([values, values * values], axis=1)
+    sums = lax.dot_general(
         resp,
-        values,
+        both,
         (((0,), (0,)), ((), ())),
         precision=lax.Precision.HIGHEST,
         preferred_element_type=jnp.float32,
     )
-    second = lax.dot_general(
-        resp,
-        values * values,
-        (((0,), (0,)), ((), ())),
-        precision=lax.Precision.HIGHEST,
-        preferred_element_type=jnp.float32,
+    sent = with_total(sums, jnp.sum(resp, axis=0)).reshape(2, comp // 2, 2 * width + PAD)
+    got = lax.all_to_all(
+        sent, "wide", split_axis=0, concat_axis=0, tiled=True, axis_index_groups=pairs
     )
-    total = jnp.sum(resp, axis=0)
-    total, first, second = lax.psum((total, first, second), "wide")
-    new_mean, new_var = finish(total, first, second)
-    return (new_mean, new_var)
+    sums, total = split_total(jnp.sum(got.astype(jnp.float32), axis=0))
+    sent = with_total(sums, total).reshape(deep, comp // members, 2 * width + PAD)
+    got = lax.all_to_all(
+        sent, "wide", split_axis=0, concat_axis=0, tiled=True, axis_index_groups=lines
+    )
+    sums, total = split_total(jnp.sum(got.astype(jnp.float32), axis=0))
+    new_mean = sums[:, :width] / total[:, None]
+    new_var = sums[:, width:] / total[:, None] - new_mean * new_mean + 0.01
+    mine = jnp.concatenate([new_mean, new_var], axis=1).astype(jnp.float16)
+    sent = jnp.broadcast_to(mine[None], (deep,) + mine.shape)
+    got = lax.all_to_all(
+        sent, "wide", split_axis=0, concat_axis=0, tiled=True, axis_index_groups=lines
+    )
+    half = got.reshape(1, comp // 2, 2 * width)
+    sent = jnp.broadcast_to(half, (2,) + half.shape[1:])
+    got = lax.all_to_all(
+        sent, "wide", split_axis=0, concat_axis=0, tiled=True, axis_index_groups=pairs
+    )
+    out = got.reshape(comp, 2 * width).astype(jnp.float32)
+    return (out[:, :width], out[:, width:])
 
 
 def solution(mesh):

time: 607 us -> 225 us (0.37)
  waiting for transfers between devices: 252 us -> 41.6 us
  blocking collectives: 304 us -> 120 us
  between operations: 14.1 us -> 0.82 us
  starting transfers between devices: 5.81 us -> 18 us
  other arithmetic: 13.1 us -> 24.1 us
    psum x4 -> x0, blocking collectives: 304 us -> none  [the longest x3 228 us: on_device(): mass = lax.psum(jnp.sum(resp, axis=0), 'wide')]
    psum x1 -> x0, waiting for transfers between devices: 233 us -> none  [on_device(): total, first, second = lax.psum((total, first, second), 'wide')]
    all_to_all x0 -> x5, blocking collectives: none -> 120 us  [the longest x4 89.8 us: on_device(): lax.all_to_all(sent, 'wide', split_axis=0, concat_axis=0, tiled=True, axi...]
    all_to_all x0 -> x2, waiting for transfers between devices: none -> 23 us  [sum_small(): got = lax.all_to_all(sent, 'wide', split_axis=0, concat_axis=0, tiled=True)]
    all_to_all x0 -> x2, starting transfers between devices: none -> 12.3 us  [sum_small(): got = lax.all_to_all(sent, 'wide', split_axis=0, concat_axis=0, tiled=True)]
  transfers between devices with their start and end apart: 2 -> 3, of which waited for: 2 -> 3; matrix products, arithmetic and copies ran while one was open for 0% -> 2% of each run, Pallas kernels for 0% -> 0%
where the time goes in v1:
time: 225 us; the launch traced here: 222 us
  blocking collectives  120 us (53%)
  waiting for transfers between devices  41.6 us (18%)
  other arithmetic  24.1 us (11%)
  starting transfers between devices  18 us (8%)
  matrix products  9.56 us (4%)
  local copies, waits for them, and re-layouts  7.39 us (3%)
    all_to_all x4, blocking collectives, on_device(): lax.all_to_all(sent, 'wide', split_axis=0, concat_axis=0, tiled=True, axi...  89.8 us
    all_to_all x1, blocking collectives, sum_small(): got = lax.all_to_all(sent, 'wide', split_axis=0, concat_axis=0, tiled=True)  30.5 us
    all_to_all x2, waiting for transfers between devices, sum_small(): got = lax.all_to_all(sent, 'wide', split_axis=0, concat_axis=0, tiled=True)  23 us
    all_to_all x1, waiting for transfers between devices, on_device(): lax.all_to_all(ordered, 'narrow', split_axis=0, concat_axis=0, tiled=True)  18.7 us
    all_to_all x2, starting transfers between devices, sum_small(): got = lax.all_to_all(sent, 'wide', split_axis=0, concat_axis=0, tiled=True)  12.3 us
    dot_general x1, matrix products, on_device(): lax.dot_general(resp, both, (((0,), (0,)), ((), ())), precision=lax.Preci...  8.52 us
    all_to_all x1, starting transfers between devices, on_device(): lax.all_to_all(ordered, 'narrow', split_axis=0, concat_axis=0, tiled=True)  5.77 us
    sort x1, other arithmetic, on_device(): order = jnp.argsort(dest, stable=True)  5.17 us
  transfers between devices with their start and end apart: 3, of which 3 were waited for; matrix products, arithmetic and copies ran while one was open for 2% of the time, Pallas kernels for 0%

profile of v1, /device:TPU:24, one launch (start us, length us, event | category | flops | bytes accessed | tf_op | source)
XLA Modules:
  0.0 221.9 jit_solution(9072210614422996507)
XLA Ops:
  0.7 5.2 %sort.17 = (s32[768]{0:T(1024)}, s32[768]{0:T(1024)S(1)}) sort(s32[768]{0:T(1024)} %param.5, s32[768]{0:T(1024)S(1)} %iota.16), dimensions={0}, to_apply=%region_0.0 | sort | flops 7680 | bytes 12288 | tf_op jit(solution)/shard_map/jit(argsort)/sort | solution.py:57
  5.8 3.6 %gather_fusion = bf16[768,1024]{1,0:T(8,128)(2,1)} fusion(bf16[768,1024]{1,0:T(8,128)(2,1)S(1)} %copy-done, s32[1024]{0:T(1024)S(1)} %pad_clamp_fusion), kind=kCustom, calls=%fused_computation | custom fusion | bytes 3148800 | tf_op jit(solution)/shard_map/gather | solution.py:58
  9.4 5.8 %all-to-all-start = ((bf16[16,48,1024]{2,1,0:T(8,128)(2,1)}), bf16[16,48,1024]{2,1,0:T(8,128)(2,1)S(1)}, u32[]{:S(2)}, u32[]{:S(2)}) async-start(bf16[16,48,1024]{2,1,0:T(8,128)(2,1)} %bitcast.27), calls=%async_computation | async-start | bytes 3145728 | tf_op jit(solution)/shard_map/all_to_all | solution.py:59
  15.2 2.6 %fusion.18 = (f32[256]{0:T(256)S(1)}, bf16[256,1024]{1,0:T(8,128)(2,1)}, bf16[256,1024]{1,0:T(8,128)(2,1)}) fusion(bf16[256,1024]{1,0:T(8,128)(2,1)} %param.7, bf16[256,1024]{1,0:T(8,128)(2,1)} %param.6), kind=kLoop, calls=%fused_computation.20 | loop fusion | flops 2883328 | bytes 2098176 | tf_op jit(solution)/shard_map/reduce_sum | solution.py:15
  17.8 18.7 %all-to-all-done = bf16[16,48,1024]{2,1,0:T(8,128)(2,1)S(1)} async-done(((bf16[16,48,1024]{2,1,0:T(8,128)(2,1)}), bf16[16,48,1024]{2,1,0:T(8,128)(2,1)S(1)}, u32[]{:S(2)}, u32[]{:S(2)}) %all-to-all-start) | async-done | bytes 1572896 | tf_op jit(solution)/shard_map/all_to_all | solution.py:59
  36.4 2.3 %convert_multiply_fusion.2 = (f32[768,1024]{1,0:T(8,128)}, bf16[768,1024]{1,0:T(8,128)(2,1)S(1)}) fusion(bf16[16,48,1024]{2,1,0:T(8,128)(2,1)S(1)} %all-to-all-done), kind=kLoop, calls=%fused_computation.30 | loop fusion | flops 2359296 | bytes 6291456 | tf_op jit(solution)/shard_map/mul | solution.py:18
  38.8 1.0 fusion.41
  40.0 0.7 copy-done.1
  40.7 0.2 fusion.37
  40.9 30.5 %all_to_all.40 = f32[32,2,128]{2,1,0:T(2,128)S(1)} all-to-all(f32[32,2,128]{2,1,0:T(2,128)S(1)} %broadcast_in_dim.90), channel_id=1, replica_groups=mesh['wide'=32,'narrow'=16] {'wide'}, dimensions={0} | all-to-all | bytes 65536 | tf_op jit(solution)/shard_map/all_to_all | solution.py:31
  71.5 1.3 multiply_reduce_fusion.2
  72.8 2.2 fusion.39
  75.0 0.6 broadcast_in_dim.92
  75.7 6.1 %all-to-all-start.2 = ((f32[32,2,128]{2,1,0:T(2,128)}), f32[32,2,128]{2,1,0:T(2,128)S(1)}, u32[]{:S(2)}, u32[]{:S(2)}) async-start(f32[32,2,128]{2,1,0:T(2,128)} %broadcast_in_dim.92), calls=%async_computation.2 | async-start | bytes 65536 | tf_op jit(solution)/shard_map/all_to_all | solution.py:31
  81.8 12.6 %all-to-all-done.2 = f32[32,2,128]{2,1,0:T(2,128)S(1)} async-done(((f32[32,2,128]{2,1,0:T(2,128)}), f32[32,2,128]{2,1,0:T(2,128)S(1)}, u32[]{:S(2)}, u32[]{:S(2)}) %all-to-all-start.2) | async-done | bytes 32800 | tf_op jit(solution)/shard_map/all_to_all | solution.py:31
  94.4 1.3 multiply_reduce_fusion.1
  95.7 2.2 fusion.38
  97.8 0.6 broadcast_in_dim.94
  98.5 6.2 %all-to-all-start.3 = ((f32[32,2,128]{2,1,0:T(2,128)}), f32[32,2,128]{2,1,0:T(2,128)S(1)}, u32[]{:S(2)}, u32[]{:S(2)}) async-start(f32[32,2,128]{2,1,0:T(2,128)} %broadcast_in_dim.94), calls=%async_computation.3 | async-start | bytes 65536 | tf_op jit(solution)/shard_map/all_to_all | solution.py:31
  104.6 2.2 bitcast_convert_fusion.1
  106.8 10.4 %all-to-all-done.3 = f32[32,2,128]{2,1,0:T(2,128)S(1)} async-done(((f32[32,2,128]{2,1,0:T(2,128)}), f32[32,2,128]{2,1,0:T(2,128)S(1)}, u32[]{:S(2)}, u32[]{:S(2)}) %all-to-all-start.3) | async-done | bytes 32800 | tf_op jit(solution)/shard_map/all_to_all | solution.py:31
  117.3 1.3 multiply_reduce_fusion
  118.5 1.4 fusion.28
  119.9 8.5 %fusion.8 = f16[256,2048]{1,0:T(8,128)(2,1)S(1)} fusion(f32[768,1024]{1,0:T(8,128)} %get-tuple-element.12, f32[768,1024]{1,0:T(8,128)} %bitcast_convert_fusion.1, f32[768,256]{0,1:T(8,128)} %get-tuple-element.7, f32[768]{0:T(1024)S(1)} %multiply_reduce_fusion, f32[256]{0:T(256)S(1)} %divide_bitcast_fusion), kind=kOutput, calls=%fused_computation.9 | convolution fusion | flops 4834328576 | bytes 8130560 | tf_op jit(solution)/shard_map/dot_general | solution.py:71
  128.6 0.3 pad_maximum_fusion
  128.9 14.6 %all_to_all.41 = f16[2,128,2176]{2,1,0:T(8,128)(2,1)S(1)} all-to-all(f16[2,128,2176]{2,1,0:T(8,128)(2,1)S(1)} %pad_maximum_fusion), channel_id=1, replica_groups={{0,16},{32,48},{64,80},{96,112},{128,144},{160,176},{192,208},{224,240}..., dimensions={0} | all-to-all | bytes 2228224 | tf_op jit(solution)/shard_map/all_to_all | solution.py:79
  143.7 0.2 reduce-precision_reduce_fusion
  144.4 33.2 %all_to_all.42 = f16[16,8,2176]{2,1,0:T(8,128)(2,1)S(1)} all-to-all(f16[16,8,2176]{2,1,0:T(8,128)(2,1)S(1)} %pad_maximum_fusion.1), channel_id=1, replica_groups={{0,32,64,96,128,160,192,224,256,288,320,352,384,416,448,480},{16,48,80,..., dimensions={0} | all-to-all | bytes 1114112 | tf_op jit(solution)/shard_map/all_to_all | solution.py:84
  178.0 29.3 %all_to_all.43 = f16[16,8,2048]{2,1,0:T(8,128)(2,1)S(1)} all-to-all(f16[16,8,2048]{2,1,0:T(8,128)(2,1)S(1)} %broadcast_in_dim.101), channel_id=1, replica_groups={{0,32,64,96,128,160,192,224,256,288,320,352,384,416,448,480},{16,48,80,..., dimensions={0} | all-to-all | bytes 1048576 | tf_op jit(solution)/shard_map/all_to_all | solution.py:92
  207.5 12.7 %all_to_all.44 = f16[2,128,2048]{2,1,0:T(8,128)(2,1)S(1)} all-to-all(f16[2,128,2048]{2,1,0:T(8,128)(2,1)S(1)} %broadcast_in_dim.103), channel_id=1, replica_groups={{0,16},{32,48},{64,80},{96,112},{128,144},{160,176},{192,208},{224,240}..., dimensions={0} | all-to-all | bytes 2097152 | tf_op jit(solution)/shard_map/all_to_all | solution.py:97
  220.2 0.2 bitcast_convert_fusion
  220.4 1.5 fusion.40
  (34 shorter events, 1.7 us)
Async XLA Ops:
  0.6 5.2 %copy-start = (bf16[768,1024]{1,0:T(8,128)(2,1)S(1)}, bf16[768,1024]{1,0:T(8,128)(2,1)}, u32[]{:S(2)}) copy-start(bf16[768,1024]{1,0:T(8,128)(2,1)} %param.4) | copy-start | bytes 4718596
  9.4 27.0 %all-to-all-start = ((bf16[16,48,1024]{2,1,0:T(8,128)(2,1)}), bf16[16,48,1024]{2,1,0:T(8,128)(2,1)S(1)}, u32[]{:S(2)}, u32[]{:S(2)}) async-start(bf16[16,48,1024]{2,1,0:T(8,128)(2,1)} %bitcast.27), calls=%async_computation | async-start | bytes 3145728 | tf_op jit(solution)/shard_map/all_to_all | solution.py:59
  36.4 2.4 %copy-start.2 = (bf16[256,1024]{1,0:T(8,128)(2,1)S(1)}, bf16[256,1024]{1,0:T(8,128)(2,1)}, u32[]{:S(2)}) copy-start(bf16[256,1024]{1,0:T(8,128)(2,1)} %get-tuple-element.15) | copy-start | bytes 1572868
  36.4 2.4 %copy-start.3 = (bf16[256,1024]{1,0:T(8,128)(2,1)S(1)}, bf16[256,1024]{1,0:T(8,128)(2,1)}, u32[]{:S(2)}) copy-start(bf16[256,1024]{1,0:T(8,128)(2,1)} %get-tuple-element.16) | copy-start | bytes 1572868
  39.8 0.9 copy-start.1
  75.7 18.7 %all-to-all-start.2 = ((f32[32,2,128]{2,1,0:T(2,128)}), f32[32,2,128]{2,1,0:T(2,128)S(1)}, u32[]{:S(2)}, u32[]{:S(2)}) async-start(f32[32,2,128]{2,1,0:T(2,128)} %broadcast_in_dim.92), calls=%async_computation.2 | async-start | bytes 65536 | tf_op jit(solution)/shard_map/all_to_all | solution.py:31
  98.5 18.7 %all-to-all-start.3 = ((f32[32,2,128]{2,1,0:T(2,128)}), f32[32,2,128]{2,1,0:T(2,128)S(1)}, u32[]{:S(2)}, u32[]{:S(2)}) async-start(f32[32,2,128]{2,1,0:T(2,128)} %broadcast_in_dim.94), calls=%async_computation.3 | async-start | bytes 65536 | tf_op jit(solution)/shard_map/all_to_all | solution.py:31

commit v2 on v0

v2 whole, which is shorter than its diff:
```python
import functools

import jax
import jax.numpy as jnp
from jax import lax
from jax.experimental import pallas as pl
from jax.experimental.pallas import tpu as pltpu
from jax.sharding import PartitionSpec as P

SINK = 3
LANES = 128
ROW_STEP = 256
F32 = jnp.float32
BF16 = jnp.bfloat16
VMEM_LIMIT = 40 * 1024 * 1024


def call(kernel, out_shape, n_in, flops, moved, scalars=0, scratch=()):
    smem = pl.BlockSpec(memory_space=pltpu.SMEM)
    vmem = pl.BlockSpec(memory_space=pltpu.VMEM)
    return pl.pallas_call(
        kernel,
        out_shape=out_shape,
        in_specs=[smem] * scalars + [vmem] * n_in,
        out_specs=jax.tree.map(lambda _: vmem, out_shape),
        scratch_shapes=scratch,
        compiler_params=pltpu.CompilerParams(vmem_limit_bytes=VMEM_LIMIT),
        cost_estimate=pl.CostEstimate(flops=flops, bytes_accessed=moved, transcendentals=0),
    )


def dot_nt(a, b):
    return lax.dot_general(a, b, (((1,), (1,)), ((), ())), preferred_element_type=F32)


def dot_tn(a, b):
    return lax.dot_general(a, b, (((0,), (0,)), ((), ())), preferred_element_type=F32)


def order_kernel(groups, dest_ref, embed_ref, out_ref):
    rows = embed_ref.shape[0]
    block = rows // groups
    before = lax.broadcasted_iota(jnp.int32, (LANES, LANES), 0)
    after = lax.broadcasted_iota(jnp.int32, (LANES, LANES), 1)
    earlier = jnp.where(before < after, 1.0, 0.0).astype(BF16)
    group = lax.broadcasted_iota(jnp.int32, (groups, LANES), 0)
    base = (group * block).astype(F32)
    count = jnp.zeros((groups, 1), F32)
    places = []
    for start in range(0, rows, LANES):
        hot = jnp.where(group == dest_ref[:, start : start + LANES], 1.0, 0.0)
        rank = jnp.dot(hot.astype(BF16), earlier, preferred_element_type=F32) + count
        places.append(jnp.sum(hot * (rank + base), axis=0, keepdims=True))
        count = count + jnp.sum(hot, axis=1, keepdims=True)
    place = jnp.concatenate(places, axis=1).astype(jnp.int32)
    for start in range(0, rows, ROW_STEP):
        slot = lax.broadcasted_iota(jnp.int32, (ROW_STEP, rows), 0) + start
        pick = jnp.where(slot == place, 1.0, 0.0).astype(BF16)
        got = jnp.dot(pick, embed_ref[...], preferred_element_type=F32)
        out_ref[start : start + ROW_STEP, :] = got.astype(BF16)


def put_mass(mass, sent_ref):
    comp = mass.shape[1]
    parts = [mass[:, s : s + LANES] for s in range(0, comp, LANES)]
    block = jnp.concatenate(parts + [jnp.zeros((8 - len(parts), LANES), F32)], axis=0)
    sent_ref[...] = jnp.broadcast_to(block[None], sent_ref.shape)


def get_mass(got_ref, comp):
    block = jnp.sum(got_ref[...], axis=0)
    return jnp.concatenate([block[i : i + 1] for i in range(comp // LANES)], axis=1)


def score_step(x, quad_ref, lin_ref, off_ref, scale):
    wide = x.astype(F32)
    raw = dot_nt((wide * wide).astype(BF16), quad_ref[...]) + dot_nt(x, lin_ref[...])
    score = scale * (raw + off_ref[...])
    lifted = jnp.exp(score - jnp.max(score, axis=1, keepdims=True))
    return lifted / jnp.sum(lifted, axis=1, keepdims=True)


def score_kernel(scale, x_ref, quad_ref, lin_ref, off_ref, resp_ref, sent_ref=None):
    rows = x_ref.shape[0]
    mass = jnp.zeros((1, resp_ref.shape[1]), F32)
    for start in range(0, rows, ROW_STEP):
        span = slice(start, start + ROW_STEP)
        resp = score_step(x_ref[span, :], quad_ref, lin_ref, off_ref, scale)
        resp_ref[span, :] = resp
        mass = mass + jnp.sum(resp, axis=0, keepdims=True)
    if sent_ref is not None:
        put_mass(mass, sent_ref)


def balance_step(resp, pull):
    scaled = resp * pull
    return scaled / jnp.sum(scaled, axis=1, keepdims=True)


def balance_kernel(target, got_ref, resp_ref, out_ref, sent_ref=None):
    rows, comp = resp_ref.shape
    pull = target / get_mass(got_ref, comp)
    mass = jnp.zeros((1, comp), F32)
    for start in range(0, rows, ROW_STEP):
        span = slice(start, start + ROW_STEP)
        resp = balance_step(resp_ref[span, :], pull)
        out_ref[span, :] = resp
        mass = mass + jnp.sum(resp, axis=0, keepdims=True)
    if sent_ref is not None:
        put_mass(mass, sent_ref)


def moment_kernel(
    target, side_ref, got_ref, mine_ref, theirs_ref, x_ref, y_ref, first_ref, second_ref, total_ref
):
    rows, comp = mine_ref.shape
    half = comp // 2
    width = x_ref.shape[1]
    pull = target / get_mass(got_ref, comp)
    upper = side_ref[0] == 1
    first = jnp.zeros((2 * half, width), F32)
    second = jnp.zeros((2 * half, width), F32)
    third = jnp.zeros((half, width), F32)
    total = jnp.zeros((2 * half, LANES), F32)
    ones = jnp.ones((ROW_STEP, LANES), BF16)
    for resp_ref, rows_ref in ((mine_ref, x_ref), (theirs_ref, y_ref)):
        for start in range(0, rows, ROW_STEP):
            span = slice(start, start + ROW_STEP)
            resp = balance_step(resp_ref[span, :], pull)
            resp = jnp.where(upper, resp[:, half:], resp[:, :half])
            high = resp.astype(BF16)
            low = (resp - high.astype(F32)).astype(BF16)
            both = jnp.concatenate([high, low], axis=1)
            x = rows_ref[span, :]
            wide = x.astype(F32)
            square = wide * wide
            square_high = square.astype(BF16)
            square_low = (square - square_high.astype(F32)).astype(BF16)
            first = first + dot_tn(both, x)
            second = second + dot_tn(both, square_high)
            third = third + dot_tn(high, square_low)
            total = total + dot_tn(both, ones)
    first_ref[...] = first[:half] + first[half:]
    second_ref[...] = second[:half] + second[half:] + third
    total_ref[...] = total[:half] + total[half:]


def weights(mean_block, var_block):
    prec = 1.0 / var_block.astype(F32)
    mean_wide = mean_block.astype(F32)
    quad = (-0.5 * prec).astype(BF16)
    linear = (mean_wide * prec).astype(BF16)
    offset = -0.5 * jnp.sum(
        jnp.log(var_block.astype(F32)) + mean_wide * mean_wide * prec, axis=1
    )
    return quad, linear, offset[None, :]


def with_total(first, second, total):
    high = lax.reduce_precision(total, 5, 10)
    lane = lax.broadcasted_iota(jnp.int32, total.shape, 1)
    tail = jnp.where(lane < LANES // 2, high, total - high)
    return jnp.concatenate([first, second, tail], axis=1).astype(jnp.float16)


def on_device(embed, dest, means, variances):
    rows_dev, width = embed.shape
    groups = lax.axis_size("narrow")
    members = lax.axis_size("wide")
    block = rows_dev // groups
    comp = means.shape[0]
    half = comp // 2
    deep = members // 2
    pairs = [[2 * z, 2 * z + 1] for z in range(deep)]
    lines = [[2 * z + y for z in range(deep)] for y in range(2)]
    swap = [(i, i ^ 1) for i in range(members)]
    side = (lax.axis_index("wide") % 2).astype(jnp.int32).reshape(1)
    scale = width ** (-0.5)
    target = float(rows_dev * members / comp)
    big = rows_dev * width
    area = rows_dev * comp

    everyone = functools.partial(
        lax.all_to_all, axis_name="wide", split_axis=0, concat_axis=0, tiled=True
    )
    resp_shape = jax.ShapeDtypeStruct((rows_dev, comp), F32)
    sent_shape = jax.ShapeDtypeStruct((members, 8, LANES), F32)

    ordered = call(
        functools.partial(order_kernel, groups),
        jax.ShapeDtypeStruct(embed.shape, BF16), 2, 2 * rows_dev * big, 4 * big,
    )(dest.reshape(1, rows_dev), embed)
    mine = lax.all_to_all(
        ordered.reshape(groups, block, width), "narrow", split_axis=0, concat_axis=0, tiled=True
    ).reshape(rows_dev, width)
    theirs = lax.ppermute(mine, "wide", swap)
    quad, linear, offset = weights(means, variances)
    resp, sent = call(
        functools.partial(score_kernel, scale), (resp_shape, sent_shape),
        4, 4 * big * comp, 2 * big + 4 * area,
    )(mine, quad, linear, offset)
    got = everyone(sent)
    other = call(
        functools.partial(score_kernel, scale), resp_shape,
        4, 4 * big * comp, 2 * big + 4 * area,
    )(theirs, quad, linear, offset)
    for step in range(SINK - 1):
        last = got
        resp, sent = call(
            functools.partial(balance_kernel, target), (resp_shape, sent_shape),
            2, 4 * area, 8 * area,
        )(last, resp)
        got = everyone(sent)
        other = call(
            functools.partial(balance_kernel, target), resp_shape, 2, 4 * area, 8 * area,
        )(last, other)
    first, second, total = call(
        functools.partial(moment_kernel, target),
        (
            jax.ShapeDtypeStruct((half, width), F32),
            jax.ShapeDtypeStruct((half, width), F32),
            jax.ShapeDtypeStruct((half, LANES), F32),
        ),
        5, 10 * big * comp, 4 * big + 8 * area, scalars=1,
    )(side, got, resp, other, mine, theirs)
    sent = with_total(first, second, total).reshape(deep, comp // members, 2 * width + LANES)
    got = everyone(sent, axis_index_groups=lines)
    sums = jnp.sum(got.astype(F32), axis=0)
    total = (sums[:, 2 * width] + sums[:, 2 * width + LANES // 2])[:, None]
    new_mean = sums[:, :width] / total
    new_var = sums[:, width : 2 * width] / total - new_mean * new_mean + 0.01
    done = jnp.concatenate([new_mean, new_var], axis=1).astype(jnp.float16)
    got = everyone(jnp.broadcast_to(done[None], (deep,) + done.shape), axis_index_groups=lines)
    got = got.reshape(1, half, 2 * width)
    got = everyone(jnp.broadcast_to(got, (2,) + got.shape[1:]), axis_index_groups=pairs)
    out = got.reshape(comp, 2 * width).astype(F32)
    return (out[:, :width], out[:, width:])


def solution(mesh):
    return jax.shard_map(
        on_device,
        mesh=mesh,
        in_specs=(
            P(("wide", "narrow"), None),
            P(("wide", "narrow")),
            P("narrow", None),
            P("narrow", None),
        ),
        out_specs=(P("narrow", None), P("narrow", None)),
        check_vma=False,
    )
```

time: 607 us -> 220 us (0.36)
  waiting for transfers between devices: 252 us -> 31.9 us
  blocking collectives: 304 us -> 146 us
  between operations: 14.1 us -> 0.8 us
  Pallas kernels: 0 us -> 12.2 us
  starting transfers between devices: 5.81 us -> 17.9 us
  other arithmetic: 13.1 us -> 2.42 us
  matrix products: 10.3 us -> 0 us
    psum x4 -> x0, blocking collectives: 304 us -> none  [the longest x3 228 us: on_device(): mass = lax.psum(jnp.sum(resp, axis=0), 'wide')]
    psum x1 -> x0, waiting for transfers between devices: 233 us -> none  [on_device(): total, first, second = lax.psum((total, first, second), 'wide')]
    all_to_all x0 -> x5, blocking collectives: none -> 146 us  [the longest x2 67.2 us: on_device(): got = everyone(sent)]
    all_to_all x1 -> x2, waiting for transfers between devices: 18.6 us -> 31.8 us  [the longest x1 19.7 us: on_device(): lax.all_to_all(ordered.reshape(groups, block, width), 'narrow', split_axi...]
    pallas_call x0 -> x8, Pallas kernels: none -> 12.2 us  [the longest x1 4.11 us: on_device(): call(functools.partial(moment_kernel, target), (jax.ShapeDtypeStruct((hal...]
    dot_general x3 -> x0, matrix products: 10.3 us -> none  [the longest x1 5.39 us: on_device(): lax.dot_general(resp, values * values, (((0,), (0,)), ((), ())), precisio...]
    ppermute x0 -> x1, starting transfers between devices: none -> 6.7 us  [on_device(): theirs = lax.ppermute(mine, 'wide', swap)]
  transfers between devices with their start and end apart: 2 -> 3, of which waited for: 2 -> 2; matrix products, arithmetic and copies ran while one was open for 0% -> 1% of each run, Pallas kernels for 0% -> 2%
where the time goes in v2:
time: 220 us; the launch traced here: 217 us
  blocking collectives  146 us (66%)
  waiting for transfers between devices  31.9 us (14%)
  starting transfers between devices  17.9 us (8%)
  Pallas kernels  12.2 us (6%)
  local copies, waits for them, and re-layouts  5.74 us (3%)
  other arithmetic  2.42 us (1%)
    all_to_all x2, blocking collectives, on_device(): got = everyone(sent)  67.2 us
    all_to_all x1, blocking collectives, on_device(): got = everyone(sent, axis_index_groups=lines)  35.4 us
    all_to_all x1, blocking collectives, on_device(): everyone(jnp.broadcast_to(done[None], (deep,) + done.shape), axis_index_g...  30.6 us
    all_to_all x1, waiting for transfers between devices, on_device(): lax.all_to_all(ordered.reshape(groups, block, width), 'narrow', split_axi...  19.7 us
    all_to_all x1, blocking collectives, on_device(): everyone(jnp.broadcast_to(got, (2,) + got.shape[1:]), axis_index_groups=p...  12.8 us
    all_to_all x1, waiting for transfers between devices, on_device(): got = everyone(sent)  12.1 us
    ppermute x1, starting transfers between devices, on_device(): theirs = lax.ppermute(mine, 'wide', swap)  6.7 us
    all_to_all x1, starting transfers between devices, on_device(): lax.all_to_all(ordered.reshape(groups, block, width), 'narrow', split_axi...  5.9 us
  transfers between devices with their start and end apart: 3, of which 2 were waited for; matrix products, arithmetic and copies ran while one was open for 1% of the time, Pallas kernels for 2%

profile of v2, /device:TPU:24, one launch (start us, length us, event | category | flops | bytes accessed | tf_op | source)
XLA Modules:
  0.0 216.9 jit_solution(10152309078270899506)
XLA Ops:
  0.6 0.7 reshape.53.dest_ref
  1.3 1.4 copy-done
  2.7 2.7 %shard_map.59 = bf16[768,1024]{1,0:T(8,128)(2,1)} custom-call(s32[1,768]{1,0:T(1,128)S(1)} %reshape.53.dest_ref, bf16[768,1024]{1,0:T(8,128)(2,1)S(1)} %copy-done), custom_call_target="tpu_custom_call" | custom-call | flops 1207959552 | bytes 3145728 | tf_op jit(solution)/shard_map/pallas_call | solution.py:189
  5.4 5.9 %all-to-all-start = ((bf16[16,48,1024]{2,1,0:T(8,128)(2,1)}), bf16[16,48,1024]{2,1,0:T(8,128)(2,1)S(1)}, u32[]{:S(2)}, u32[]{:S(2)}) async-start(bf16[16,48,1024]{2,1,0:T(8,128)(2,1)} %bitcast.1), calls=%async_computation | async-start | bytes 3145728 | tf_op jit(solution)/shard_map/all_to_all | solution.py:193
  11.3 1.5 fusion.1
  12.9 19.7 %all-to-all-done = bf16[16,48,1024]{2,1,0:T(8,128)(2,1)S(1)} async-done(((bf16[16,48,1024]{2,1,0:T(8,128)(2,1)}), bf16[16,48,1024]{2,1,0:T(8,128)(2,1)S(1)}, u32[]{:S(2)}, u32[]{:S(2)}) %all-to-all-start) | async-done | bytes 1572896 | tf_op jit(solution)/shard_map/all_to_all | solution.py:193
  32.6 6.7 %collective-permute-start = (bf16[768,1024]{1,0:T(8,128)(2,1)S(1)}, bf16[768,1024]{1,0:T(8,128)(2,1)}, u32[]{:S(2)}, u32[]{:S(2)}) collective-permute-start(bf16[768,1024]{1,0:T(8,128)(2,1)S(1)} %bitcast.14), channel_id=1, source_target_pairs={{0,16},{16,0},{32,48},{48,32},{64,80},{80,64},{96,112},{112,96},{1... | collective-permute-start | bytes 4718600 | tf_op jit(solution)/shard_map/ppermute | solution.py:196
  39.3 1.2 shard_map.60
  40.5 35.1 %all_to_all.35.got_ref = f32[32,8,128]{2,1,0:T(8,128)S(1)} all-to-all(f32[32,8,128]{2,1,0:T(8,128)S(1)} %get-tuple-element.11), channel_id=1, replica_groups=mesh['wide'=32,'narrow'=16] {'wide'}, dimensions={0} | all-to-all | bytes 262144 | tf_op jit(solution)/shard_map/all_to_all | solution.py:202
  75.6 0.2 shard_map.61
  75.8 32.1 %all_to_all.36.got_ref = f32[32,8,128]{2,1,0:T(8,128)S(1)} all-to-all(f32[32,8,128]{2,1,0:T(8,128)S(1)} %get-tuple-element.13), channel_id=1, replica_groups=mesh['wide'=32,'narrow'=16] {'wide'}, dimensions={0} | all-to-all | bytes 262144 | tf_op jit(solution)/shard_map/all_to_all | solution.py:213
  108.0 0.9 shard_map.62
  108.9 0.9 copy-done.1
  109.7 5.3 %all-to-all-start.3 = ((f32[32,8,128]{2,1,0:T(8,128)}), f32[32,8,128]{2,1,0:T(8,128)S(1)}, u32[]{:S(2)}, u32[]{:S(2)}) async-start(f32[32,8,128]{2,1,0:T(8,128)} %get-tuple-element.15), calls=%async_computation.3 | async-start | bytes 262144 | tf_op jit(solution)/shard_map/all_to_all | solution.py:213
  115.0 0.0 collective-permute-done.x_ref.y_ref
  115.1 2.6 %shard_map.63.resp_ref = f32[768,256]{1,0:T(8,128)S(1)} custom-call(bf16[768,1024]{1,0:T(8,128)(2,1)} %collective-permute-done.x_ref.y_ref, bf16[256,1024]{1,0:T(8,128)(2,1)S(1)} %get-tuple-element.24.quad_ref, bf16[256,1024]{1,0:T(8,128)(2,1)S(1)} %get-tuple-element.23.lin_ref, f32[1,256]{1,0:T(1,128)S(1)} %bitcast.18), custom_call_target="tpu_custom_call" | custom-call | flops 805306368 | bytes 2359296 | tf_op jit(solution)/shard_map/pallas_call | solution.py:203
  117.7 0.2 shard_map.64.resp_ref
  117.9 0.2 shard_map.65.theirs_ref
  118.1 12.1 %all-to-all-done.3.got_ref = f32[32,8,128]{2,1,0:T(8,128)S(1)} async-done(((f32[32,8,128]{2,1,0:T(8,128)}), f32[32,8,128]{2,1,0:T(8,128)S(1)}, u32[]{:S(2)}, u32[]{:S(2)}) %all-to-all-start.3) | async-done | bytes 131104 | tf_op jit(solution)/shard_map/all_to_all | solution.py:213
  130.3 1.1 copy-done.2
  131.4 4.1 %shard_map.66 = (f32[128,1024]{1,0:T(8,128)S(1)}, f32[128,1024]{1,0:T(8,128)S(1)}, f32[128,128]{1,0:T(8,128)S(1)}) custom-call(s32[1]{0:T(128)} %bitcast.side_ref, f32[32,8,128]{2,1,0:T(8,128)S(1)} %all-to-all-done.3.got_ref, f32[768,256]{1,0:T(8,128)S(1)} %copy-done.2, f32[768,256]{1,0:T(8,128)S(1)} %shard_map.65.theirs_ref, ...), custom_call_target="tpu_custom_call" | custom-call | flops 2013265920 | bytes 4718592 | tf_op jit(solution)/shard_map/pallas_call | solution.py:217
  135.5 0.1 convert_bitcast_fusion
  135.7 0.2 pad_maximum_fusion
  135.8 35.4 %all_to_all.37 = f16[16,8,2176]{2,1,0:T(8,128)(2,1)S(1)} all-to-all(f16[16,8,2176]{2,1,0:T(8,128)(2,1)S(1)} %pad_maximum_fusion), channel_id=1, replica_groups={{0,32,64,96,128,160,192,224,256,288,320,352,384,416,448,480},{16,48,80,..., dimensions={0} | all-to-all | bytes 1114112 | tf_op jit(solution)/shard_map/all_to_all | solution.py:227
  171.2 0.1 convert_reduce_fusion
  171.3 0.2 fusion.9
  171.5 0.1 fusion.10
  171.7 30.6 %all_to_all.38 = f16[16,8,2048]{2,1,0:T(8,128)(2,1)S(1)} all-to-all(f16[16,8,2048]{2,1,0:T(8,128)(2,1)S(1)} %broadcast_in_dim.6), channel_id=1, replica_groups={{0,32,64,96,128,160,192,224,256,288,320,352,384,416,448,480},{16,48,80,..., dimensions={0} | all-to-all | bytes 1048576 | tf_op jit(solution)/shard_map/all_to_all | solution.py:233
  202.2 0.1 broadcast_in_dim.8
  202.4 12.8 %all_to_all.39 = f16[2,128,2048]{2,1,0:T(8,128)(2,1)S(1)} all-to-all(f16[2,128,2048]{2,1,0:T(8,128)(2,1)S(1)} %broadcast_in_dim.8), channel_id=1, replica_groups={{0,16},{32,48},{64,80},{96,112},{128,144},{160,176},{192,208},{224,240}..., dimensions={0} | all-to-all | bytes 2097152 | tf_op jit(solution)/shard_map/all_to_all | solution.py:235
  215.2 0.2 bitcast_convert_fusion
  215.4 1.5 fusion.11
  (10 shorter events, 0.1 us)
Async XLA Ops:
  1.3 1.4 copy-start
  5.4 5.9 %copy-start.3 = (bf16[256,1024]{1,0:T(8,128)(2,1)S(1)}, bf16[256,1024]{1,0:T(8,128)(2,1)}, u32[]{:S(2)}) copy-start(bf16[256,1024]{1,0:T(8,128)(2,1)} %param.7) | copy-start | bytes 1572868
  5.4 27.1 %all-to-all-start = ((bf16[16,48,1024]{2,1,0:T(8,128)(2,1)}), bf16[16,48,1024]{2,1,0:T(8,128)(2,1)S(1)}, u32[]{:S(2)}, u32[]{:S(2)}) async-start(bf16[16,48,1024]{2,1,0:T(8,128)(2,1)} %bitcast.1), calls=%async_computation | async-start | bytes 3145728 | tf_op jit(solution)/shard_map/all_to_all | solution.py:193
  32.6 82.5 %collective-permute-start = (bf16[768,1024]{1,0:T(8,128)(2,1)S(1)}, bf16[768,1024]{1,0:T(8,128)(2,1)}, u32[]{:S(2)}, u32[]{:S(2)}) collective-permute-start(bf16[768,1024]{1,0:T(8,128)(2,1)S(1)} %bitcast.14), channel_id=1, source_target_pairs={{0,16},{16,0},{32,48},{48,32},{64,80},{80,64},{96,112},{112,96},{1... | collective-permute-start | bytes 4718600 | tf_op jit(solution)/shard_map/ppermute | solution.py:196
  108.9 0.9 copy-start.1
  109.7 20.5 %all-to-all-start.3 = ((f32[32,8,128]{2,1,0:T(8,128)}), f32[32,8,128]{2,1,0:T(8,128)S(1)}, u32[]{:S(2)}, u32[]{:S(2)}) async-start(f32[32,8,128]{2,1,0:T(8,128)} %get-tuple-element.15), calls=%async_computation.3 | async-start | bytes 262144 | tf_op jit(solution)/shard_map/all_to_all | solution.py:213
  130.3 1.1 copy-start.2

commit v3 on v2

--- a/solution.py
+++ b/solution.py
@@ -110,39 +110,48 @@
         put_mass(mass, sent_ref)
 
 
-def moment_kernel(
-    target, side_ref, got_ref, mine_ref, theirs_ref, x_ref, y_ref, first_ref, second_ref, total_ref
+def square_kernel(x_ref, high_ref, low_ref):
+    for start in range(0, x_ref.shape[0], ROW_STEP):
+        span = slice(start, start + ROW_STEP)
+        wide = x_ref[span, :].astype(F32)
+        square = wide * wide
+        high = square.astype(BF16)
+        high_ref[span, :] = high
+        low_ref[span, :] = (square - high.astype(F32)).astype(BF16)
+
+
+def put_moments(both, x_ref, high_ref, low_ref, first_ref, second_ref, total_ref):
+    half = first_ref.shape[0]
+    first = dot_tn(both, x_ref[...])
+    first_ref[...] = first[:half] + first[half:]
+    second = dot_tn(both, high_ref[...])
+    second_ref[...] = second[:half] + second[half:] + dot_tn(both[:, :half], low_ref[...])
+    total = dot_tn(both, jnp.ones((both.shape[0], LANES), BF16))
+    total_ref[...] = total[:half] + total[half:]
+
+
+def crossed_kernel(
+    target, side_ref, got_ref, resp_ref, x_ref, high_ref, low_ref,
+    kept_ref, first_ref, second_ref, total_ref, lent_ref,
 ):
-    rows, comp = mine_ref.shape
+    rows, comp = resp_ref.shape
     half = comp // 2
-    width = x_ref.shape[1]
+    upper = side_ref[0] == 1
     pull = target / get_mass(got_ref, comp)
-    upper = side_ref[0] == 1
-    first = jnp.zeros((2 * half, width), F32)
-    second = jnp.zeros((2 * half, width), F32)
-    third = jnp.zeros((half, width), F32)
-    total = jnp.zeros((2 * half, LANES), F32)
-    ones = jnp.ones((ROW_STEP, LANES), BF16)
-    for resp_ref, rows_ref in ((mine_ref, x_ref), (theirs_ref, y_ref)):
-        for start in range(0, rows, ROW_STEP):
-            span = slice(start, start + ROW_STEP)
-            resp = balance_step(resp_ref[span, :], pull)
-            resp = jnp.where(upper, resp[:, half:], resp[:, :half])
-            high = resp.astype(BF16)
-            low = (resp - high.astype(F32)).astype(BF16)
-            both = jnp.concatenate([high, low], axis=1)
-            x = rows_ref[span, :]
-            wide = x.astype(F32)
-            square = wide * wide
-            square_high = square.astype(BF16)
-            square_low = (square - square_high.astype(F32)).astype(BF16)
-            first = first + dot_tn(both, x)
-            second = second + dot_tn(both, square_high)
-            third = third + dot_tn(high, square_low)
-            total = total + dot_tn(both, ones)
-    first_ref[...] = first[:half] + first[half:]
-    second_ref[...] = second[:half] + second[half:] + third
-    total_ref[...] = total[:half] + total[half:]
+    for start in range(0, rows, ROW_STEP):
+        span = slice(start, start + ROW_STEP)
+        resp = balance_step(resp_ref[span, :], pull)
+        high = resp.astype(BF16).astype(F32)
+        low = resp - high
+        lower_half = jnp.concatenate([high[:, :half], low[:, :half]], axis=1)
+        upper_half = jnp.concatenate([high[:, half:], low[:, half:]], axis=1)
+        kept_ref[span, :] = jnp.where(upper, upper_half, lower_half).astype(BF16)
+        lent_ref[span, :] = jnp.where(upper, lower_half, upper_half).astype(BF16)
+    put_moments(lent_ref[...], x_ref, high_ref, low_ref, first_ref, second_ref, total_ref)
+
+
+def kept_kernel(kept_ref, x_ref, high_ref, low_ref, first_ref, second_ref, total_ref):
+    put_moments(kept_ref[...], x_ref, high_ref, low_ref, first_ref, second_ref, total_ref)
 
 
 def weights(mean_block, var_block):
@@ -161,6 +170,11 @@
     lane = lax.broadcasted_iota(jnp.int32, total.shape, 1)
     tail = jnp.where(lane < LANES // 2, high, total - high)
     return jnp.concatenate([first, second, tail], axis=1).astype(jnp.float16)
+
+
+def split_total(payload, part):
+    total = payload[:, 2 * part : 2 * part + 1] + payload[:, 2 * part + LANES // 2 :][:, :1]
+    return payload[:, :part], payload[:, part : 2 * part], total
 
 
 def on_device(embed, dest, means, variances):
@@ -171,10 +185,10 @@
     comp = means.shape[0]
     half = comp // 2
     deep = members // 2
-    pairs = [[2 * z, 2 * z + 1] for z in range(deep)]
     lines = [[2 * z + y for z in range(deep)] for y in range(2)]
     swap = [(i, i ^ 1) for i in range(members)]
-    side = (lax.axis_index("wide") % 2).astype(jnp.int32).reshape(1)
+    upper = lax.axis_index("wide") % 2
+    own = upper.astype(jnp.int32).reshape(1)
     scale = width ** (-0.5)
     target = float(rows_dev * members / comp)
     big = rows_dev * width
@@ -193,47 +207,45 @@
     mine = lax.all_to_all(
         ordered.reshape(groups, block, width), "narrow", split_axis=0, concat_axis=0, tiled=True
     ).reshape(rows_dev, width)
-    theirs = lax.ppermute(mine, "wide", swap)
     quad, linear, offset = weights(means, variances)
     resp, sent = call(
         functools.partial(score_kernel, scale), (resp_shape, sent_shape),
         4, 4 * big * comp, 2 * big + 4 * area,
     )(mine, quad, linear, offset)
     got = everyone(sent)
-    other = call(
-        functools.partial(score_kernel, scale), resp_shape,
-        4, 4 * big * comp, 2 * big + 4 * area,
-    )(theirs, quad, linear, offset)
     for step in range(SINK - 1):
-        last = got
         resp, sent = call(
             functools.partial(balance_kernel, target), (resp_shape, sent_shape),
             2, 4 * area, 8 * area,
-        )(last, resp)
+        )(got, resp)
         got = everyone(sent)
-        other = call(
-            functools.partial(balance_kernel, target), resp_shape, 2, 4 * area, 8 * area,
-        )(last, other)
-    first, second, total = call(
-        functools.partial(moment_kernel, target),
-        (
-            jax.ShapeDtypeStruct((half, width), F32),
-            jax.ShapeDtypeStruct((half, width), F32),
-            jax.ShapeDtypeStruct((half, LANES), F32),
-        ),
-        5, 10 * big * comp, 4 * big + 8 * area, scalars=1,
-    )(side, got, resp, other, mine, theirs)
-    sent = with_total(first, second, total).reshape(deep, comp // members, 2 * width + LANES)
-    got = everyone(sent, axis_index_groups=lines)
-    sums = jnp.sum(got.astype(F32), axis=0)
-    total = (sums[:, 2 * width] + sums[:, 2 * width + LANES // 2])[:, None]
-    new_mean = sums[:, :width] / total
-    new_var = sums[:, width : 2 * width] / total - new_mean * new_mean + 0.01
+    plain = jax.ShapeDtypeStruct((rows_dev, width), BF16)
+    high, low = call(square_kernel, (plain, plain), 1, 4 * big, 6 * big)(mine)
+    sums = (
+        jax.ShapeDtypeStruct((half, width), F32),
+        jax.ShapeDtypeStruct((half, width), F32),
+        jax.ShapeDtypeStruct((half, LANES), F32),
+    )
+    slab = jax.ShapeDtypeStruct((rows_dev, comp), BF16)
+    kept, *lent = call(
+        functools.partial(crossed_kernel, target), (slab, *sums), 5, 5 * big * comp,
+        6 * big + 8 * area, scalars=1, scratch=[pltpu.VMEM((rows_dev, comp), BF16)],
+    )(own, got, resp, mine, high, low)
+    there = lax.ppermute(with_total(*lent), "wide", swap)
+    here = call(kept_kernel, sums, 4, 5 * big * comp, 6 * big + 2 * area)(kept, mine, high, low)
+    first, second, total = split_total(there.astype(F32), width)
+    sent = with_total(first + here[0], second + here[1], total + here[2])
+    got = everyone(sent.reshape(deep, half // deep, sent.shape[1]), axis_index_groups=lines)
+    first, second, total = split_total(jnp.sum(got.astype(F32), axis=0), width)
+    new_mean = first / total
+    new_var = second / total - new_mean * new_mean + 0.01
     done = jnp.concatenate([new_mean, new_var], axis=1).astype(jnp.float16)
     got = everyone(jnp.broadcast_to(done[None], (deep,) + done.shape), axis_index_groups=lines)
-    got = got.reshape(1, half, 2 * width)
-    got = everyone(jnp.broadcast_to(got, (2,) + got.shape[1:]), axis_index_groups=pairs)
-    out = got.reshape(comp, 2 * width).astype(F32)
+    here = got.reshape(half, 2 * width)
+    there = lax.ppermute(here, "wide", swap)
+    low = jnp.where(upper == 0, here, there)
+    high = jnp.where(upper == 0, there, here)
+    out = jnp.concatenate([low, high], axis=0).astype(F32)
     return (out[:, :width], out[:, width:])
 
 

time: 220 us -> 216 us (0.982); the launches traced: 217 us -> 215 us
  blocking collectives: 146 us -> 123 us
  waiting for transfers between devices: 31.9 us -> 54.6 us
  Pallas kernels: 12.2 us -> 8.54 us
  local copies, waits for them, and re-layouts: 5.74 us -> 8.16 us
    ppermute x1 -> x2, waiting for transfers between devices: 0.01 us -> 21.2 us  [the longest x1 10.7 us: on_device(): there = lax.ppermute(with_total(*lent), 'wide', swap)]
    all_to_all x2, blocking collectives: 67.2 us -> 55 us  [on_device(): got = everyone(sent)]
    all_to_all x2 -> x1, blocking collectives: 48.2 us -> 37.2 us  [on_device(): everyone(sent.reshape(deep, half // deep, sent.shape[1]), axis_index_grou...]
    pallas_call x4 -> x3, Pallas kernels: 7.16 us -> 3.46 us  [the longest x1 1.54 us: on_device(): call(functools.partial(crossed_kernel, target), (slab, *sums), 5, 5 * big...]
    unnamed x8 -> x12, local copies, waits for them, and re-layouts: 3.42 us -> 5.98 us
    ppermute x1 -> x2, starting transfers between devices: 6.7 us -> 5.61 us  [the longest x1 3.47 us: on_device(): there = lax.ppermute(with_total(*lent), 'wide', swap)]
  transfers between devices with their start and end apart: 3 -> 4, of which waited for: 2 -> 4; matrix products, arithmetic and copies ran while one was open for 1% -> 1% of each run, Pallas kernels for 2% -> 1%
where the time goes in v3:
time: 216 us; the launch traced here: 215 us
  blocking collectives  123 us (57%)
  waiting for transfers between devices  54.6 us (25%)
  starting transfers between devices  16.8 us (8%)
  Pallas kernels  8.54 us (4%)
  local copies, waits for them, and re-layouts  8.16 us (4%)
  other arithmetic  3.32 us (2%)
    all_to_all x2, blocking collectives, on_device(): got = everyone(sent)  55 us
    all_to_all x1, blocking collectives, on_device(): everyone(sent.reshape(deep, half // deep, sent.shape[1]), axis_index_grou...  37.2 us
    all_to_all x1, blocking collectives, on_device(): everyone(jnp.broadcast_to(done[None], (deep,) + done.shape), axis_index_g...  30.9 us
    all_to_all x1, waiting for transfers between devices, on_device(): lax.all_to_all(ordered.reshape(groups, block, width), 'narrow', split_axi...  19.7 us
    all_to_all x1, waiting for transfers between devices, on_device(): got = everyone(sent)  13.8 us
    ppermute x1, waiting for transfers between devices, on_device(): there = lax.ppermute(with_total(*lent), 'wide', swap)  10.7 us
    ppermute x1, waiting for transfers between devices, on_device(): there = lax.ppermute(here, 'wide', swap)  10.4 us
    unnamed x12, local copies, waits for them, and re-layouts  5.98 us
  transfers between devices with their start and end apart: 4, of which 4 were waited for; matrix products, arithmetic and copies ran while one was open for 1% of the time, Pallas kernels for 1%

profile of v3, /device:TPU:24, one launch (start us, length us, event | category | flops | bytes accessed | tf_op | source)
XLA Modules:
  0.0 215.4 jit_solution(8246562173253132382)
XLA Ops:
  0.6 0.7 reshape.51.dest_ref
  1.3 1.4 copy-done.4
  2.7 2.7 %shard_map.59 = bf16[768,1024]{1,0:T(8,128)(2,1)} custom-call(s32[1,768]{1,0:T(1,128)S(1)} %reshape.51.dest_ref, bf16[768,1024]{1,0:T(8,128)(2,1)S(1)} %copy-done.4), custom_call_target="tpu_custom_call" | custom-call | flops 1207959552 | bytes 3145728 | tf_op jit(solution)/shard_map/pallas_call | solution.py:203
  5.4 5.9 %all-to-all-start = ((bf16[16,48,1024]{2,1,0:T(8,128)(2,1)}), bf16[16,48,1024]{2,1,0:T(8,128)(2,1)S(1)}, u32[]{:S(2)}, u32[]{:S(2)}) async-start(bf16[16,48,1024]{2,1,0:T(8,128)(2,1)} %bitcast.1), calls=%async_computation | async-start | bytes 3145728 | tf_op jit(solution)/shard_map/all_to_all | solution.py:207
  11.3 1.5 fusion.1
  12.9 19.7 %all-to-all-done = bf16[16,48,1024]{2,1,0:T(8,128)(2,1)S(1)} async-done(((bf16[16,48,1024]{2,1,0:T(8,128)(2,1)}), bf16[16,48,1024]{2,1,0:T(8,128)(2,1)S(1)}, u32[]{:S(2)}, u32[]{:S(2)}) %all-to-all-start) | async-done | bytes 1572896 | tf_op jit(solution)/shard_map/all_to_all | solution.py:207
  32.6 1.2 shard_map.60
  33.8 34.5 %all_to_all.30.got_ref = f32[32,8,128]{2,1,0:T(8,128)S(1)} all-to-all(f32[32,8,128]{2,1,0:T(8,128)S(1)} %get-tuple-element.17), channel_id=1, replica_groups=mesh['wide'=32,'narrow'=16] {'wide'}, dimensions={0} | all-to-all | bytes 262144 | tf_op jit(solution)/shard_map/all_to_all | solution.py:215
  68.3 0.2 shard_map.61
  68.5 20.6 %all_to_all.31.got_ref = f32[32,8,128]{2,1,0:T(8,128)S(1)} all-to-all(f32[32,8,128]{2,1,0:T(8,128)S(1)} %get-tuple-element.19), channel_id=1, replica_groups=mesh['wide'=32,'narrow'=16] {'wide'}, dimensions={0} | all-to-all | bytes 262144 | tf_op jit(solution)/shard_map/all_to_all | solution.py:221
  89.1 0.9 shard_map.62
  90.0 0.9 copy-done.2
  90.9 5.3 %all-to-all-start.3 = ((f32[32,8,128]{2,1,0:T(8,128)}), f32[32,8,128]{2,1,0:T(8,128)S(1)}, u32[]{:S(2)}, u32[]{:S(2)}) async-start(f32[32,8,128]{2,1,0:T(8,128)} %get-tuple-element.21), calls=%async_computation.3 | async-start | bytes 262144 | tf_op jit(solution)/shard_map/all_to_all | solution.py:221
  96.2 0.6 shard_map.63
  96.8 1.1 copy-done
  98.0 13.8 %all-to-all-done.3.got_ref = f32[32,8,128]{2,1,0:T(8,128)S(1)} async-done(((f32[32,8,128]{2,1,0:T(8,128)}), f32[32,8,128]{2,1,0:T(8,128)S(1)}, u32[]{:S(2)}, u32[]{:S(2)}) %all-to-all-start.3) | async-done | bytes 131104 | tf_op jit(solution)/shard_map/all_to_all | solution.py:221
  111.7 1.4 copy-done.1
  113.1 1.1 copy-done.3
  114.3 1.5 shard_map.64
  115.9 0.2 pad_maximum_fusion
  116.1 3.5 %collective-permute-start = (f16[128,2176]{1,0:T(8,128)(2,1)S(1)}, f16[128,2176]{1,0:T(8,128)(2,1)S(1)}, u32[]{:S(2)}, u32[]{:S(2)}) collective-permute-start(f16[128,2176]{1,0:T(8,128)(2,1)S(1)} %pad_maximum_fusion), channel_id=1, source_target_pairs={{0,16},{16,0},{32,48},{48,32},{64,80},{80,64},{96,112},{112,96},{1... | collective-permute-start | bytes 1671176 | tf_op jit(solution)/shard_map/ppermute | solution.py:234
  119.6 1.3 shard_map.65
  120.9 10.7 %collective-permute-done = f16[128,2176]{1,0:T(8,128)(2,1)S(1)} collective-permute-done((f16[128,2176]{1,0:T(8,128)(2,1)S(1)}, f16[128,2176]{1,0:T(8,128)(2,1)S(1)}, u32[]{:S(2)}, u32[]{:S(2)}) %collective-permute-start) | collective-permute-done | bytes 557088 | tf_op jit(solution)/shard_map/ppermute | solution.py:234
  131.7 0.2 fusion.10
  132.4 37.2 %all_to_all.32 = f16[16,8,2176]{2,1,0:T(8,128)(2,1)S(1)} all-to-all(f16[16,8,2176]{2,1,0:T(8,128)(2,1)S(1)} %pad_maximum_fusion.1), channel_id=1, replica_groups={{0,32,64,96,128,160,192,224,256,288,320,352,384,416,448,480},{16,48,80,..., dimensions={0} | all-to-all | bytes 1114112 | tf_op jit(solution)/shard_map/all_to_all | solution.py:238
  169.6 0.2 fusion.15
  170.0 30.9 %all_to_all.33 = f16[16,8,2048]{2,1,0:T(8,128)(2,1)S(1)} all-to-all(f16[16,8,2048]{2,1,0:T(8,128)(2,1)S(1)} %broadcast_in_dim.2), channel_id=1, replica_groups={{0,32,64,96,128,160,192,224,256,288,320,352,384,416,448,480},{16,48,80,..., dimensions={0} | all-to-all | bytes 1048576 | tf_op jit(solution)/shard_map/all_to_all | solution.py:243
  200.9 2.1 collective-permute-start.1
  203.1 10.4 %collective-permute-done.1 = f16[128,2048]{1,0:T(8,128)(2,1)S(1)} collective-permute-done((f16[128,2048]{1,0:T(8,128)(2,1)S(1)}, f16[128,2048]{1,0:T(8,128)(2,1)S(1)}, u32[]{:S(2)}, u32[]{:S(2)}) %collective-permute-start.1) | collective-permute-done | bytes 524320 | tf_op jit(solution)/shard_map/ppermute | solution.py:245
  213.5 0.2 broadcast_select_fusion.1
  213.7 0.2 maximum_convert_fusion
  214.0 1.5 fusion.17
  (20 shorter events, 0.9 us)
Async XLA Ops:
  1.3 1.4 copy-start.4
  5.4 5.9 %copy-start.5 = (bf16[256,1024]{1,0:T(8,128)(2,1)S(1)}, bf16[256,1024]{1,0:T(8,128)(2,1)}, u32[]{:S(2)}) copy-start(bf16[256,1024]{1,0:T(8,128)(2,1)} %param.7) | copy-start | bytes 1572868
  5.4 27.1 %all-to-all-start = ((bf16[16,48,1024]{2,1,0:T(8,128)(2,1)}), bf16[16,48,1024]{2,1,0:T(8,128)(2,1)S(1)}, u32[]{:S(2)}, u32[]{:S(2)}) async-start(bf16[16,48,1024]{2,1,0:T(8,128)(2,1)} %bitcast.1), calls=%async_computation | async-start | bytes 3145728 | tf_op jit(solution)/shard_map/all_to_all | solution.py:207
  90.0 0.9 copy-start.2
  90.9 20.8 %all-to-all-start.3 = ((f32[32,8,128]{2,1,0:T(8,128)}), f32[32,8,128]{2,1,0:T(8,128)S(1)}, u32[]{:S(2)}, u32[]{:S(2)}) async-start(f32[32,8,128]{2,1,0:T(8,128)} %get-tuple-element.21), calls=%async_computation.3 | async-start | bytes 262144 | tf_op jit(solution)/shard_map/all_to_all | solution.py:221
  96.8 1.2 copy-start
  111.7 1.4 copy-start.1
  113.1 1.1 copy-start.3
  116.1 15.5 %collective-permute-start = (f16[128,2176]{1,0:T(8,128)(2,1)S(1)}, f16[128,2176]{1,0:T(8,128)(2,1)S(1)}, u32[]{:S(2)}, u32[]{:S(2)}) collective-permute-start(f16[128,2176]{1,0:T(8,128)(2,1)S(1)} %pad_maximum_fusion), channel_id=1, source_target_pairs={{0,16},{16,0},{32,48},{48,32},{64,80},{80,64},{96,112},{112,96},{1... | collective-permute-start | bytes 1671176 | tf_op jit(solution)/shard_map/ppermute | solution.py:234
  200.9 12.6 %collective-permute-start.1 = (f16[128,2048]{1,0:T(8,128)(2,1)S(1)}, f16[128,2048]{1,0:T(8,128)(2,1)S(1)}, u32[]{:S(2)}, u32[]{:S(2)}) collective-permute-start(f16[128,2048]{1,0:T(8,128)(2,1)S(1)} %bitcast.18), channel_id=1, source_target_pairs={{0,16},{16,0},{32,48},{48,32},{64,80},{80,64},{96,112},{112,96},{1... | collective-permute-start | bytes 1572872 | tf_op jit(solution)/shard_map/ppermute | solution.py:245

commit v4 on v3

--- a/solution.py
+++ b/solution.py
@@ -10,9 +10,10 @@
 SINK = 3
 LANES = 128
 ROW_STEP = 256
+SAFE = 0.25
 F32 = jnp.float32
 BF16 = jnp.bfloat16
-VMEM_LIMIT = 40 * 1024 * 1024
+VMEM_LIMIT = 24 * 1024 * 1024
 
 
 def call(kernel, out_shape, n_in, flops, moved, scalars=0, scratch=()):
@@ -61,15 +62,14 @@
 
 
 def put_mass(mass, sent_ref):
-    comp = mass.shape[1]
-    parts = [mass[:, s : s + LANES] for s in range(0, comp, LANES)]
-    block = jnp.concatenate(parts + [jnp.zeros((8 - len(parts), LANES), F32)], axis=0)
-    sent_ref[...] = jnp.broadcast_to(block[None], sent_ref.shape)
-
-
-def get_mass(got_ref, comp):
+    for i in range(sent_ref.shape[1]):
+        part = mass[:, i * LANES : (i + 1) * LANES]
+        sent_ref[:, i, :] = jnp.broadcast_to(part, (sent_ref.shape[0], LANES))
+
+
+def get_mass(got_ref):
     block = jnp.sum(got_ref[...], axis=0)
-    return jnp.concatenate([block[i : i + 1] for i in range(comp // LANES)], axis=1)
+    return jnp.concatenate([block[i : i + 1] for i in range(block.shape[0])], axis=1)
 
 
 def score_step(x, quad_ref, lin_ref, off_ref, scale):
@@ -99,7 +99,7 @@
 
 def balance_kernel(target, got_ref, resp_ref, out_ref, sent_ref=None):
     rows, comp = resp_ref.shape
-    pull = target / get_mass(got_ref, comp)
+    pull = target / get_mass(got_ref)
     mass = jnp.zeros((1, comp), F32)
     for start in range(0, rows, ROW_STEP):
         span = slice(start, start + ROW_STEP)
@@ -121,32 +121,41 @@
 
 
 def put_moments(both, x_ref, high_ref, low_ref, first_ref, second_ref, total_ref):
-    half = first_ref.shape[0]
+    part = first_ref.shape[0]
     first = dot_tn(both, x_ref[...])
-    first_ref[...] = first[:half] + first[half:]
+    first_ref[...] = first[:part] + first[part:]
     second = dot_tn(both, high_ref[...])
-    second_ref[...] = second[:half] + second[half:] + dot_tn(both[:, :half], low_ref[...])
+    second_ref[...] = second[:part] + second[part:] + dot_tn(both[:, :part], low_ref[...])
     total = dot_tn(both, jnp.ones((both.shape[0], LANES), BF16))
-    total_ref[...] = total[:half] + total[half:]
+    total_ref[...] = total[:part] + total[part:]
+
+
+def split_parts(resp):
+    high = resp.astype(BF16)
+    low = (resp - high.astype(F32)).astype(BF16)
+    return jnp.concatenate([high, low], axis=1)
 
 
 def crossed_kernel(
-    target, side_ref, got_ref, resp_ref, x_ref, high_ref, low_ref,
+    target, place_ref, got_ref, resp_ref, x_ref, high_ref, low_ref,
     kept_ref, first_ref, second_ref, total_ref, lent_ref,
 ):
     rows, comp = resp_ref.shape
     half = comp // 2
-    upper = side_ref[0] == 1
-    pull = target / get_mass(got_ref, comp)
+    y, z = place_ref[0] % 2, place_ref[0] // 2
+    pull = target / get_mass(got_ref)
+    left = lax.broadcasted_iota(jnp.int32, (ROW_STEP, half), 1) < half // 2
     for start in range(0, rows, ROW_STEP):
         span = slice(start, start + ROW_STEP)
         resp = balance_step(resp_ref[span, :], pull)
-        high = resp.astype(BF16).astype(F32)
-        low = resp - high
-        lower_half = jnp.concatenate([high[:, :half], low[:, :half]], axis=1)
-        upper_half = jnp.concatenate([high[:, half:], low[:, half:]], axis=1)
-        kept_ref[span, :] = jnp.where(upper, upper_half, lower_half).astype(BF16)
-        lent_ref[span, :] = jnp.where(upper, lower_half, upper_half).astype(BF16)
+        same = jnp.where(z == 0, resp[:, :half], resp[:, half:])
+        other = jnp.where(z == 0, resp[:, half:], resp[:, :half])
+        same_turned = pltpu.roll(same, half // 2, 1)
+        other_turned = pltpu.roll(other, half // 2, 1)
+        lower = jnp.where(left, same, other_turned)
+        upper = jnp.where(left, same_turned, other)
+        kept_ref[span, :] = split_parts(jnp.where(y == 0, lower, upper))
+        lent_ref[span, :] = split_parts(jnp.where(y == 0, upper, lower))
     put_moments(lent_ref[...], x_ref, high_ref, low_ref, first_ref, second_ref, total_ref)
 
 
@@ -184,11 +193,11 @@
     block = rows_dev // groups
     comp = means.shape[0]
     half = comp // 2
-    deep = members // 2
-    lines = [[2 * z + y for z in range(deep)] for y in range(2)]
-    swap = [(i, i ^ 1) for i in range(members)]
-    upper = lax.axis_index("wide") % 2
-    own = upper.astype(jnp.int32).reshape(1)
+    quarter = comp // 4
+    deep = members // 4
+    lines = [[4 * z + i for z in range(deep)] for i in range(4)]
+    place = lax.axis_index("wide") % 4
+    y, z = place % 2, place // 2
     scale = width ** (-0.5)
     target = float(rows_dev * members / comp)
     big = rows_dev * width
@@ -198,7 +207,7 @@
         lax.all_to_all, axis_name="wide", split_axis=0, concat_axis=0, tiled=True
     )
     resp_shape = jax.ShapeDtypeStruct((rows_dev, comp), F32)
-    sent_shape = jax.ShapeDtypeStruct((members, 8, LANES), F32)
+    sent_shape = jax.ShapeDtypeStruct((members, comp // LANES, LANES), F32)
 
     ordered = call(
         functools.partial(order_kernel, groups),
@@ -230,22 +239,33 @@
     kept, *lent = call(
         functools.partial(crossed_kernel, target), (slab, *sums), 5, 5 * big * comp,
         6 * big + 8 * area, scalars=1, scratch=[pltpu.VMEM((rows_dev, comp), BF16)],
-    )(own, got, resp, mine, high, low)
-    there = lax.ppermute(with_total(*lent), "wide", swap)
+    )(place.astype(jnp.int32).reshape(1), got, resp, mine, high, low)
+
+    def to_partner(values, flip):
+        return lax.ppermute(values, "wide", [(i, i ^ flip) for i in range(members)])
+
+    sent = with_total(*lent)
+    there = [to_partner(sent[:quarter], 1), to_partner(sent[quarter:], 3)]
     here = call(kept_kernel, sums, 4, 5 * big * comp, 6 * big + 2 * area)(kept, mine, high, low)
-    first, second, total = split_total(there.astype(F32), width)
-    sent = with_total(first + here[0], second + here[1], total + here[2])
-    got = everyone(sent.reshape(deep, half // deep, sent.shape[1]), axis_index_groups=lines)
+    there.append(to_partner(with_total(*(h[quarter:] for h in here)), 2))
+    first, second, total = (h[:quarter] for h in here)
+    for got in there:
+        more = split_total(got.astype(F32), width)
+        first, second, total = first + more[0], second + more[1], total + more[2]
+    sent = with_total(SAFE * first, SAFE * second, SAFE * total)
+    got = everyone(sent.reshape(deep, quarter // deep, sent.shape[1]), axis_index_groups=lines)
     first, second, total = split_total(jnp.sum(got.astype(F32), axis=0), width)
     new_mean = first / total
     new_var = second / total - new_mean * new_mean + 0.01
     done = jnp.concatenate([new_mean, new_var], axis=1).astype(jnp.float16)
     got = everyone(jnp.broadcast_to(done[None], (deep,) + done.shape), axis_index_groups=lines)
-    here = got.reshape(half, 2 * width)
-    there = lax.ppermute(here, "wide", swap)
-    low = jnp.where(upper == 0, here, there)
-    high = jnp.where(upper == 0, there, here)
-    out = jnp.concatenate([low, high], axis=0).astype(F32)
+    here = got.reshape(quarter, 2 * width)
+    by = [here] + [to_partner(here, flip) for flip in (1, 2, 3)]
+    near = [jnp.where(y == 0, by[0], by[1]), jnp.where(y == 0, by[1], by[0])]
+    far = [jnp.where(y == 0, by[2], by[3]), jnp.where(y == 0, by[3], by[2])]
+    low = [jnp.where(z == 0, a, b) for a, b in zip(near, far)]
+    high = [jnp.where(z == 0, b, a) for a, b in zip(near, far)]
+    out = jnp.concatenate(low + high, axis=0).astype(F32)
     return (out[:, :width], out[:, width:])
 
 

time: 216 us -> 191 us (0.88)
  blocking collectives: 123 us -> 91.9 us
  starting transfers between devices: 16.8 us -> 33.5 us
  waiting for transfers between devices: 54.6 us -> 43.2 us
    ppermute x2 -> x6, starting transfers between devices: 5.61 us -> 21.4 us  [to_partner(): return lax.ppermute(values, 'wide', [(i, i ^ flip) for i in range(members)])]
    all_to_all x1, blocking collectives: 37.2 us -> 23 us  [on_device(): everyone(sent.reshape(deep, quarter // deep, sent.shape[1]), axis_index_g...]
    all_to_all x1, blocking collectives: 30.9 us -> 20.5 us  [on_device(): everyone(jnp.broadcast_to(done[None], (deep,) + done.shape), axis_index_g...]
    ppermute x2 -> x6, waiting for transfers between devices: 21.2 us -> 12.7 us  [to_partner(): return lax.ppermute(values, 'wide', [(i, i ^ flip) for i in range(members)])]
    all_to_all x2, blocking collectives: 55 us -> 48.3 us  [on_device(): got = everyone(sent)]
    all_to_all x1, waiting for transfers between devices: 13.8 us -> 10.8 us  [on_device(): got = everyone(sent)]
  transfers between devices with their start and end apart: 4 -> 8, of which waited for: 4 -> 8; matrix products, arithmetic and copies ran while one was open for 1% -> 1% of each run, Pallas kernels for 1% -> 1%
where the time goes in v4:
time: 191 us; the launch traced here: 190 us
  blocking collectives  91.9 us (48%)
  waiting for transfers between devices  43.2 us (23%)
  starting transfers between devices  33.5 us (18%)
  Pallas kernels  8.79 us (5%)
  local copies, waits for them, and re-layouts  8.24 us (4%)
  other arithmetic  3.87 us (2%)
    all_to_all x2, blocking collectives, on_device(): got = everyone(sent)  48.3 us
    all_to_all x1, blocking collectives, on_device(): everyone(sent.reshape(deep, quarter // deep, sent.shape[1]), axis_index_g...  23 us
    ppermute x6, starting transfers between devices, to_partner(): return lax.ppermute(values, 'wide', [(i, i ^ flip) for i in range(members)])  21.4 us
    all_to_all x1, blocking collectives, on_device(): everyone(jnp.broadcast_to(done[None], (deep,) + done.shape), axis_index_g...  20.5 us
    all_to_all x1, waiting for transfers between devices, on_device(): lax.all_to_all(ordered.reshape(groups, block, width), 'narrow', split_axi...  19.7 us
    ppermute x6, waiting for transfers between devices, to_partner(): return lax.ppermute(values, 'wide', [(i, i ^ flip) for i in range(members)])  12.7 us
    all_to_all x1, waiting for transfers between devices, on_device(): got = everyone(sent)  10.8 us
    all_to_all x1, starting transfers between devices, on_device(): got = everyone(sent)  6.15 us
  transfers between devices with their start and end apart: 8, of which 8 were waited for; matrix products, arithmetic and copies ran while one was open for 1% of the time, Pallas kernels for 1%

profile of v4, /device:TPU:24, one launch (start us, length us, event | category | flops | bytes accessed | tf_op | source)
XLA Modules:
  0.0 190.4 jit_solution(9542582891852017926)
XLA Ops:
  0.6 0.7 reshape.51.dest_ref
  1.3 1.4 copy-done.4
  2.7 2.7 %shard_map.59 = bf16[768,1024]{1,0:T(8,128)(2,1)} custom-call(s32[1,768]{1,0:T(1,128)S(1)} %reshape.51.dest_ref, bf16[768,1024]{1,0:T(8,128)(2,1)S(1)} %copy-done.4), custom_call_target="tpu_custom_call" | custom-call | flops 1207959552 | bytes 3145728 | tf_op jit(solution)/shard_map/pallas_call | solution.py:212
  5.5 5.9 %all-to-all-start = ((bf16[16,48,1024]{2,1,0:T(8,128)(2,1)}), bf16[16,48,1024]{2,1,0:T(8,128)(2,1)S(1)}, u32[]{:S(2)}, u32[]{:S(2)}) async-start(bf16[16,48,1024]{2,1,0:T(8,128)(2,1)} %bitcast.1), calls=%async_computation | async-start | bytes 3145728 | tf_op jit(solution)/shard_map/all_to_all | solution.py:216
  11.4 1.5 fusion.1
  12.9 19.7 %all-to-all-done = bf16[16,48,1024]{2,1,0:T(8,128)(2,1)S(1)} async-done(((bf16[16,48,1024]{2,1,0:T(8,128)(2,1)}), bf16[16,48,1024]{2,1,0:T(8,128)(2,1)S(1)}, u32[]{:S(2)}, u32[]{:S(2)}) %all-to-all-start) | async-done | bytes 1572896 | tf_op jit(solution)/shard_map/all_to_all | solution.py:216
  32.6 1.2 shard_map.60
  33.8 30.5 %all_to_all.30.got_ref = f32[32,2,128]{2,1,0:T(2,128)S(1)} all-to-all(f32[32,2,128]{2,1,0:T(2,128)S(1)} %get-tuple-element.17), channel_id=1, replica_groups=mesh['wide'=32,'narrow'=16] {'wide'}, dimensions={0} | all-to-all | bytes 65536 | tf_op jit(solution)/shard_map/all_to_all | solution.py:224
  64.6 17.8 %all_to_all.31.got_ref = f32[32,2,128]{2,1,0:T(2,128)S(1)} all-to-all(f32[32,2,128]{2,1,0:T(2,128)S(1)} %get-tuple-element.19), channel_id=1, replica_groups=mesh['wide'=32,'narrow'=16] {'wide'}, dimensions={0} | all-to-all | bytes 65536 | tf_op jit(solution)/shard_map/all_to_all | solution.py:230
  82.4 0.9 shard_map.62
  83.3 0.9 copy-done.2
  84.2 6.1 %all-to-all-start.3 = ((f32[32,2,128]{2,1,0:T(2,128)}), f32[32,2,128]{2,1,0:T(2,128)S(1)}, u32[]{:S(2)}, u32[]{:S(2)}) async-start(f32[32,2,128]{2,1,0:T(2,128)} %get-tuple-element.21), calls=%async_computation.3 | async-start | bytes 65536 | tf_op jit(solution)/shard_map/all_to_all | solution.py:230
  91.0 1.1 copy-done
  92.1 10.8 %all-to-all-done.3.got_ref = f32[32,2,128]{2,1,0:T(2,128)S(1)} async-done(((f32[32,2,128]{2,1,0:T(2,128)}), f32[32,2,128]{2,1,0:T(2,128)S(1)}, u32[]{:S(2)}, u32[]{:S(2)}) %all-to-all-start.3) | async-done | bytes 32800 | tf_op jit(solution)/shard_map/all_to_all | solution.py:230
  102.9 1.4 copy-done.1
  104.3 1.1 copy-done.3
  105.5 1.8 shard_map.64
  107.7 4.5 %collective-permute-start = (f16[64,2176]{1,0:T(8,128)(2,1)S(1)}, f16[64,2176]{1,0:T(8,128)(2,1)S(1)}, u32[]{:S(2)}, u32[]{:S(2)}) collective-permute-start(f16[64,2176]{1,0:T(8,128)(2,1)S(1)} %get-tuple-element.42), channel_id=1, source_target_pairs={{0,16},{16,0},{32,48},{48,32},{64,80},{80,64},{96,112},{112,96},{1... | collective-permute-start | bytes 835592 | tf_op jit(solution)/shard_map/ppermute | solution.py:245
  112.2 2.9 %collective-permute-start.1 = (f16[64,2176]{1,0:T(8,128)(2,1)S(1)}, f16[64,2176]{1,0:T(8,128)(2,1)S(1)}, u32[]{:S(2)}, u32[]{:S(2)}) collective-permute-start(f16[64,2176]{1,0:T(8,128)(2,1)S(1)} %get-tuple-element.43), channel_id=1, source_target_pairs={{0,48},{16,32},{32,16},{48,0},{64,112},{80,96},{96,80},{112,64},{1... | collective-permute-start | bytes 835592 | tf_op jit(solution)/shard_map/ppermute | solution.py:245
  115.1 1.3 shard_map.65
  116.6 3.3 %collective-permute-start.2 = (f16[64,2176]{1,0:T(8,128)(2,1)S(1)}, f16[64,2176]{1,0:T(8,128)(2,1)S(1)}, u32[]{:S(2)}, u32[]{:S(2)}) collective-permute-start(f16[64,2176]{1,0:T(8,128)(2,1)S(1)} %pad_maximum_fusion.1), channel_id=1, source_target_pairs={{0,32},{16,48},{32,0},{48,16},{64,96},{80,112},{96,64},{112,80},{1... | collective-permute-start | bytes 835592 | tf_op jit(solution)/shard_map/ppermute | solution.py:245
  119.9 1.2 collective-permute-done
  121.1 3.8 %collective-permute-done.1 = f16[64,2176]{1,0:T(8,128)(2,1)S(1)} collective-permute-done((f16[64,2176]{1,0:T(8,128)(2,1)S(1)}, f16[64,2176]{1,0:T(8,128)(2,1)S(1)}, u32[]{:S(2)}, u32[]{:S(2)}) %collective-permute-start.1) | collective-permute-done | bytes 278560 | tf_op jit(solution)/shard_map/ppermute | solution.py:245
  126.6 23.0 %all_to_all.32 = f16[8,8,2176]{2,1,0:T(8,128)(2,1)S(1)} all-to-all(f16[8,8,2176]{2,1,0:T(8,128)(2,1)S(1)} %pad_maximum_fusion.2), channel_id=1, replica_groups={{0,64,128,192,256,320,384,448},{16,80,144,208,272,336,400,464},{32,96,1..., dimensions={0} | all-to-all | bytes 557056 | tf_op jit(solution)/shard_map/all_to_all | solution.py:256
  149.9 20.5 %all_to_all.33 = f16[8,8,2048]{2,1,0:T(8,128)(2,1)S(1)} all-to-all(f16[8,8,2048]{2,1,0:T(8,128)(2,1)S(1)} %broadcast_in_dim.2), channel_id=1, replica_groups={{0,64,128,192,256,320,384,448},{16,80,144,208,272,336,400,464},{32,96,1..., dimensions={0} | all-to-all | bytes 524288 | tf_op jit(solution)/shard_map/all_to_all | solution.py:261
  170.5 5.0 %collective-permute-start.3 = (f16[64,2048]{1,0:T(8,128)(2,1)S(1)}, f16[64,2048]{1,0:T(8,128)(2,1)S(1)}, u32[]{:S(2)}, u32[]{:S(2)}) collective-permute-start(f16[64,2048]{1,0:T(8,128)(2,1)S(1)} %bitcast.20), channel_id=1, source_target_pairs={{0,16},{16,0},{32,48},{48,32},{64,80},{80,64},{96,112},{112,96},{1... | collective-permute-start | bytes 786440 | tf_op jit(solution)/shard_map/ppermute | solution.py:245
  175.5 1.9 %collective-permute-start.4 = (f16[64,2048]{1,0:T(8,128)(2,1)S(1)}, f16[64,2048]{1,0:T(8,128)(2,1)S(1)}, u32[]{:S(2)}, u32[]{:S(2)}) collective-permute-start(f16[64,2048]{1,0:T(8,128)(2,1)S(1)} %bitcast.21), channel_id=1, source_target_pairs={{0,32},{16,48},{32,0},{48,16},{64,96},{80,112},{96,64},{112,80},{1... | collective-permute-start | bytes 786440 | tf_op jit(solution)/shard_map/ppermute | solution.py:245
  177.4 3.8 %collective-permute-start.5 = (f16[64,2048]{1,0:T(8,128)(2,1)S(1)}, f16[64,2048]{1,0:T(8,128)(2,1)S(1)}, u32[]{:S(2)}, u32[]{:S(2)}) collective-permute-start(f16[64,2048]{1,0:T(8,128)(2,1)S(1)} %bitcast.22), channel_id=1, source_target_pairs={{0,48},{16,32},{32,16},{48,0},{64,112},{80,96},{96,80},{112,64},{1... | collective-permute-start | bytes 786440 | tf_op jit(solution)/shard_map/ppermute | solution.py:245
  181.3 0.9 collective-permute-done.3
  182.2 1.6 collective-permute-done.4
  183.8 4.6 %collective-permute-done.5 = f16[64,2048]{1,0:T(8,128)(2,1)S(1)} collective-permute-done((f16[64,2048]{1,0:T(8,128)(2,1)S(1)}, f16[64,2048]{1,0:T(8,128)(2,1)S(1)}, u32[]{:S(2)}, u32[]{:S(2)}) %collective-permute-start.5) | collective-permute-done | bytes 262176 | tf_op jit(solution)/shard_map/ppermute | solution.py:245
  189.0 1.5 fusion.22
  (36 shorter events, 4.0 us)
Async XLA Ops:
  1.3 1.4 copy-start.4
  5.5 5.9 %copy-start.5 = (bf16[256,1024]{1,0:T(8,128)(2,1)S(1)}, bf16[256,1024]{1,0:T(8,128)(2,1)}, u32[]{:S(2)}) copy-start(bf16[256,1024]{1,0:T(8,128)(2,1)} %param.7) | copy-start | bytes 1572868
  5.5 27.1 %all-to-all-start = ((bf16[16,48,1024]{2,1,0:T(8,128)(2,1)}), bf16[16,48,1024]{2,1,0:T(8,128)(2,1)S(1)}, u32[]{:S(2)}, u32[]{:S(2)}) async-start(bf16[16,48,1024]{2,1,0:T(8,128)(2,1)} %bitcast.1), calls=%async_computation | async-start | bytes 3145728 | tf_op jit(solution)/shard_map/all_to_all | solution.py:216
  83.3 0.9 copy-start.2
  84.2 18.7 %all-to-all-start.3 = ((f32[32,2,128]{2,1,0:T(2,128)}), f32[32,2,128]{2,1,0:T(2,128)S(1)}, u32[]{:S(2)}, u32[]{:S(2)}) async-start(f32[32,2,128]{2,1,0:T(2,128)} %get-tuple-element.21), calls=%async_computation.3 | async-start | bytes 65536 | tf_op jit(solution)/shard_map/all_to_all | solution.py:230
  91.0 1.2 copy-start
  102.9 1.4 copy-start.1
  104.3 1.1 copy-start.3
  107.7 13.4 %collective-permute-start = (f16[64,2176]{1,0:T(8,128)(2,1)S(1)}, f16[64,2176]{1,0:T(8,128)(2,1)S(1)}, u32[]{:S(2)}, u32[]{:S(2)}) collective-permute-start(f16[64,2176]{1,0:T(8,128)(2,1)S(1)} %get-tuple-element.42), channel_id=1, source_target_pairs={{0,16},{16,0},{32,48},{48,32},{64,80},{80,64},{96,112},{112,96},{1... | collective-permute-start | bytes 835592 | tf_op jit(solution)/shard_map/ppermute | solution.py:245
  112.2 12.7 %collective-permute-start.1 = (f16[64,2176]{1,0:T(8,128)(2,1)S(1)}, f16[64,2176]{1,0:T(8,128)(2,1)S(1)}, u32[]{:S(2)}, u32[]{:S(2)}) collective-permute-start(f16[64,2176]{1,0:T(8,128)(2,1)S(1)} %get-tuple-element.43), channel_id=1, source_target_pairs={{0,48},{16,32},{32,16},{48,0},{64,112},{80,96},{96,80},{112,64},{1... | collective-permute-start | bytes 835592 | tf_op jit(solution)/shard_map/ppermute | solution.py:245
  116.6 9.4 %collective-permute-start.2 = (f16[64,2176]{1,0:T(8,128)(2,1)S(1)}, f16[64,2176]{1,0:T(8,128)(2,1)S(1)}, u32[]{:S(2)}, u32[]{:S(2)}) collective-permute-start(f16[64,2176]{1,0:T(8,128)(2,1)S(1)} %pad_maximum_fusion.1), channel_id=1, source_target_pairs={{0,32},{16,48},{32,0},{48,16},{64,96},{80,112},{96,64},{112,80},{1... | collective-permute-start | bytes 835592 | tf_op jit(solution)/shard_map/ppermute | solution.py:245
  170.5 11.7 %collective-permute-start.3 = (f16[64,2048]{1,0:T(8,128)(2,1)S(1)}, f16[64,2048]{1,0:T(8,128)(2,1)S(1)}, u32[]{:S(2)}, u32[]{:S(2)}) collective-permute-start(f16[64,2048]{1,0:T(8,128)(2,1)S(1)} %bitcast.20), channel_id=1, source_target_pairs={{0,16},{16,0},{32,48},{48,32},{64,80},{80,64},{96,112},{112,96},{1... | collective-permute-start | bytes 786440 | tf_op jit(solution)/shard_map/ppermute | solution.py:245
  175.5 8.3 %collective-permute-start.4 = (f16[64,2048]{1,0:T(8,128)(2,1)S(1)}, f16[64,2048]{1,0:T(8,128)(2,1)S(1)}, u32[]{:S(2)}, u32[]{:S(2)}) collective-permute-start(f16[64,2048]{1,0:T(8,128)(2,1)S(1)} %bitcast.21), channel_id=1, source_target_pairs={{0,32},{16,48},{32,0},{48,16},{64,96},{80,112},{96,64},{112,80},{1... | collective-permute-start | bytes 786440 | tf_op jit(solution)/shard_map/ppermute | solution.py:245
  177.4 10.9 %collective-permute-start.5 = (f16[64,2048]{1,0:T(8,128)(2,1)S(1)}, f16[64,2048]{1,0:T(8,128)(2,1)S(1)}, u32[]{:S(2)}, u32[]{:S(2)}) collective-permute-start(f16[64,2048]{1,0:T(8,128)(2,1)S(1)} %bitcast.22), channel_id=1, source_target_pairs={{0,48},{16,32},{32,16},{48,0},{64,112},{80,96},{96,80},{112,64},{1... | collective-permute-start | bytes 786440 | tf_op jit(solution)/shard_map/ppermute | solution.py:245

commit v5 on v4

v5 whole, which is shorter than its diff:
```python
import functools

import jax
import jax.numpy as jnp
from jax import lax
from jax.experimental import pallas as pl
from jax.experimental.pallas import tpu as pltpu
from jax.sharding import PartitionSpec as P

SINK = 3
LANES = 128
ROW_STEP = 256
SAFE = 0.25
F32 = jnp.float32
BF16 = jnp.bfloat16
VMEM_LIMIT = 24 * 1024 * 1024
ALL_VMEM = 60 * 1024 * 1024


def call(
    kernel, out_shape, n_in, flops, moved, scalars=0, remote=0, scratch=(), room=VMEM_LIMIT
):
    smem = pl.BlockSpec(memory_space=pltpu.SMEM)
    vmem = pl.BlockSpec(memory_space=pltpu.VMEM)
    hbm = pl.BlockSpec(memory_space=pltpu.HBM)
    return pl.pallas_call(
        kernel,
        out_shape=out_shape,
        in_specs=[smem] * scalars + [vmem] * n_in + [hbm] * remote,
        out_specs=jax.tree.map(lambda _: vmem, out_shape),
        scratch_shapes=scratch,
        compiler_params=pltpu.CompilerParams(vmem_limit_bytes=room),
        cost_estimate=pl.CostEstimate(flops=flops, bytes_accessed=moved, transcendentals=0),
    )


def dot_nt(a, b):
    return lax.dot_general(a, b, (((1,), (1,)), ((), ())), preferred_element_type=F32)


def dot_tn(a, b):
    return lax.dot_general(a, b, (((0,), (0,)), ((), ())), preferred_element_type=F32)


def order_kernel(groups, dest_ref, embed_hbm, out_ref, embed_ref, arrival):
    rows = embed_ref.shape[0]
    load = pltpu.make_async_copy(embed_hbm, embed_ref, arrival)
    load.start()
    block = rows // groups
    before = lax.broadcasted_iota(jnp.int32, (LANES, LANES), 0)
    after = lax.broadcasted_iota(jnp.int32, (LANES, LANES), 1)
    earlier = jnp.where(before < after, 1.0, 0.0).astype(BF16)
    group = lax.broadcasted_iota(jnp.int32, (groups, LANES), 0)
    base = (group * block).astype(F32)
    count = jnp.zeros((groups, 1), F32)
    places = []
    for start in range(0, rows, LANES):
        hot = jnp.where(group == dest_ref[:, start : start + LANES], 1.0, 0.0)
        rank = jnp.dot(hot.astype(BF16), earlier, preferred_element_type=F32) + count
        places.append(jnp.sum(hot * (rank + base), axis=0, keepdims=True))
        count = count + jnp.sum(hot, axis=1, keepdims=True)
    place = jnp.concatenate(places, axis=1).astype(jnp.int32)
    load.wait()
    for start in range(0, rows, ROW_STEP):
        slot = lax.broadcasted_iota(jnp.int32, (ROW_STEP, rows), 0) + start
        pick = jnp.where(slot == place, 1.0, 0.0).astype(BF16)
        got = jnp.dot(pick, embed_ref[...], preferred_element_type=F32)
        out_ref[start : start + ROW_STEP, :] = got.astype(BF16)


def put_mass(mass, sent_ref):
    for i in range(sent_ref.shape[1]):
        part = mass[:, i * LANES : (i + 1) * LANES]
        sent_ref[:, i, :] = jnp.broadcast_to(part, (sent_ref.shape[0], LANES))


def get_mass(got_ref):
    block = jnp.sum(got_ref[...], axis=0)
    return jnp.concatenate([block[i : i + 1] for i in range(block.shape[0])], axis=1)


def score_kernel(
    scale, x_ref, quad_ref, lin_ref, off_ref, resp_ref, high_ref, low_ref, sent_ref
):
    rows = x_ref.shape[0]
    mass = jnp.zeros((1, resp_ref.shape[1]), F32)
    for start in range(0, rows, ROW_STEP):
        span = slice(start, start + ROW_STEP)
        x = x_ref[span, :]
        wide = x.astype(F32)
        square = wide * wide
        high = square.astype(BF16)
        high_ref[span, :] = high
        low_ref[span, :] = (square - high.astype(F32)).astype(BF16)
        raw = dot_nt(high, quad_ref[...]) + dot_nt(x, lin_ref[...])
        score = scale * (raw + off_ref[...])
        lifted = jnp.exp(score - jnp.max(score, axis=1, keepdims=True))
        resp = lifted / jnp.sum(lifted, axis=1, keepdims=True)
        resp_ref[span, :] = resp
        mass = mass + jnp.sum(resp, axis=0, keepdims=True)
    put_mass(mass, sent_ref)


def balance_step(resp, pull):
    scaled = resp * pull
    return scaled / jnp.sum(scaled, axis=1, keepdims=True)


def balance_kernel(target, got_ref, resp_ref, out_ref, sent_ref):
    rows, comp = resp_ref.shape
    pull = target / get_mass(got_ref)
    mass = jnp.zeros((1, comp), F32)
    for start in range(0, rows, ROW_STEP):
        span = slice(start, start + ROW_STEP)
        resp = balance_step(resp_ref[span, :], pull)
        out_ref[span, :] = resp
        mass = mass + jnp.sum(resp, axis=0, keepdims=True)
    put_mass(mass, sent_ref)


def total_parts(total):
    coarse = jnp.floor(total / 8)
    rest = total - 8 * coarse
    middle = jnp.floor(rest * 2**6)
    rest = (rest - middle / 2**6) * 2**15
    fine = jnp.floor(rest)
    lane = lax.broadcasted_iota(jnp.int32, total.shape, 1)
    return jnp.where(
        lane < 64,
        jnp.where(lane < 32, coarse, middle),
        jnp.where(lane < 96, fine, rest - fine),
    )


def put_moments(both, x_ref, high_ref, low_ref, out_ref):
    part = out_ref.shape[0]
    width = x_ref.shape[1]
    first = dot_tn(both, x_ref[...])
    out_ref[:, :width] = first[:part] + first[part:]
    second = dot_tn(both, high_ref[...])
    out_ref[:, width : 2 * width] = (
        second[:part] + second[part:] + dot_tn(both[:, :part], low_ref[...])
    )
    total = dot_tn(both, jnp.ones((both.shape[0], LANES), BF16))
    out_ref[:, 2 * width :] = total_parts(total[:part] + total[part:])


def split_parts(resp):
    high = resp.astype(BF16)
    low = (resp - high.astype(F32)).astype(BF16)
    return jnp.concatenate([high, low], axis=1)


def crossed_kernel(
    target, place_ref, got_ref, resp_ref, x_ref, high_ref, low_ref,
    kept_ref, out_ref, lent_ref,
):
    rows, comp = resp_ref.shape
    half = comp // 2
    y, z = place_ref[0] % 2, place_ref[0] // 2
    pull = target / get_mass(got_ref)
    left = lax.broadcasted_iota(jnp.int32, (ROW_STEP, half), 1) < half // 2
    for start in range(0, rows, ROW_STEP):
        span = slice(start, start + ROW_STEP)
        resp = balance_step(resp_ref[span, :], pull)
        same = jnp.where(z == 0, resp[:, :half], resp[:, half:])
        other = jnp.where(z == 0, resp[:, half:], resp[:, :half])
        same_turned = pltpu.roll(same, half // 2, 1)
        other_turned = pltpu.roll(other, half // 2, 1)
        lower = jnp.where(left, same, other_turned)
        upper = jnp.where(left, same_turned, other)
        kept_ref[span, :] = split_parts(jnp.where(y == 0, lower, upper))
        lent_ref[span, :] = split_parts(jnp.where(y == 0, upper, lower))
    put_moments(lent_ref[...], x_ref, high_ref, low_ref, out_ref)


def kept_kernel(kept_ref, x_ref, high_ref, low_ref, out_ref):
    put_moments(kept_ref[...], x_ref, high_ref, low_ref, out_ref)


def weights(mean_block, var_block):
    prec = 1.0 / var_block.astype(F32)
    mean_wide = mean_block.astype(F32)
    quad = (-0.5 * prec).astype(BF16)
    linear = (mean_wide * prec).astype(BF16)
    offset = -0.5 * jnp.sum(
        jnp.log(var_block.astype(F32)) + mean_wide * mean_wide * prec, axis=1
    )
    return quad, linear, offset[None, :]


def on_device(embed, dest, means, variances):
    rows_dev, width = embed.shape
    groups = lax.axis_size("narrow")
    members = lax.axis_size("wide")
    block = rows_dev // groups
    comp = means.shape[0]
    half = comp // 2
    quarter = comp // 4
    deep = members // 4
    lines = [[4 * z + i for z in range(deep)] for i in range(4)]
    blocks = [[4 * z + i for i in range(4)] for z in range(deep)]
    place = (lax.axis_index("wide") % 4).astype(jnp.int32).reshape(1)
    scale = width ** (-0.5)
    target = float(rows_dev * members / comp)
    big = rows_dev * width
    area = rows_dev * comp

    everyone = functools.partial(
        lax.all_to_all, axis_name="wide", split_axis=0, concat_axis=0, tiled=True
    )
    resp_shape = jax.ShapeDtypeStruct((rows_dev, comp), F32)
    sent_shape = jax.ShapeDtypeStruct((members, comp // LANES, LANES), F32)

    ordered = call(
        functools.partial(order_kernel, groups),
        jax.ShapeDtypeStruct(embed.shape, BF16), 1, 2 * rows_dev * big, 4 * big, remote=1,
        scratch=[pltpu.VMEM(embed.shape, BF16), pltpu.SemaphoreType.DMA], room=ALL_VMEM,
    )(dest.reshape(1, rows_dev), embed)
    mine = lax.all_to_all(
        ordered.reshape(groups, block, width), "narrow", split_axis=0, concat_axis=0, tiled=True
    ).reshape(rows_dev, width)
    mine, place = lax.optimization_barrier((mine, place))
    quad, linear, offset = weights(means, variances)
    plain = jax.ShapeDtypeStruct((rows_dev, width), BF16)
    resp, high, low, sent = call(
        functools.partial(score_kernel, scale), (resp_shape, plain, plain, sent_shape),
        4, 4 * big * comp, 6 * big + 4 * area,
    )(mine, quad, linear, offset)
    got = everyone(sent)
    for step in range(SINK - 1):
        resp, sent = call(
            functools.partial(balance_kernel, target), (resp_shape, sent_shape),
            2, 4 * area, 8 * area,
        )(got, resp)
        got = everyone(sent)
    sums = jax.ShapeDtypeStruct((half, 2 * width + LANES), F32)
    slab = jax.ShapeDtypeStruct((rows_dev, comp), BF16)
    kept, lent = call(
        functools.partial(crossed_kernel, target), (slab, sums), 5, 5 * big * comp,
        6 * big + 8 * area, scalars=1, scratch=[pltpu.VMEM((rows_dev, comp), BF16)],
    )(place, got, resp, mine, high, low)

    def to_partner(values, flip):
        swap = [(i, i ^ flip) for i in range(members)]
        return lax.ppermute(values.astype(jnp.float16), "wide", swap).astype(F32)

    there = to_partner(lent[quarter:], 3), to_partner(lent[:quarter], 1)
    here = call(kept_kernel, sums, 4, 5 * big * comp, 6 * big + 2 * area)(kept, mine, high, low)
    near = to_partner(here[quarter:], 2)
    sent = (SAFE * (here[:quarter] + near + there[0] + there[1])).astype(jnp.float16)
    got = everyone(sent.reshape(deep, quarter // deep, sent.shape[1]), axis_index_groups=lines)
    got = jnp.sum(got.astype(F32), axis=0)
    first, second = got[:, :width], got[:, width : 2 * width]
    units = (8.0, 2.0**-6, 2.0**-15, 2.0**-15)
    total = sum(u * got[:, 2 * width + 32 * i :][:, :1] for i, u in enumerate(units))
    new_mean = first / total
    new_var = second / total - new_mean * new_mean + 0.01
    done = jnp.concatenate([new_mean, new_var], axis=1).astype(jnp.float16)
    got = everyone(jnp.broadcast_to(done[None], (deep,) + done.shape), axis_index_groups=lines)
    here = got.reshape(1, quarter, 2 * width)
    got = everyone(jnp.broadcast_to(here, (4,) + here.shape[1:]), axis_index_groups=blocks)
    out = got.reshape(comp, 2 * width).astype(F32)
    return (out[:, :width], out[:, width:])


def solution(mesh):
    return jax.shard_map(
        on_device,
        mesh=mesh,
        in_specs=(
            P(("wide", "narrow"), None),
            P(("wide", "narrow")),
            P("narrow", None),
            P("narrow", None),
        ),
        out_specs=(P("narrow", None), P("narrow", None)),
        check_vma=False,
    )
```

time: 191 us -> 184 us (0.963)
  blocking collectives: 91.9 us -> 124 us
  waiting for transfers between devices: 43.2 us -> 25.8 us
  starting transfers between devices: 33.5 us -> 16.6 us
  local copies, waits for them, and re-layouts: 8.24 us -> 2.96 us
    all_to_all x2 -> x3, blocking collectives: 48.3 us -> 66.2 us  [on_device(): got = everyone(sent)]
    all_to_all x0 -> x1, blocking collectives: none -> 14 us  [on_device(): everyone(jnp.broadcast_to(here, (4,) + here.shape[1:]), axis_index_groups...]
    all_to_all x1 -> x0, waiting for transfers between devices: 10.8 us -> none  [on_device(): got = everyone(sent)]
    ppermute x6 -> x3, starting transfers between devices: 21.4 us -> 10.7 us  [to_partner(): return lax.ppermute(values.astype(jnp.float16), 'wide', swap).astype(F32)]
    ppermute x6 -> x3, waiting for transfers between devices: 12.7 us -> 6.11 us  [to_partner(): return lax.ppermute(values.astype(jnp.float16), 'wide', swap).astype(F32)]
    all_to_all x1 -> x0, starting transfers between devices: 6.15 us -> none  [on_device(): got = everyone(sent)]
    unnamed x12 -> x2, local copies, waits for them, and re-layouts: 5.98 us -> 0.01 us
    pallas_call x1, Pallas kernels: 2.74 us -> 4.65 us  [on_device(): call(functools.partial(order_kernel, groups), jax.ShapeDtypeStruct(embed....]
  transfers between devices with their start and end apart: 8 -> 4, of which waited for: 8 -> 4; matrix products, arithmetic and copies ran while one was open for 1% -> 1% of each run, Pallas kernels for 1% -> 1%
where the time goes in v5:
time: 184 us; the launch traced here: 182 us
  blocking collectives  124 us (67%)
  waiting for transfers between devices  25.8 us (14%)
  starting transfers between devices  16.6 us (9%)
  Pallas kernels  9.6 us (5%)
  local copies, waits for them, and re-layouts  2.96 us (2%)
  other arithmetic  2.35 us (1%)
    all_to_all x3, blocking collectives, on_device(): got = everyone(sent)  66.2 us
    all_to_all x1, blocking collectives, on_device(): everyone(sent.reshape(deep, quarter // deep, sent.shape[1]), axis_index_g...  23 us
    all_to_all x1, blocking collectives, on_device(): everyone(jnp.broadcast_to(done[None], (deep,) + done.shape), axis_index_g...  20.4 us
    all_to_all x1, waiting for transfers between devices, on_device(): lax.all_to_all(ordered.reshape(groups, block, width), 'narrow', split_axi...  19.7 us
    all_to_all x1, blocking collectives, on_device(): everyone(jnp.broadcast_to(here, (4,) + here.shape[1:]), axis_index_groups...  14 us
    ppermute x3, starting transfers between devices, to_partner(): return lax.ppermute(values.astype(jnp.float16), 'wide', swap).astype(F32)  10.7 us
    ppermute x3, waiting for transfers between devices, to_partner(): return lax.ppermute(values.astype(jnp.float16), 'wide', swap).astype(F32)  6.11 us
    all_to_all x1, starting transfers between devices, on_device(): lax.all_to_all(ordered.reshape(groups, block, width), 'narrow', split_axi...  5.92 us
  transfers between devices with their start and end apart: 4, of which 4 were waited for; matrix products, arithmetic and copies ran while one was open for 1% of the time, Pallas kernels for 1%

profile of v5, /device:TPU:24, one launch (start us, length us, event | category | flops | bytes accessed | tf_op | source)
XLA Modules:
  0.0 181.9 jit_solution(1214265839205065086)
XLA Ops:
  0.6 1.3 reshape.48.dest_ref
  1.9 4.6 %shard_map.59 = bf16[768,1024]{1,0:T(8,128)(2,1)} custom-call(s32[1,768]{1,0:T(1,128)} %reshape.48.dest_ref, bf16[768,1024]{1,0:T(8,128)(2,1)} %embed_hbm.1), custom_call_target="tpu_custom_call" | custom-call | flops 1207959552 | bytes 3145728 | tf_op jit(solution)/shard_map/pallas_call | solution.py:215
  6.6 0.0 copy-start
  6.6 5.9 %all-to-all-start = ((bf16[16,48,1024]{2,1,0:T(8,128)(2,1)}), bf16[16,48,1024]{2,1,0:T(8,128)(2,1)S(1)}, u32[]{:S(2)}, u32[]{:S(2)}) async-start(bf16[16,48,1024]{2,1,0:T(8,128)(2,1)} %bitcast.14), calls=%async_computation | async-start | bytes 3145728 | tf_op jit(solution)/shard_map/all_to_all | solution.py:220
  12.5 0.0 copy-done
  12.5 1.5 fusion.1
  14.0 19.7 %all-to-all-done = bf16[16,48,1024]{2,1,0:T(8,128)(2,1)S(1)} async-done(((bf16[16,48,1024]{2,1,0:T(8,128)(2,1)}), bf16[16,48,1024]{2,1,0:T(8,128)(2,1)S(1)}, u32[]{:S(2)}, u32[]{:S(2)}) %all-to-all-start) | async-done | bytes 1572896 | tf_op jit(solution)/shard_map/all_to_all | solution.py:220
  33.7 1.3 shard_map.60
  35.0 30.5 %all_to_all.35.got_ref = f32[32,2,128]{2,1,0:T(2,128)S(1)} all-to-all(f32[32,2,128]{2,1,0:T(2,128)S(1)} %get-tuple-element.16), channel_id=1, replica_groups=mesh['wide'=32,'narrow'=16] {'wide'}, dimensions={0} | all-to-all | bytes 65536 | tf_op jit(solution)/shard_map/all_to_all | solution.py:230
  65.6 0.3 shard_map.61
  65.8 17.8 %all_to_all.36.got_ref = f32[32,2,128]{2,1,0:T(2,128)S(1)} all-to-all(f32[32,2,128]{2,1,0:T(2,128)S(1)} %get-tuple-element.18), channel_id=1, replica_groups=mesh['wide'=32,'narrow'=16] {'wide'}, dimensions={0} | all-to-all | bytes 65536 | tf_op jit(solution)/shard_map/all_to_all | solution.py:236
  83.6 0.3 shard_map.62
  83.9 17.8 %all_to_all.37.got_ref = f32[32,2,128]{2,1,0:T(2,128)S(1)} all-to-all(f32[32,2,128]{2,1,0:T(2,128)S(1)} %get-tuple-element.20), channel_id=1, replica_groups=mesh['wide'=32,'narrow'=16] {'wide'}, dimensions={0} | all-to-all | bytes 65536 | tf_op jit(solution)/shard_map/all_to_all | solution.py:236
  101.7 1.8 shard_map.63
  103.5 0.1 convert.15
  103.6 0.1 fusion.18
  103.7 4.6 %collective-permute-start.2 = (f16[64,2176]{1,0:T(8,128)(2,1)S(1)}, f16[64,2176]{1,0:T(8,128)(2,1)S(1)}, u32[]{:S(2)}, u32[]{:S(2)}) collective-permute-start(f16[64,2176]{1,0:T(8,128)(2,1)S(1)} %get-tuple-element.31), channel_id=1, source_target_pairs={{0,16},{16,0},{32,48},{48,32},{64,80},{80,64},{96,112},{112,96},{1... | collective-permute-start | bytes 835592 | tf_op jit(solution)/shard_map/ppermute | solution.py:246
  108.3 2.8 %collective-permute-start.1 = (f16[64,2176]{1,0:T(8,128)(2,1)S(1)}, f16[64,2176]{1,0:T(8,128)(2,1)S(1)}, u32[]{:S(2)}, u32[]{:S(2)}) collective-permute-start(f16[64,2176]{1,0:T(8,128)(2,1)S(1)} %get-tuple-element.30), channel_id=1, source_target_pairs={{0,48},{16,32},{32,16},{48,0},{64,112},{80,96},{96,80},{112,64},{1... | collective-permute-start | bytes 835592 | tf_op jit(solution)/shard_map/ppermute | solution.py:246
  111.1 1.3 shard_map.64
  112.5 3.3 %collective-permute-start = (f16[64,2176]{1,0:T(8,128)(2,1)S(1)}, f16[64,2176]{1,0:T(8,128)(2,1)S(1)}, u32[]{:S(2)}, u32[]{:S(2)}) collective-permute-start(f16[64,2176]{1,0:T(8,128)(2,1)S(1)} %slice_convert_fusion), channel_id=1, source_target_pairs={{0,32},{16,48},{32,0},{48,16},{64,96},{80,112},{96,64},{112,80},{1... | collective-permute-start | bytes 835592 | tf_op jit(solution)/shard_map/ppermute | solution.py:246
  115.8 1.2 collective-permute-done.2
  117.0 3.9 %collective-permute-done.1 = f16[64,2176]{1,0:T(8,128)(2,1)S(1)} collective-permute-done((f16[64,2176]{1,0:T(8,128)(2,1)S(1)}, f16[64,2176]{1,0:T(8,128)(2,1)S(1)}, u32[]{:S(2)}, u32[]{:S(2)}) %collective-permute-start.1) | collective-permute-done | bytes 278560 | tf_op jit(solution)/shard_map/ppermute | solution.py:246
  120.9 1.1 collective-permute-done
  122.0 0.2 fusion.8
  122.1 23.0 %all_to_all.38 = f16[8,8,2176]{2,1,0:T(8,128)(2,1)S(1)} all-to-all(f16[8,8,2176]{2,1,0:T(8,128)(2,1)S(1)} %fusion.8), channel_id=1, replica_groups={{0,64,128,192,256,320,384,448},{16,80,144,208,272,336,400,464},{32,96,1..., dimensions={0} | all-to-all | bytes 557056 | tf_op jit(solution)/shard_map/all_to_all | solution.py:252
  145.2 0.2 fusion.13
  145.4 0.1 fusion.16
  145.5 20.4 %all_to_all.39 = f16[8,8,2048]{2,1,0:T(8,128)(2,1)S(1)} all-to-all(f16[8,8,2048]{2,1,0:T(8,128)(2,1)S(1)} %broadcast_in_dim.6), channel_id=1, replica_groups={{0,64,128,192,256,320,384,448},{16,80,144,208,272,336,400,464},{32,96,1..., dimensions={0} | all-to-all | bytes 524288 | tf_op jit(solution)/shard_map/all_to_all | solution.py:260
  166.0 0.1 broadcast_in_dim.16
  166.1 14.0 %all_to_all.40 = f16[4,64,2048]{2,1,0:T(8,128)(2,1)S(1)} all-to-all(f16[4,64,2048]{2,1,0:T(8,128)(2,1)S(1)} %broadcast_in_dim.16), channel_id=1, replica_groups={{0,16,32,48},{64,80,96,112},{128,144,160,176},{192,208,224,240},{256,27..., dimensions={0} | all-to-all | bytes 2097152 | tf_op jit(solution)/shard_map/all_to_all | solution.py:262
  180.2 0.2 bitcast_convert_fusion
  180.4 1.5 fusion.17
  (5 shorter events, 0.1 us)
Async XLA Ops:
  6.6 5.9 %copy-start = (bf16[256,1024]{1,0:T(8,128)(2,1)S(1)}, bf16[256,1024]{1,0:T(8,128)(2,1)}, u32[]{:S(2)}) copy-start(bf16[256,1024]{1,0:T(8,128)(2,1)} %param.7) | copy-start | bytes 1572868
  6.6 27.2 %all-to-all-start = ((bf16[16,48,1024]{2,1,0:T(8,128)(2,1)}), bf16[16,48,1024]{2,1,0:T(8,128)(2,1)S(1)}, u32[]{:S(2)}, u32[]{:S(2)}) async-start(bf16[16,48,1024]{2,1,0:T(8,128)(2,1)} %bitcast.14), calls=%async_computation | async-start | bytes 3145728 | tf_op jit(solution)/shard_map/all_to_all | solution.py:220
  103.7 13.3 %collective-permute-start.2 = (f16[64,2176]{1,0:T(8,128)(2,1)S(1)}, f16[64,2176]{1,0:T(8,128)(2,1)S(1)}, u32[]{:S(2)}, u32[]{:S(2)}) collective-permute-start(f16[64,2176]{1,0:T(8,128)(2,1)S(1)} %get-tuple-element.31), channel_id=1, source_target_pairs={{0,16},{16,0},{32,48},{48,32},{64,80},{80,64},{96,112},{112,96},{1... | collective-permute-start | bytes 835592 | tf_op jit(solution)/shard_map/ppermute | solution.py:246
  108.3 12.6 %collective-permute-start.1 = (f16[64,2176]{1,0:T(8,128)(2,1)S(1)}, f16[64,2176]{1,0:T(8,128)(2,1)S(1)}, u32[]{:S(2)}, u32[]{:S(2)}) collective-permute-start(f16[64,2176]{1,0:T(8,128)(2,1)S(1)} %get-tuple-element.30), channel_id=1, source_target_pairs={{0,48},{16,32},{32,16},{48,0},{64,112},{80,96},{96,80},{112,64},{1... | collective-permute-start | bytes 835592 | tf_op jit(solution)/shard_map/ppermute | solution.py:246
  112.5 9.4 %collective-permute-start = (f16[64,2176]{1,0:T(8,128)(2,1)S(1)}, f16[64,2176]{1,0:T(8,128)(2,1)S(1)}, u32[]{:S(2)}, u32[]{:S(2)}) collective-permute-start(f16[64,2176]{1,0:T(8,128)(2,1)S(1)} %slice_convert_fusion), channel_id=1, source_target_pairs={{0,32},{16,48},{32,0},{48,16},{64,96},{80,112},{96,64},{112,80},{1... | collective-permute-start | bytes 835592 | tf_op jit(solution)/shard_map/ppermute | solution.py:246

commit v6 on v5

--- a/solution.py
+++ b/solution.py
@@ -14,22 +14,18 @@
 F32 = jnp.float32
 BF16 = jnp.bfloat16
 VMEM_LIMIT = 24 * 1024 * 1024
-ALL_VMEM = 60 * 1024 * 1024
-
-
-def call(
-    kernel, out_shape, n_in, flops, moved, scalars=0, remote=0, scratch=(), room=VMEM_LIMIT
-):
-    smem = pl.BlockSpec(memory_space=pltpu.SMEM)
+
+
+def call(kernel, out_shape, n_in, flops, moved, remote=0, scratch=()):
     vmem = pl.BlockSpec(memory_space=pltpu.VMEM)
     hbm = pl.BlockSpec(memory_space=pltpu.HBM)
     return pl.pallas_call(
         kernel,
         out_shape=out_shape,
-        in_specs=[smem] * scalars + [vmem] * n_in + [hbm] * remote,
+        in_specs=[vmem] * n_in + [hbm] * remote,
         out_specs=jax.tree.map(lambda _: vmem, out_shape),
         scratch_shapes=scratch,
-        compiler_params=pltpu.CompilerParams(vmem_limit_bytes=room),
+        compiler_params=pltpu.CompilerParams(vmem_limit_bytes=VMEM_LIMIT),
         cost_estimate=pl.CostEstimate(flops=flops, bytes_accessed=moved, transcendentals=0),
     )
 
@@ -42,11 +38,20 @@
     return lax.dot_general(a, b, (((0,), (0,)), ((), ())), preferred_element_type=F32)
 
 
-def order_kernel(groups, dest_ref, embed_hbm, out_ref, embed_ref, arrival):
-    rows = embed_ref.shape[0]
-    load = pltpu.make_async_copy(embed_hbm, embed_ref, arrival)
-    load.start()
+def prepare_kernel(
+    groups, dest_hbm, var_hbm, mean_hbm, embed_hbm, out_ref, quad_ref, lin_ref, off_ref,
+    dest_ref, var_ref, mean_ref, embed_ref, arrivals,
+):
+    rows, width = embed_ref.shape
+    comp = mean_ref.shape[0]
     block = rows // groups
+    spans = [slice(start, start + ROW_STEP) for start in range(0, rows, ROW_STEP)]
+    pairs = [(dest_hbm, dest_ref), (var_hbm, var_ref), (mean_hbm, mean_ref)]
+    pairs += [(embed_hbm.at[span], embed_ref.at[span]) for span in spans]
+    loads = [pltpu.make_async_copy(*pair, arrivals.at[i]) for i, pair in enumerate(pairs)]
+    for load in loads:
+        load.start()
+    loads[0].wait()
     before = lax.broadcasted_iota(jnp.int32, (LANES, LANES), 0)
     after = lax.broadcasted_iota(jnp.int32, (LANES, LANES), 1)
     earlier = jnp.where(before < after, 1.0, 0.0).astype(BF16)
@@ -55,17 +60,33 @@
     count = jnp.zeros((groups, 1), F32)
     places = []
     for start in range(0, rows, LANES):
-        hot = jnp.where(group == dest_ref[:, start : start + LANES], 1.0, 0.0)
+        hot = jnp.where(group == dest_ref[start : start + LANES][None, :], 1.0, 0.0)
         rank = jnp.dot(hot.astype(BF16), earlier, preferred_element_type=F32) + count
         places.append(jnp.sum(hot * (rank + base), axis=0, keepdims=True))
         count = count + jnp.sum(hot, axis=1, keepdims=True)
     place = jnp.concatenate(places, axis=1).astype(jnp.int32)
-    load.wait()
-    for start in range(0, rows, ROW_STEP):
-        slot = lax.broadcasted_iota(jnp.int32, (ROW_STEP, rows), 0) + start
+    loads[1].wait()
+    loads[2].wait()
+    offsets = []
+    for start in range(0, comp, LANES):
+        span = slice(start, start + LANES)
+        var = var_ref[span, :].astype(F32)
+        mean = mean_ref[span, :].astype(F32)
+        prec = 1.0 / var
+        scaled = mean * prec
+        quad_ref[span, :] = (-0.5 * prec).astype(BF16)
+        lin_ref[span, :] = scaled.astype(BF16)
+        term = jnp.log(var) + mean * scaled
+        part = sum(term[:, i : i + LANES] for i in range(0, width, LANES))
+        offsets.append(-0.5 * jnp.sum(jnp.transpose(part), axis=0, keepdims=True))
+    off_ref[...] = jnp.concatenate(offsets, axis=1)
+    for load in loads[3:]:
+        load.wait()
+    for span in spans:
+        slot = lax.broadcasted_iota(jnp.int32, (ROW_STEP, rows), 0) + span.start
         pick = jnp.where(slot == place, 1.0, 0.0).astype(BF16)
         got = jnp.dot(pick, embed_ref[...], preferred_element_type=F32)
-        out_ref[start : start + ROW_STEP, :] = got.astype(BF16)
+        out_ref[span, :] = got.astype(BF16)
 
 
 def put_mass(mass, sent_ref):
@@ -145,48 +166,18 @@
     out_ref[:, 2 * width :] = total_parts(total[:part] + total[part:])
 
 
-def split_parts(resp):
-    high = resp.astype(BF16)
-    low = (resp - high.astype(F32)).astype(BF16)
-    return jnp.concatenate([high, low], axis=1)
-
-
-def crossed_kernel(
-    target, place_ref, got_ref, resp_ref, x_ref, high_ref, low_ref,
-    kept_ref, out_ref, lent_ref,
+def moment_kernel(
+    target, got_ref, resp_ref, x_ref, high_ref, low_ref, out_ref, both_ref
 ):
     rows, comp = resp_ref.shape
-    half = comp // 2
-    y, z = place_ref[0] % 2, place_ref[0] // 2
     pull = target / get_mass(got_ref)
-    left = lax.broadcasted_iota(jnp.int32, (ROW_STEP, half), 1) < half // 2
     for start in range(0, rows, ROW_STEP):
         span = slice(start, start + ROW_STEP)
         resp = balance_step(resp_ref[span, :], pull)
-        same = jnp.where(z == 0, resp[:, :half], resp[:, half:])
-        other = jnp.where(z == 0, resp[:, half:], resp[:, :half])
-        same_turned = pltpu.roll(same, half // 2, 1)
-        other_turned = pltpu.roll(other, half // 2, 1)
-        lower = jnp.where(left, same, other_turned)
-        upper = jnp.where(left, same_turned, other)
-        kept_ref[span, :] = split_parts(jnp.where(y == 0, lower, upper))
-        lent_ref[span, :] = split_parts(jnp.where(y == 0, upper, lower))
-    put_moments(lent_ref[...], x_ref, high_ref, low_ref, out_ref)
-
-
-def kept_kernel(kept_ref, x_ref, high_ref, low_ref, out_ref):
-    put_moments(kept_ref[...], x_ref, high_ref, low_ref, out_ref)
-
-
-def weights(mean_block, var_block):
-    prec = 1.0 / var_block.astype(F32)
-    mean_wide = mean_block.astype(F32)
-    quad = (-0.5 * prec).astype(BF16)
-    linear = (mean_wide * prec).astype(BF16)
-    offset = -0.5 * jnp.sum(
-        jnp.log(var_block.astype(F32)) + mean_wide * mean_wide * prec, axis=1
-    )
-    return quad, linear, offset[None, :]
+        high = resp.astype(BF16)
+        both_ref[span, :comp] = high
+        both_ref[span, comp:] = (resp - high.astype(F32)).astype(BF16)
+    put_moments(both_ref[...], x_ref, high_ref, low_ref, out_ref)
 
 
 def on_device(embed, dest, means, variances):
@@ -195,12 +186,10 @@
     members = lax.axis_size("wide")
     block = rows_dev // groups
     comp = means.shape[0]
-    half = comp // 2
     quarter = comp // 4
     deep = members // 4
     lines = [[4 * z + i for z in range(deep)] for i in range(4)]
     blocks = [[4 * z + i for i in range(4)] for z in range(deep)]
-    place = (lax.axis_index("wide") % 4).astype(jnp.int32).reshape(1)
     scale = width ** (-0.5)
     target = float(rows_dev * members / comp)
     big = rows_dev * width
@@ -212,17 +201,23 @@
     resp_shape = jax.ShapeDtypeStruct((rows_dev, comp), F32)
     sent_shape = jax.ShapeDtypeStruct((members, comp // LANES, LANES), F32)
 
-    ordered = call(
-        functools.partial(order_kernel, groups),
-        jax.ShapeDtypeStruct(embed.shape, BF16), 1, 2 * rows_dev * big, 4 * big, remote=1,
-        scratch=[pltpu.VMEM(embed.shape, BF16), pltpu.SemaphoreType.DMA], room=ALL_VMEM,
-    )(dest.reshape(1, rows_dev), embed)
+    plain = jax.ShapeDtypeStruct((rows_dev, width), BF16)
+    weight = jax.ShapeDtypeStruct((comp, width), BF16)
+    ordered, quad, linear, offset = call(
+        functools.partial(prepare_kernel, groups),
+        (plain, weight, weight, jax.ShapeDtypeStruct((1, comp), F32)),
+        0, 2 * rows_dev * big, 4 * big, remote=4,
+        scratch=[
+            pltpu.VMEM(dest.shape, jnp.int32),
+            pltpu.VMEM(variances.shape, BF16),
+            pltpu.VMEM(means.shape, BF16),
+            pltpu.VMEM(embed.shape, BF16),
+            pltpu.SemaphoreType.DMA((3 + rows_dev // ROW_STEP,)),
+        ],
+    )(*(pltpu.with_memory_space_constraint(a, pltpu.HBM) for a in (dest, variances, means, embed)))
     mine = lax.all_to_all(
         ordered.reshape(groups, block, width), "narrow", split_axis=0, concat_axis=0, tiled=True
     ).reshape(rows_dev, width)
-    mine, place = lax.optimization_barrier((mine, place))
-    quad, linear, offset = weights(means, variances)
-    plain = jax.ShapeDtypeStruct((rows_dev, width), BF16)
     resp, high, low, sent = call(
         functools.partial(score_kernel, scale), (resp_shape, plain, plain, sent_shape),
         4, 4 * big * comp, 6 * big + 4 * area,
@@ -234,21 +229,14 @@
             2, 4 * area, 8 * area,
         )(got, resp)
         got = everyone(sent)
-    sums = jax.ShapeDtypeStruct((half, 2 * width + LANES), F32)
-    slab = jax.ShapeDtypeStruct((rows_dev, comp), BF16)
-    kept, lent = call(
-        functools.partial(crossed_kernel, target), (slab, sums), 5, 5 * big * comp,
-        6 * big + 8 * area, scalars=1, scratch=[pltpu.VMEM((rows_dev, comp), BF16)],
-    )(place, got, resp, mine, high, low)
-
-    def to_partner(values, flip):
-        swap = [(i, i ^ flip) for i in range(members)]
-        return lax.ppermute(values.astype(jnp.float16), "wide", swap).astype(F32)
-
-    there = to_partner(lent[quarter:], 3), to_partner(lent[:quarter], 1)
-    here = call(kept_kernel, sums, 4, 5 * big * comp, 6 * big + 2 * area)(kept, mine, high, low)
-    near = to_partner(here[quarter:], 2)
-    sent = (SAFE * (here[:quarter] + near + there[0] + there[1])).astype(jnp.float16)
+    sums = call(
+        functools.partial(moment_kernel, target),
+        jax.ShapeDtypeStruct((comp, 2 * width + LANES), F32), 5, 10 * big * comp,
+        6 * big + 8 * area, scratch=[pltpu.VMEM((rows_dev, 2 * comp), BF16)],
+    )(got, resp, mine, high, low)
+    sent = sums.astype(jnp.float16).reshape(4, quarter, sums.shape[1])
+    got = everyone(sent, axis_index_groups=blocks)
+    sent = (SAFE * jnp.sum(got.astype(F32), axis=0)).astype(jnp.float16)
     got = everyone(sent.reshape(deep, quarter // deep, sent.shape[1]), axis_index_groups=lines)
     got = jnp.sum(got.astype(F32), axis=0)
     first, second = got[:, :width], got[:, width : 2 * width]

time: 184 us -> 176 us (0.957)
  blocking collectives: 124 us -> 163 us
  waiting for transfers between devices: 25.8 us -> 0 us
  starting transfers between devices: 16.6 us -> 0 us
  Pallas kernels: 9.6 us -> 7.55 us
    all_to_all x0 -> x2, blocking collectives: none -> 41.9 us  [the longest x1 26.1 us: on_device(): lax.all_to_all(ordered.reshape(groups, block, width), 'narrow', split_axi...]
    all_to_all x1 -> x0, waiting for transfers between devices: 19.7 us -> none  [on_device(): lax.all_to_all(ordered.reshape(groups, block, width), 'narrow', split_axi...]
    ppermute x3 -> x0, starting transfers between devices: 10.7 us -> none  [to_partner(): return lax.ppermute(values.astype(jnp.float16), 'wide', swap).astype(F32)]
    ppermute x3 -> x0, waiting for transfers between devices: 6.11 us -> none  [to_partner(): return lax.ppermute(values.astype(jnp.float16), 'wide', swap).astype(F32)]
    all_to_all x1 -> x0, starting transfers between devices: 5.92 us -> none  [on_device(): lax.all_to_all(ordered.reshape(groups, block, width), 'narrow', split_axi...]
    all_to_all x1, blocking collectives: 23 us -> 20.1 us  [on_device(): everyone(sent.reshape(deep, quarter // deep, sent.shape[1]), axis_index_g...]
    pallas_call x3 -> x2, Pallas kernels: 7.79 us -> 5.74 us  [the longest x1 3.13 us: on_device(): call(functools.partial(prepare_kernel, groups), (plain, weight, weight, j...]
  transfers between devices with their start and end apart: 4 -> 0, of which waited for: 4 -> 0; matrix products, arithmetic and copies ran while one was open for 1% -> 0% of each run, Pallas kernels for 1% -> 0%
where the time goes in v6:
time: 176 us; the launch traced here: 174 us
  blocking collectives  163 us (93%)
  Pallas kernels  7.55 us (4%)
    all_to_all x3, blocking collectives, on_device(): got = everyone(sent)  66.2 us
    all_to_all x1, blocking collectives, on_device(): lax.all_to_all(ordered.reshape(groups, block, width), 'narrow', split_axi...  26.1 us
    all_to_all x1, blocking collectives, on_device(): everyone(jnp.broadcast_to(done[None], (deep,) + done.shape), axis_index_g...  21.4 us
    all_to_all x1, blocking collectives, on_device(): everyone(sent.reshape(deep, quarter // deep, sent.shape[1]), axis_index_g...  20.1 us
    all_to_all x1, blocking collectives, on_device(): got = everyone(sent, axis_index_groups=blocks)  15.7 us
    all_to_all x1, blocking collectives, on_device(): everyone(jnp.broadcast_to(here, (4,) + here.shape[1:]), axis_index_groups...  13.8 us

profile of v6, /device:TPU:24, one launch (start us, length us, event | category | flops | bytes accessed | tf_op | source)
XLA Modules:
  0.0 174.1 jit_solution(1612317483737822485)
XLA Ops:
  0.6 3.1 %shard_map.59 = (bf16[768,1024]{1,0:T(8,128)(2,1)S(1)}, bf16[256,1024]{1,0:T(8,128)(2,1)S(1)}, bf16[256,1024]{1,0:T(8,128)(2,1)S(1)}, f32[1,256]{1,0:T(1,128)S(1)}) custom-call(s32[768]{0:T(1024)} %dest_hbm.1, bf16[256,1024]{1,0:T(8,128)(2,1)} %var_hbm.1, bf16[256,1024]{1,0:T(8,128)(2,1)} %mean_hbm.1, bf16[768,1024]{1,0:T(8,128)(2,1)} %embed_hbm.1), custom_call_target="tpu_custom_call" | custom-call | flops 1207959552 | bytes 3145728 | tf_op jit(solution)/shard_map/pallas_call | solution.py:206
  3.8 26.1 %all_to_all.40 = bf16[16,48,1024]{2,1,0:T(8,128)(2,1)S(1)} all-to-all(bf16[16,48,1024]{2,1,0:T(8,128)(2,1)S(1)} %bitcast.11), channel_id=1, replica_groups=mesh['wide'=32,'narrow'=16] {'narrow'}, dimensions={0} | all-to-all | bytes 3145728 | tf_op jit(solution)/shard_map/all_to_all | solution.py:218
  29.9 1.3 shard_map.60
  31.2 30.5 %all_to_all.41.got_ref = f32[32,2,128]{2,1,0:T(2,128)S(1)} all-to-all(f32[32,2,128]{2,1,0:T(2,128)S(1)} %get-tuple-element.18), channel_id=1, replica_groups=mesh['wide'=32,'narrow'=16] {'wide'}, dimensions={0} | all-to-all | bytes 65536 | tf_op jit(solution)/shard_map/all_to_all | solution.py:225
  61.7 0.3 shard_map.61
  62.0 17.8 %all_to_all.42.got_ref = f32[32,2,128]{2,1,0:T(2,128)S(1)} all-to-all(f32[32,2,128]{2,1,0:T(2,128)S(1)} %get-tuple-element.20), channel_id=1, replica_groups=mesh['wide'=32,'narrow'=16] {'wide'}, dimensions={0} | all-to-all | bytes 65536 | tf_op jit(solution)/shard_map/all_to_all | solution.py:231
  79.8 0.3 shard_map.62
  80.1 17.8 %all_to_all.43.got_ref = f32[32,2,128]{2,1,0:T(2,128)S(1)} all-to-all(f32[32,2,128]{2,1,0:T(2,128)S(1)} %get-tuple-element.22), channel_id=1, replica_groups=mesh['wide'=32,'narrow'=16] {'wide'}, dimensions={0} | all-to-all | bytes 65536 | tf_op jit(solution)/shard_map/all_to_all | solution.py:231
  97.9 2.6 %shard_map.63 = f32[256,2176]{1,0:T(8,128)S(1)} custom-call(f32[32,2,128]{2,1,0:T(2,128)S(1)} %all_to_all.43.got_ref, f32[768,256]{1,0:T(8,128)S(1)} %get-tuple-element.23.resp_ref, bf16[768,1024]{1,0:T(8,128)(2,1)S(1)} %bitcast.10, bf16[768,1024]{1,0:T(8,128)(2,1)S(1)} %get-tuple-element.24.high_ref, bf16[768,1024]{1,0:T(8,128)(2,1)S(1)} %get-tuple-element.25.low_ref), custom_call_target="tpu_custom_call" | custom-call | flops 2013265920 | bytes 6291456 | tf_op jit(solution)/shard_map/pallas_call | solution.py:232
  100.5 0.1 convert_element_type.27
  100.6 15.7 %all_to_all.44 = f16[4,64,2176]{2,1,0:T(8,128)(2,1)S(1)} all-to-all(f16[4,64,2176]{2,1,0:T(8,128)(2,1)S(1)} %bitcast.12), channel_id=1, replica_groups={{0,16,32,48},{64,80,96,112},{128,144,160,176},{192,208,224,240},{256,27..., dimensions={0} | all-to-all | bytes 2228224 | tf_op jit(solution)/shard_map/all_to_all | solution.py:238
  116.4 0.1 convert_reduce_fusion
  116.5 0.1 fusion
  116.6 20.1 %all_to_all.45 = f16[8,8,2176]{2,1,0:T(8,128)(2,1)S(1)} all-to-all(f16[8,8,2176]{2,1,0:T(8,128)(2,1)S(1)} %fusion), channel_id=1, replica_groups={{0,64,128,192,256,320,384,448},{16,80,144,208,272,336,400,464},{32,96,1..., dimensions={0} | all-to-all | bytes 557056 | tf_op jit(solution)/shard_map/all_to_all | solution.py:240
  136.7 0.2 fusion.5
  136.9 0.1 fusion.8
  137.1 21.4 %all_to_all.46 = f16[8,8,2048]{2,1,0:T(8,128)(2,1)S(1)} all-to-all(f16[8,8,2048]{2,1,0:T(8,128)(2,1)S(1)} %broadcast_in_dim.6), channel_id=1, replica_groups={{0,64,128,192,256,320,384,448},{16,80,144,208,272,336,400,464},{32,96,1..., dimensions={0} | all-to-all | bytes 524288 | tf_op jit(solution)/shard_map/all_to_all | solution.py:248
  158.5 0.1 broadcast_in_dim.15
  158.6 13.8 %all_to_all.47 = f16[4,64,2048]{2,1,0:T(8,128)(2,1)S(1)} all-to-all(f16[4,64,2048]{2,1,0:T(8,128)(2,1)S(1)} %broadcast_in_dim.15), channel_id=1, replica_groups={{0,16,32,48},{64,80,96,112},{128,144,160,176},{192,208,224,240},{256,27..., dimensions={0} | all-to-all | bytes 2097152 | tf_op jit(solution)/shard_map/all_to_all | solution.py:250
  172.4 0.2 bitcast_convert_fusion
  172.6 1.5 fusion.9
  (3 shorter events, 0.1 us)

commit v7 on v6

--- a/solution.py
+++ b/solution.py
@@ -30,6 +30,10 @@
     )
 
 
+def in_hbm(array):
+    return pltpu.with_memory_space_constraint(array, pltpu.HBM)
+
+
 def dot_nt(a, b):
     return lax.dot_general(a, b, (((1,), (1,)), ((), ())), preferred_element_type=F32)
 
@@ -38,15 +42,11 @@
     return lax.dot_general(a, b, (((0,), (0,)), ((), ())), preferred_element_type=F32)
 
 
-def prepare_kernel(
-    groups, dest_hbm, var_hbm, mean_hbm, embed_hbm, out_ref, quad_ref, lin_ref, off_ref,
-    dest_ref, var_ref, mean_ref, embed_ref, arrivals,
-):
-    rows, width = embed_ref.shape
-    comp = mean_ref.shape[0]
+def order_kernel(groups, dest_hbm, embed_hbm, out_ref, dest_ref, embed_ref, arrivals):
+    rows = embed_ref.shape[0]
     block = rows // groups
     spans = [slice(start, start + ROW_STEP) for start in range(0, rows, ROW_STEP)]
-    pairs = [(dest_hbm, dest_ref), (var_hbm, var_ref), (mean_hbm, mean_ref)]
+    pairs = [(dest_hbm, dest_ref)]
     pairs += [(embed_hbm.at[span], embed_ref.at[span]) for span in spans]
     loads = [pltpu.make_async_copy(*pair, arrivals.at[i]) for i, pair in enumerate(pairs)]
     for load in loads:
@@ -65,8 +65,25 @@
         places.append(jnp.sum(hot * (rank + base), axis=0, keepdims=True))
         count = count + jnp.sum(hot, axis=1, keepdims=True)
     place = jnp.concatenate(places, axis=1).astype(jnp.int32)
-    loads[1].wait()
-    loads[2].wait()
+    for load in loads[1:]:
+        load.wait()
+    for span in spans:
+        slot = lax.broadcasted_iota(jnp.int32, (ROW_STEP, rows), 0) + span.start
+        pick = jnp.where(slot == place, 1.0, 0.0).astype(BF16)
+        got = jnp.dot(pick, embed_ref[...], preferred_element_type=F32)
+        out_ref[span, :] = got.astype(BF16)
+
+
+def weight_kernel(
+    var_hbm, mean_hbm, quad_ref, lin_ref, off_ref, var_ref, mean_ref, arrivals
+):
+    comp, width = mean_ref.shape
+    pairs = [(var_hbm, var_ref), (mean_hbm, mean_ref)]
+    loads = [pltpu.make_async_copy(*pair, arrivals.at[i]) for i, pair in enumerate(pairs)]
+    for load in loads:
+        load.start()
+    for load in loads:
+        load.wait()
     offsets = []
     for start in range(0, comp, LANES):
         span = slice(start, start + LANES)
@@ -80,13 +97,6 @@
         part = sum(term[:, i : i + LANES] for i in range(0, width, LANES))
         offsets.append(-0.5 * jnp.sum(jnp.transpose(part), axis=0, keepdims=True))
     off_ref[...] = jnp.concatenate(offsets, axis=1)
-    for load in loads[3:]:
-        load.wait()
-    for span in spans:
-        slot = lax.broadcasted_iota(jnp.int32, (ROW_STEP, rows), 0) + span.start
-        pick = jnp.where(slot == place, 1.0, 0.0).astype(BF16)
-        got = jnp.dot(pick, embed_ref[...], preferred_element_type=F32)
-        out_ref[span, :] = got.astype(BF16)
 
 
 def put_mass(mass, sent_ref):
@@ -203,18 +213,23 @@
 
     plain = jax.ShapeDtypeStruct((rows_dev, width), BF16)
     weight = jax.ShapeDtypeStruct((comp, width), BF16)
-    ordered, quad, linear, offset = call(
-        functools.partial(prepare_kernel, groups),
-        (plain, weight, weight, jax.ShapeDtypeStruct((1, comp), F32)),
-        0, 2 * rows_dev * big, 4 * big, remote=4,
+    ordered = call(
+        functools.partial(order_kernel, groups), plain, 0, 2 * rows_dev * big, 4 * big, remote=2,
         scratch=[
             pltpu.VMEM(dest.shape, jnp.int32),
+            pltpu.VMEM(embed.shape, BF16),
+            pltpu.SemaphoreType.DMA((1 + rows_dev // ROW_STEP,)),
+        ],
+    )(*(in_hbm(a) for a in (dest, embed)))
+    quad, linear, offset = call(
+        weight_kernel, (weight, weight, jax.ShapeDtypeStruct((1, comp), F32)),
+        0, 8 * comp * width, 8 * comp * width, remote=2,
+        scratch=[
             pltpu.VMEM(variances.shape, BF16),
             pltpu.VMEM(means.shape, BF16),
-            pltpu.VMEM(embed.shape, BF16),
-            pltpu.SemaphoreType.DMA((3 + rows_dev // ROW_STEP,)),
+            pltpu.SemaphoreType.DMA((2,)),
         ],
-    )(*(pltpu.with_memory_space_constraint(a, pltpu.HBM) for a in (dest, variances, means, embed)))
+    )(*(in_hbm(a) for a in (variances, means)))
     mine = lax.all_to_all(
         ordered.reshape(groups, block, width), "narrow", split_axis=0, concat_axis=0, tiled=True
     ).reshape(rows_dev, width)
@@ -248,8 +263,8 @@
     got = everyone(jnp.broadcast_to(done[None], (deep,) + done.shape), axis_index_groups=lines)
     here = got.reshape(1, quarter, 2 * width)
     got = everyone(jnp.broadcast_to(here, (4,) + here.shape[1:]), axis_index_groups=blocks)
-    out = got.reshape(comp, 2 * width).astype(F32)
-    return (out[:, :width], out[:, width:])
+    out = lax.optimization_barrier(got.reshape(comp, 2 * width))
+    return (out[:, :width].astype(F32), out[:, width:].astype(F32))
 
 
 def solution(mesh):

time: 176 us -> 177 us (level)
  blocking collectives: 163 us -> 137 us
  waiting for transfers between devices: 0 us -> 19.6 us
  starting transfers between devices: 0 us -> 5.79 us
  Pallas kernels: 7.55 us -> 10 us
    all_to_all x1 -> x0, blocking collectives: 26.1 us -> none  [on_device(): lax.all_to_all(ordered.reshape(groups, block, width), 'narrow', split_axi...]
    all_to_all x0 -> x1, waiting for transfers between devices: none -> 19.6 us  [on_device(): lax.all_to_all(ordered.reshape(groups, block, width), 'narrow', split_axi...]
    all_to_all x0 -> x1, starting transfers between devices: none -> 5.79 us  [on_device(): lax.all_to_all(ordered.reshape(groups, block, width), 'narrow', split_axi...]
    pallas_call x1 -> x2, Pallas kernels: 3.13 us -> 5.62 us  [the longest x1 3.95 us: on_device(): call(functools.partial(order_kernel, groups), plain, 0, 2 * rows_dev * bi...]
  transfers between devices with their start and end apart: 0 -> 1, of which waited for: 0 -> 1; matrix products, arithmetic and copies ran while one was open for 0% -> 0% of each run, Pallas kernels for 0% -> 1%
where the time goes in v7:
time: 177 us; the launch traced here: 176 us
  blocking collectives  137 us (77%)
  waiting for transfers between devices  19.6 us (11%)
  Pallas kernels  10 us (6%)
  starting transfers between devices  5.79 us (3%)
  other arithmetic  2.16 us (1%)
    all_to_all x3, blocking collectives, on_device(): got = everyone(sent)  66.2 us
    all_to_all x1, blocking collectives, on_device(): everyone(jnp.broadcast_to(done[None], (deep,) + done.shape), axis_index_g...  21.4 us
    all_to_all x1, blocking collectives, on_device(): everyone(sent.reshape(deep, quarter // deep, sent.shape[1]), axis_index_g...  20.1 us
    all_to_all x1, waiting for transfers between devices, on_device(): lax.all_to_all(ordered.reshape(groups, block, width), 'narrow', split_axi...  19.6 us
    all_to_all x1, blocking collectives, on_device(): got = everyone(sent, axis_index_groups=blocks)  15.7 us
    all_to_all x1, blocking collectives, on_device(): everyone(jnp.broadcast_to(here, (4,) + here.shape[1:]), axis_index_groups...  13.8 us
    all_to_all x1, starting transfers between devices, on_device(): lax.all_to_all(ordered.reshape(groups, block, width), 'narrow', split_axi...  5.79 us
    pallas_call x1, Pallas kernels, on_device(): call(functools.partial(order_kernel, groups), plain, 0, 2 * rows_dev * bi...  3.95 us
  transfers between devices with their start and end apart: 1, of which 1 were waited for; matrix products, arithmetic and copies ran while one was open for 0% of the time, Pallas kernels for 1%

profile of v7, /device:TPU:24, one launch (start us, length us, event | category | flops | bytes accessed | tf_op | source)
XLA Modules:
  0.0 175.6 jit_solution(4499231762114581323)
XLA Ops:
  0.6 4.0 %shard_map.59 = bf16[768,1024]{1,0:T(8,128)(2,1)} custom-call(s32[768]{0:T(1024)} %dest_hbm.1, bf16[768,1024]{1,0:T(8,128)(2,1)} %embed_hbm.1), custom_call_target="tpu_custom_call" | custom-call | flops 1207959552 | bytes 3145728 | tf_op jit(solution)/shard_map/pallas_call | solution.py:216
  4.6 5.8 %all-to-all-start = ((bf16[16,48,1024]{2,1,0:T(8,128)(2,1)}), bf16[16,48,1024]{2,1,0:T(8,128)(2,1)S(1)}, u32[]{:S(2)}, u32[]{:S(2)}) async-start(bf16[16,48,1024]{2,1,0:T(8,128)(2,1)} %bitcast), calls=%async_computation | async-start | bytes 3145728 | tf_op jit(solution)/shard_map/all_to_all | solution.py:233
  10.4 1.7 shard_map.60
  12.1 19.6 %all-to-all-done = bf16[16,48,1024]{2,1,0:T(8,128)(2,1)S(1)} async-done(((bf16[16,48,1024]{2,1,0:T(8,128)(2,1)}), bf16[16,48,1024]{2,1,0:T(8,128)(2,1)S(1)}, u32[]{:S(2)}, u32[]{:S(2)}) %all-to-all-start) | async-done | bytes 1572896 | tf_op jit(solution)/shard_map/all_to_all | solution.py:233
  31.6 1.3 shard_map.61
  32.9 30.5 %all_to_all.40.got_ref = f32[32,2,128]{2,1,0:T(2,128)S(1)} all-to-all(f32[32,2,128]{2,1,0:T(2,128)S(1)} %get-tuple-element.16), channel_id=1, replica_groups=mesh['wide'=32,'narrow'=16] {'wide'}, dimensions={0} | all-to-all | bytes 65536 | tf_op jit(solution)/shard_map/all_to_all | solution.py:240
  63.4 0.3 shard_map.62
  63.7 17.8 %all_to_all.41.got_ref = f32[32,2,128]{2,1,0:T(2,128)S(1)} all-to-all(f32[32,2,128]{2,1,0:T(2,128)S(1)} %get-tuple-element.18), channel_id=1, replica_groups=mesh['wide'=32,'narrow'=16] {'wide'}, dimensions={0} | all-to-all | bytes 65536 | tf_op jit(solution)/shard_map/all_to_all | solution.py:246
  81.5 0.3 shard_map.63
  81.8 17.8 %all_to_all.42.got_ref = f32[32,2,128]{2,1,0:T(2,128)S(1)} all-to-all(f32[32,2,128]{2,1,0:T(2,128)S(1)} %get-tuple-element.20), channel_id=1, replica_groups=mesh['wide'=32,'narrow'=16] {'wide'}, dimensions={0} | all-to-all | bytes 65536 | tf_op jit(solution)/shard_map/all_to_all | solution.py:246
  99.6 2.6 %shard_map.64 = f32[256,2176]{1,0:T(8,128)S(1)} custom-call(f32[32,2,128]{2,1,0:T(2,128)S(1)} %all_to_all.42.got_ref, f32[768,256]{1,0:T(8,128)S(1)} %get-tuple-element.21.resp_ref, bf16[768,1024]{1,0:T(8,128)(2,1)S(1)} %bitcast.8, bf16[768,1024]{1,0:T(8,128)(2,1)S(1)} %get-tuple-element.22.high_ref, bf16[768,1024]{1,0:T(8,128)(2,1)S(1)} %get-tuple-element.23.low_ref), custom_call_target="tpu_custom_call" | custom-call | flops 2013265920 | bytes 6291456 | tf_op jit(solution)/shard_map/pallas_call | solution.py:247
  102.2 0.1 convert_element_type.27
  102.4 15.7 %all_to_all.43 = f16[4,64,2176]{2,1,0:T(8,128)(2,1)S(1)} all-to-all(f16[4,64,2176]{2,1,0:T(8,128)(2,1)S(1)} %bitcast.9), channel_id=1, replica_groups={{0,16,32,48},{64,80,96,112},{128,144,160,176},{192,208,224,240},{256,27..., dimensions={0} | all-to-all | bytes 2228224 | tf_op jit(solution)/shard_map/all_to_all | solution.py:253
  118.1 0.1 convert_reduce_fusion
  118.2 0.1 fusion
  118.3 20.1 %all_to_all.44 = f16[8,8,2176]{2,1,0:T(8,128)(2,1)S(1)} all-to-all(f16[8,8,2176]{2,1,0:T(8,128)(2,1)S(1)} %fusion), channel_id=1, replica_groups={{0,64,128,192,256,320,384,448},{16,80,144,208,272,336,400,464},{32,96,1..., dimensions={0} | all-to-all | bytes 557056 | tf_op jit(solution)/shard_map/all_to_all | solution.py:255
  138.5 0.2 fusion.5
  138.6 0.1 fusion.8
  138.8 21.4 %all_to_all.45 = f16[8,8,2048]{2,1,0:T(8,128)(2,1)S(1)} all-to-all(f16[8,8,2048]{2,1,0:T(8,128)(2,1)S(1)} %broadcast_in_dim.6), channel_id=1, replica_groups={{0,64,128,192,256,320,384,448},{16,80,144,208,272,336,400,464},{32,96,1..., dimensions={0} | all-to-all | bytes 524288 | tf_op jit(solution)/shard_map/all_to_all | solution.py:263
  160.2 0.1 broadcast_in_dim.15
  160.3 13.8 %all_to_all.46 = f16[4,64,2048]{2,1,0:T(8,128)(2,1)S(1)} all-to-all(f16[4,64,2048]{2,1,0:T(8,128)(2,1)S(1)} %broadcast_in_dim.15), channel_id=1, replica_groups={{0,16,32,48},{64,80,96,112},{128,144,160,176},{192,208,224,240},{256,27..., dimensions={0} | all-to-all | bytes 2097152 | tf_op jit(solution)/shard_map/all_to_all | solution.py:265
  174.1 1.5 slice_convert_fusion
  (3 shorter events, 0.1 us)
Async XLA Ops:
  4.6 27.0 %all-to-all-start = ((bf16[16,48,1024]{2,1,0:T(8,128)(2,1)}), bf16[16,48,1024]{2,1,0:T(8,128)(2,1)S(1)}, u32[]{:S(2)}, u32[]{:S(2)}) async-start(bf16[16,48,1024]{2,1,0:T(8,128)(2,1)} %bitcast), calls=%async_computation | async-start | bytes 3145728 | tf_op jit(solution)/shard_map/all_to_all | solution.py:233

commit v8 on v7

--- a/solution.py
+++ b/solution.py
@@ -16,14 +16,16 @@
 VMEM_LIMIT = 24 * 1024 * 1024
 
 
-def call(kernel, out_shape, n_in, flops, moved, remote=0, scratch=()):
+def call(
+    kernel, out_shape, n_in, flops, moved, remote=0, scratch=(), out_space=pltpu.VMEM
+):
     vmem = pl.BlockSpec(memory_space=pltpu.VMEM)
     hbm = pl.BlockSpec(memory_space=pltpu.HBM)
     return pl.pallas_call(
         kernel,
         out_shape=out_shape,
         in_specs=[vmem] * n_in + [hbm] * remote,
-        out_specs=jax.tree.map(lambda _: vmem, out_shape),
+        out_specs=jax.tree.map(lambda _: pl.BlockSpec(memory_space=out_space), out_shape),
         scratch_shapes=scratch,
         compiler_params=pltpu.CompilerParams(vmem_limit_bytes=VMEM_LIMIT),
         cost_estimate=pl.CostEstimate(flops=flops, bytes_accessed=moved, transcendentals=0),
@@ -42,7 +44,9 @@
     return lax.dot_general(a, b, (((0,), (0,)), ((), ())), preferred_element_type=F32)
 
 
-def order_kernel(groups, dest_hbm, embed_hbm, out_ref, dest_ref, embed_ref, arrivals):
+def order_kernel(
+    groups, dest_hbm, embed_hbm, out_hbm, dest_ref, embed_ref, out_ref, arrivals, departures
+):
     rows = embed_ref.shape[0]
     block = rows // groups
     spans = [slice(start, start + ROW_STEP) for start in range(0, rows, ROW_STEP)]
@@ -67,11 +71,20 @@
     place = jnp.concatenate(places, axis=1).astype(jnp.int32)
     for load in loads[1:]:
         load.wait()
+    stores = []
     for span in spans:
         slot = lax.broadcasted_iota(jnp.int32, (ROW_STEP, rows), 0) + span.start
         pick = jnp.where(slot == place, 1.0, 0.0).astype(BF16)
         got = jnp.dot(pick, embed_ref[...], preferred_element_type=F32)
         out_ref[span, :] = got.astype(BF16)
+        stores.append(
+            pltpu.make_async_copy(
+                out_ref.at[span], out_hbm.at[span], departures.at[len(stores)]
+            )
+        )
+        stores[-1].start()
+    for store in stores:
+        store.wait()
 
 
 def weight_kernel(
@@ -218,8 +231,11 @@
         scratch=[
             pltpu.VMEM(dest.shape, jnp.int32),
             pltpu.VMEM(embed.shape, BF16),
+            pltpu.VMEM(embed.shape, BF16),
             pltpu.SemaphoreType.DMA((1 + rows_dev // ROW_STEP,)),
+            pltpu.SemaphoreType.DMA((rows_dev // ROW_STEP,)),
         ],
+        out_space=pltpu.HBM,
     )(*(in_hbm(a) for a in (dest, embed)))
     quad, linear, offset = call(
         weight_kernel, (weight, weight, jax.ShapeDtypeStruct((1, comp), F32)),

time: 177 us -> 177 us (level)
  no operation moved by 1% of the time
where the time goes in v8:
time: 177 us; the launch traced here: 175 us
  blocking collectives  137 us (77%)
  waiting for transfers between devices  19.6 us (11%)
  Pallas kernels  9.73 us (5%)
  starting transfers between devices  5.79 us (3%)
  other arithmetic  2.16 us (1%)
    all_to_all x3, blocking collectives, on_device(): got = everyone(sent)  66.2 us
    all_to_all x1, blocking collectives, on_device(): everyone(jnp.broadcast_to(done[None], (deep,) + done.shape), axis_index_g...  21.4 us
    all_to_all x1, blocking collectives, on_device(): everyone(sent.reshape(deep, quarter // deep, sent.shape[1]), axis_index_g...  20.1 us
    all_to_all x1, waiting for transfers between devices, on_device(): lax.all_to_all(ordered.reshape(groups, block, width), 'narrow', split_axi...  19.6 us
    all_to_all x1, blocking collectives, on_device(): got = everyone(sent, axis_index_groups=blocks)  15.7 us
    all_to_all x1, blocking collectives, on_device(): everyone(jnp.broadcast_to(here, (4,) + here.shape[1:]), axis_index_groups...  13.8 us
    all_to_all x1, starting transfers between devices, on_device(): lax.all_to_all(ordered.reshape(groups, block, width), 'narrow', split_axi...  5.79 us
    pallas_call x1, Pallas kernels, on_device(): call(functools.partial(order_kernel, groups), plain, 0, 2 * rows_dev * bi...  3.64 us
  transfers between devices with their start and end apart: 1, of which 1 were waited for; matrix products, arithmetic and copies ran while one was open for 0% of the time, Pallas kernels for 1%

profile of v8, /device:TPU:24, one launch (start us, length us, event | category | flops | bytes accessed | tf_op | source)
XLA Modules:
  0.0 175.3 jit_solution(11432754169343667112)
XLA Ops:
  0.6 3.6 %shard_map.59 = bf16[768,1024]{1,0:T(8,128)(2,1)} custom-call(s32[768]{0:T(1024)} %dest_hbm.1, bf16[768,1024]{1,0:T(8,128)(2,1)} %embed_hbm.1), custom_call_target="tpu_custom_call" | custom-call | flops 1207959552 | bytes 3145728 | tf_op jit(solution)/shard_map/pallas_call | solution.py:229
  4.3 5.8 %all-to-all-start = ((bf16[16,48,1024]{2,1,0:T(8,128)(2,1)}), bf16[16,48,1024]{2,1,0:T(8,128)(2,1)S(1)}, u32[]{:S(2)}, u32[]{:S(2)}) async-start(bf16[16,48,1024]{2,1,0:T(8,128)(2,1)} %bitcast), calls=%async_computation | async-start | bytes 3145728 | tf_op jit(solution)/shard_map/all_to_all | solution.py:249
  10.1 1.7 shard_map.60
  11.7 19.6 %all-to-all-done = bf16[16,48,1024]{2,1,0:T(8,128)(2,1)S(1)} async-done(((bf16[16,48,1024]{2,1,0:T(8,128)(2,1)}), bf16[16,48,1024]{2,1,0:T(8,128)(2,1)S(1)}, u32[]{:S(2)}, u32[]{:S(2)}) %all-to-all-start) | async-done | bytes 1572896 | tf_op jit(solution)/shard_map/all_to_all | solution.py:249
  31.3 1.3 shard_map.61
  32.6 30.5 %all_to_all.40.got_ref = f32[32,2,128]{2,1,0:T(2,128)S(1)} all-to-all(f32[32,2,128]{2,1,0:T(2,128)S(1)} %get-tuple-element.16), channel_id=1, replica_groups=mesh['wide'=32,'narrow'=16] {'wide'}, dimensions={0} | all-to-all | bytes 65536 | tf_op jit(solution)/shard_map/all_to_all | solution.py:256
  63.1 0.3 shard_map.62
  63.4 17.8 %all_to_all.41.got_ref = f32[32,2,128]{2,1,0:T(2,128)S(1)} all-to-all(f32[32,2,128]{2,1,0:T(2,128)S(1)} %get-tuple-element.18), channel_id=1, replica_groups=mesh['wide'=32,'narrow'=16] {'wide'}, dimensions={0} | all-to-all | bytes 65536 | tf_op jit(solution)/shard_map/all_to_all | solution.py:262
  81.2 0.3 shard_map.63
  81.5 17.8 %all_to_all.42.got_ref = f32[32,2,128]{2,1,0:T(2,128)S(1)} all-to-all(f32[32,2,128]{2,1,0:T(2,128)S(1)} %get-tuple-element.20), channel_id=1, replica_groups=mesh['wide'=32,'narrow'=16] {'wide'}, dimensions={0} | all-to-all | bytes 65536 | tf_op jit(solution)/shard_map/all_to_all | solution.py:262
  99.3 2.6 %shard_map.64 = f32[256,2176]{1,0:T(8,128)S(1)} custom-call(f32[32,2,128]{2,1,0:T(2,128)S(1)} %all_to_all.42.got_ref, f32[768,256]{1,0:T(8,128)S(1)} %get-tuple-element.21.resp_ref, bf16[768,1024]{1,0:T(8,128)(2,1)S(1)} %bitcast.8, bf16[768,1024]{1,0:T(8,128)(2,1)S(1)} %get-tuple-element.22.high_ref, bf16[768,1024]{1,0:T(8,128)(2,1)S(1)} %get-tuple-element.23.low_ref), custom_call_target="tpu_custom_call" | custom-call | flops 2013265920 | bytes 6291456 | tf_op jit(solution)/shard_map/pallas_call | solution.py:263
  101.9 0.1 convert_element_type.27
  102.0 15.7 %all_to_all.43 = f16[4,64,2176]{2,1,0:T(8,128)(2,1)S(1)} all-to-all(f16[4,64,2176]{2,1,0:T(8,128)(2,1)S(1)} %bitcast.9), channel_id=1, replica_groups={{0,16,32,48},{64,80,96,112},{128,144,160,176},{192,208,224,240},{256,27..., dimensions={0} | all-to-all | bytes 2228224 | tf_op jit(solution)/shard_map/all_to_all | solution.py:269
  117.8 0.1 convert_reduce_fusion
  117.9 0.1 fusion
  118.0 20.1 %all_to_all.44 = f16[8,8,2176]{2,1,0:T(8,128)(2,1)S(1)} all-to-all(f16[8,8,2176]{2,1,0:T(8,128)(2,1)S(1)} %fusion), channel_id=1, replica_groups={{0,64,128,192,256,320,384,448},{16,80,144,208,272,336,400,464},{32,96,1..., dimensions={0} | all-to-all | bytes 557056 | tf_op jit(solution)/shard_map/all_to_all | solution.py:271
  138.1 0.2 fusion.5
  138.3 0.1 fusion.8
  138.5 21.4 %all_to_all.45 = f16[8,8,2048]{2,1,0:T(8,128)(2,1)S(1)} all-to-all(f16[8,8,2048]{2,1,0:T(8,128)(2,1)S(1)} %broadcast_in_dim.6), channel_id=1, replica_groups={{0,64,128,192,256,320,384,448},{16,80,144,208,272,336,400,464},{32,96,1..., dimensions={0} | all-to-all | bytes 524288 | tf_op jit(solution)/shard_map/all_to_all | solution.py:279
  159.9 0.1 broadcast_in_dim.15
  160.0 13.8 %all_to_all.46 = f16[4,64,2048]{2,1,0:T(8,128)(2,1)S(1)} all-to-all(f16[4,64,2048]{2,1,0:T(8,128)(2,1)S(1)} %broadcast_in_dim.15), channel_id=1, replica_groups={{0,16,32,48},{64,80,96,112},{128,144,160,176},{192,208,224,240},{256,27..., dimensions={0} | all-to-all | bytes 2097152 | tf_op jit(solution)/shard_map/all_to_all | solution.py:281
  173.8 1.5 slice_convert_fusion
  (3 shorter events, 0.1 us)
Async XLA Ops:
  4.3 27.0 %all-to-all-start = ((bf16[16,48,1024]{2,1,0:T(8,128)(2,1)}), bf16[16,48,1024]{2,1,0:T(8,128)(2,1)S(1)}, u32[]{:S(2)}, u32[]{:S(2)}) async-start(bf16[16,48,1024]{2,1,0:T(8,128)(2,1)} %bitcast), calls=%async_computation | async-start | bytes 3145728 | tf_op jit(solution)/shard_map/all_to_all | solution.py:249

commit v9 on v6

--- a/solution.py
+++ b/solution.py
@@ -248,8 +248,8 @@
     got = everyone(jnp.broadcast_to(done[None], (deep,) + done.shape), axis_index_groups=lines)
     here = got.reshape(1, quarter, 2 * width)
     got = everyone(jnp.broadcast_to(here, (4,) + here.shape[1:]), axis_index_groups=blocks)
-    out = got.reshape(comp, 2 * width).astype(F32)
-    return (out[:, :width], out[:, width:])
+    out = lax.optimization_barrier(got.reshape(comp, 2 * width))
+    return (out[:, :width].astype(F32), out[:, width:].astype(F32))
 
 
 def solution(mesh):

time: 176 us -> 176 us (level)
  no operation moved by 1% of the time
where the time goes in v9:
time: 176 us; the launch traced here: 174 us
  blocking collectives  163 us (93%)
  Pallas kernels  7.55 us (4%)
  other arithmetic  2.16 us (1%)
    all_to_all x3, blocking collectives, on_device(): got = everyone(sent)  66.2 us
    all_to_all x1, blocking collectives, on_device(): lax.all_to_all(ordered.reshape(groups, block, width), 'narrow', split_axi...  26.1 us
    all_to_all x1, blocking collectives, on_device(): everyone(jnp.broadcast_to(done[None], (deep,) + done.shape), axis_index_g...  21.4 us
    all_to_all x1, blocking collectives, on_device(): everyone(sent.reshape(deep, quarter // deep, sent.shape[1]), axis_index_g...  20.1 us
    all_to_all x1, blocking collectives, on_device(): got = everyone(sent, axis_index_groups=blocks)  15.7 us
    all_to_all x1, blocking collectives, on_device(): everyone(jnp.broadcast_to(here, (4,) + here.shape[1:]), axis_index_groups...  13.8 us

profile of v9, /device:TPU:24, one launch (start us, length us, event | category | flops | bytes accessed | tf_op | source)
XLA Modules:
  0.0 173.9 jit_solution(17056517286592469200)
XLA Ops:
  0.6 3.1 %shard_map.59 = (bf16[768,1024]{1,0:T(8,128)(2,1)S(1)}, bf16[256,1024]{1,0:T(8,128)(2,1)S(1)}, bf16[256,1024]{1,0:T(8,128)(2,1)S(1)}, f32[1,256]{1,0:T(1,128)S(1)}) custom-call(s32[768]{0:T(1024)} %dest_hbm.1, bf16[256,1024]{1,0:T(8,128)(2,1)} %var_hbm.1, bf16[256,1024]{1,0:T(8,128)(2,1)} %mean_hbm.1, bf16[768,1024]{1,0:T(8,128)(2,1)} %embed_hbm.1), custom_call_target="tpu_custom_call" | custom-call | flops 1207959552 | bytes 3145728 | tf_op jit(solution)/shard_map/pallas_call | solution.py:206
  3.8 26.1 %all_to_all.40 = bf16[16,48,1024]{2,1,0:T(8,128)(2,1)S(1)} all-to-all(bf16[16,48,1024]{2,1,0:T(8,128)(2,1)S(1)} %bitcast.9), channel_id=1, replica_groups=mesh['wide'=32,'narrow'=16] {'narrow'}, dimensions={0} | all-to-all | bytes 3145728 | tf_op jit(solution)/shard_map/all_to_all | solution.py:218
  29.9 1.3 shard_map.60
  31.2 30.5 %all_to_all.41.got_ref = f32[32,2,128]{2,1,0:T(2,128)S(1)} all-to-all(f32[32,2,128]{2,1,0:T(2,128)S(1)} %get-tuple-element.18), channel_id=1, replica_groups=mesh['wide'=32,'narrow'=16] {'wide'}, dimensions={0} | all-to-all | bytes 65536 | tf_op jit(solution)/shard_map/all_to_all | solution.py:225
  61.7 0.3 shard_map.61
  62.0 17.8 %all_to_all.42.got_ref = f32[32,2,128]{2,1,0:T(2,128)S(1)} all-to-all(f32[32,2,128]{2,1,0:T(2,128)S(1)} %get-tuple-element.20), channel_id=1, replica_groups=mesh['wide'=32,'narrow'=16] {'wide'}, dimensions={0} | all-to-all | bytes 65536 | tf_op jit(solution)/shard_map/all_to_all | solution.py:231
  79.8 0.3 shard_map.62
  80.1 17.8 %all_to_all.43.got_ref = f32[32,2,128]{2,1,0:T(2,128)S(1)} all-to-all(f32[32,2,128]{2,1,0:T(2,128)S(1)} %get-tuple-element.22), channel_id=1, replica_groups=mesh['wide'=32,'narrow'=16] {'wide'}, dimensions={0} | all-to-all | bytes 65536 | tf_op jit(solution)/shard_map/all_to_all | solution.py:231
  97.9 2.6 %shard_map.63 = f32[256,2176]{1,0:T(8,128)S(1)} custom-call(f32[32,2,128]{2,1,0:T(2,128)S(1)} %all_to_all.43.got_ref, f32[768,256]{1,0:T(8,128)S(1)} %get-tuple-element.23.resp_ref, bf16[768,1024]{1,0:T(8,128)(2,1)S(1)} %bitcast.8, bf16[768,1024]{1,0:T(8,128)(2,1)S(1)} %get-tuple-element.24.high_ref, bf16[768,1024]{1,0:T(8,128)(2,1)S(1)} %get-tuple-element.25.low_ref), custom_call_target="tpu_custom_call" | custom-call | flops 2013265920 | bytes 6291456 | tf_op jit(solution)/shard_map/pallas_call | solution.py:232
  100.5 0.1 convert_element_type.27
  100.6 15.7 %all_to_all.44 = f16[4,64,2176]{2,1,0:T(8,128)(2,1)S(1)} all-to-all(f16[4,64,2176]{2,1,0:T(8,128)(2,1)S(1)} %bitcast.10), channel_id=1, replica_groups={{0,16,32,48},{64,80,96,112},{128,144,160,176},{192,208,224,240},{256,27..., dimensions={0} | all-to-all | bytes 2228224 | tf_op jit(solution)/shard_map/all_to_all | solution.py:238
  116.4 0.1 convert_reduce_fusion
  116.5 0.1 fusion
  116.6 20.1 %all_to_all.45 = f16[8,8,2176]{2,1,0:T(8,128)(2,1)S(1)} all-to-all(f16[8,8,2176]{2,1,0:T(8,128)(2,1)S(1)} %fusion), channel_id=1, replica_groups={{0,64,128,192,256,320,384,448},{16,80,144,208,272,336,400,464},{32,96,1..., dimensions={0} | all-to-all | bytes 557056 | tf_op jit(solution)/shard_map/all_to_all | solution.py:240
  136.7 0.2 fusion.5
  136.9 0.1 fusion.8
  137.1 21.4 %all_to_all.46 = f16[8,8,2048]{2,1,0:T(8,128)(2,1)S(1)} all-to-all(f16[8,8,2048]{2,1,0:T(8,128)(2,1)S(1)} %broadcast_in_dim.6), channel_id=1, replica_groups={{0,64,128,192,256,320,384,448},{16,80,144,208,272,336,400,464},{32,96,1..., dimensions={0} | all-to-all | bytes 524288 | tf_op jit(solution)/shard_map/all_to_all | solution.py:248
  158.5 0.1 broadcast_in_dim.15
  158.6 13.8 %all_to_all.47 = f16[4,64,2048]{2,1,0:T(8,128)(2,1)S(1)} all-to-all(f16[4,64,2048]{2,1,0:T(8,128)(2,1)S(1)} %broadcast_in_dim.15), channel_id=1, replica_groups={{0,16,32,48},{64,80,96,112},{128,144,160,176},{192,208,224,240},{256,27..., dimensions={0} | all-to-all | bytes 2097152 | tf_op jit(solution)/shard_map/all_to_all | solution.py:250
  172.4 1.5 slice_convert_fusion
  (3 shorter events, 0.1 us)

commit v10 on v9

--- a/solution.py
+++ b/solution.py
@@ -153,31 +153,26 @@
     )
 
 
-def put_moments(both, x_ref, high_ref, low_ref, out_ref):
-    part = out_ref.shape[0]
+def moment_kernel(target, got_ref, resp_ref, x_ref, high_ref, low_ref, out_ref, both_ref):
+    rows, comp = resp_ref.shape
     width = x_ref.shape[1]
-    first = dot_tn(both, x_ref[...])
-    out_ref[:, :width] = first[:part] + first[part:]
-    second = dot_tn(both, high_ref[...])
-    out_ref[:, width : 2 * width] = (
-        second[:part] + second[part:] + dot_tn(both[:, :part], low_ref[...])
-    )
-    total = dot_tn(both, jnp.ones((both.shape[0], LANES), BF16))
-    out_ref[:, 2 * width :] = total_parts(total[:part] + total[part:])
-
-
-def moment_kernel(
-    target, got_ref, resp_ref, x_ref, high_ref, low_ref, out_ref, both_ref
-):
-    rows, comp = resp_ref.shape
     pull = target / get_mass(got_ref)
+    total = jnp.zeros((1, comp), F32)
     for start in range(0, rows, ROW_STEP):
         span = slice(start, start + ROW_STEP)
         resp = balance_step(resp_ref[span, :], pull)
         high = resp.astype(BF16)
         both_ref[span, :comp] = high
         both_ref[span, comp:] = (resp - high.astype(F32)).astype(BF16)
-    put_moments(both_ref[...], x_ref, high_ref, low_ref, out_ref)
+        total = total + jnp.sum(resp, axis=0, keepdims=True)
+    both = both_ref[...]
+    first = dot_tn(both, x_ref[...])
+    out_ref[:, :width] = first[:comp] + first[comp:]
+    second = dot_tn(both, high_ref[...])
+    out_ref[:, width : 2 * width] = (
+        second[:comp] + second[comp:] + dot_tn(both[:, :comp], low_ref[...])
+    )
+    out_ref[:, 2 * width :] = total_parts(jnp.transpose(jnp.broadcast_to(total, (LANES, comp))))
 
 
 def on_device(embed, dest, means, variances):

time: 176 us -> 176 us (level)
    all_to_all x1, blocking collectives: 21.4 us -> 18.8 us  [on_device(): everyone(jnp.broadcast_to(done[None], (deep,) + done.shape), axis_index_g...]
    all_to_all x1, blocking collectives: 13.8 us -> 16.3 us  [on_device(): everyone(jnp.broadcast_to(here, (4,) + here.shape[1:]), axis_index_groups...]
where the time goes in v10:
time: 176 us; the launch traced here: 174 us
  blocking collectives  163 us (93%)
  Pallas kernels  7.38 us (4%)
  other arithmetic  2.16 us (1%)
    all_to_all x3, blocking collectives, on_device(): got = everyone(sent)  66.2 us
    all_to_all x1, blocking collectives, on_device(): lax.all_to_all(ordered.reshape(groups, block, width), 'narrow', split_axi...  26.1 us
    all_to_all x1, blocking collectives, on_device(): everyone(sent.reshape(deep, quarter // deep, sent.shape[1]), axis_index_g...  20.1 us
    all_to_all x1, blocking collectives, on_device(): everyone(jnp.broadcast_to(done[None], (deep,) + done.shape), axis_index_g...  18.8 us
    all_to_all x1, blocking collectives, on_device(): everyone(jnp.broadcast_to(here, (4,) + here.shape[1:]), axis_index_groups...  16.3 us
    all_to_all x1, blocking collectives, on_device(): got = everyone(sent, axis_index_groups=blocks)  15.7 us

profile of v10, /device:TPU:24, one launch (start us, length us, event | category | flops | bytes accessed | tf_op | source)
XLA Modules:
  0.0 173.7 jit_solution(15982970999165377594)
XLA Ops:
  0.6 3.1 %shard_map.59 = (bf16[768,1024]{1,0:T(8,128)(2,1)S(1)}, bf16[256,1024]{1,0:T(8,128)(2,1)S(1)}, bf16[256,1024]{1,0:T(8,128)(2,1)S(1)}, f32[1,256]{1,0:T(1,128)S(1)}) custom-call(s32[768]{0:T(1024)} %dest_hbm.1, bf16[256,1024]{1,0:T(8,128)(2,1)} %var_hbm.1, bf16[256,1024]{1,0:T(8,128)(2,1)} %mean_hbm.1, bf16[768,1024]{1,0:T(8,128)(2,1)} %embed_hbm.1), custom_call_target="tpu_custom_call" | custom-call | flops 1207959552 | bytes 3145728 | tf_op jit(solution)/shard_map/pallas_call | solution.py:201
  3.8 26.1 %all_to_all.40 = bf16[16,48,1024]{2,1,0:T(8,128)(2,1)S(1)} all-to-all(bf16[16,48,1024]{2,1,0:T(8,128)(2,1)S(1)} %bitcast.9), channel_id=1, replica_groups=mesh['wide'=32,'narrow'=16] {'narrow'}, dimensions={0} | all-to-all | bytes 3145728 | tf_op jit(solution)/shard_map/all_to_all | solution.py:213
  29.9 1.3 shard_map.60
  31.2 30.5 %all_to_all.41.got_ref = f32[32,2,128]{2,1,0:T(2,128)S(1)} all-to-all(f32[32,2,128]{2,1,0:T(2,128)S(1)} %get-tuple-element.18), channel_id=1, replica_groups=mesh['wide'=32,'narrow'=16] {'wide'}, dimensions={0} | all-to-all | bytes 65536 | tf_op jit(solution)/shard_map/all_to_all | solution.py:220
  61.7 0.3 shard_map.61
  62.0 17.8 %all_to_all.42.got_ref = f32[32,2,128]{2,1,0:T(2,128)S(1)} all-to-all(f32[32,2,128]{2,1,0:T(2,128)S(1)} %get-tuple-element.20), channel_id=1, replica_groups=mesh['wide'=32,'narrow'=16] {'wide'}, dimensions={0} | all-to-all | bytes 65536 | tf_op jit(solution)/shard_map/all_to_all | solution.py:226
  79.8 0.3 shard_map.62
  80.1 17.8 %all_to_all.43.got_ref = f32[32,2,128]{2,1,0:T(2,128)S(1)} all-to-all(f32[32,2,128]{2,1,0:T(2,128)S(1)} %get-tuple-element.22), channel_id=1, replica_groups=mesh['wide'=32,'narrow'=16] {'wide'}, dimensions={0} | all-to-all | bytes 65536 | tf_op jit(solution)/shard_map/all_to_all | solution.py:226
  97.9 2.4 %shard_map.63 = f32[256,2176]{1,0:T(8,128)S(1)} custom-call(f32[32,2,128]{2,1,0:T(2,128)S(1)} %all_to_all.43.got_ref, f32[768,256]{1,0:T(8,128)S(1)} %get-tuple-element.23.resp_ref, bf16[768,1024]{1,0:T(8,128)(2,1)S(1)} %bitcast.8, bf16[768,1024]{1,0:T(8,128)(2,1)S(1)} %get-tuple-element.24.high_ref, bf16[768,1024]{1,0:T(8,128)(2,1)S(1)} %get-tuple-element.25.low_ref), custom_call_target="tpu_custom_call" | custom-call | flops 2013265920 | bytes 6291456 | tf_op jit(solution)/shard_map/pallas_call | solution.py:227
  100.3 0.1 convert_element_type.27
  100.5 15.7 %all_to_all.44 = f16[4,64,2176]{2,1,0:T(8,128)(2,1)S(1)} all-to-all(f16[4,64,2176]{2,1,0:T(8,128)(2,1)S(1)} %bitcast.10), channel_id=1, replica_groups={{0,16,32,48},{64,80,96,112},{128,144,160,176},{192,208,224,240},{256,27..., dimensions={0} | all-to-all | bytes 2228224 | tf_op jit(solution)/shard_map/all_to_all | solution.py:233
  116.2 0.1 convert_reduce_fusion
  116.4 0.1 fusion
  116.4 20.1 %all_to_all.45 = f16[8,8,2176]{2,1,0:T(8,128)(2,1)S(1)} all-to-all(f16[8,8,2176]{2,1,0:T(8,128)(2,1)S(1)} %fusion), channel_id=1, replica_groups={{0,64,128,192,256,320,384,448},{16,80,144,208,272,336,400,464},{32,96,1..., dimensions={0} | all-to-all | bytes 557056 | tf_op jit(solution)/shard_map/all_to_all | solution.py:235
  136.6 0.2 fusion.5
  136.8 0.1 fusion.8
  136.9 18.8 %all_to_all.46 = f16[8,8,2048]{2,1,0:T(8,128)(2,1)S(1)} all-to-all(f16[8,8,2048]{2,1,0:T(8,128)(2,1)S(1)} %broadcast_in_dim.6), channel_id=1, replica_groups={{0,64,128,192,256,320,384,448},{16,80,144,208,272,336,400,464},{32,96,1..., dimensions={0} | all-to-all | bytes 524288 | tf_op jit(solution)/shard_map/all_to_all | solution.py:243
  155.7 0.1 broadcast_in_dim.15
  155.9 16.3 %all_to_all.47 = f16[4,64,2048]{2,1,0:T(8,128)(2,1)S(1)} all-to-all(f16[4,64,2048]{2,1,0:T(8,128)(2,1)S(1)} %broadcast_in_dim.15), channel_id=1, replica_groups={{0,16,32,48},{64,80,96,112},{128,144,160,176},{192,208,224,240},{256,27..., dimensions={0} | all-to-all | bytes 2097152 | tf_op jit(solution)/shard_map/all_to_all | solution.py:245
  172.2 1.5 slice_convert_fusion
  (3 shorter events, 0.1 us)

commit v11 on v10

--- a/solution.py
+++ b/solution.py
@@ -231,9 +231,9 @@
     )(got, resp, mine, high, low)
     sent = sums.astype(jnp.float16).reshape(4, quarter, sums.shape[1])
     got = everyone(sent, axis_index_groups=blocks)
-    sent = (SAFE * jnp.sum(got.astype(F32), axis=0)).astype(jnp.float16)
+    sent = (SAFE * sum(got[i].astype(F32) for i in range(4))).astype(jnp.float16)
     got = everyone(sent.reshape(deep, quarter // deep, sent.shape[1]), axis_index_groups=lines)
-    got = jnp.sum(got.astype(F32), axis=0)
+    got = sum(got[i].astype(F32) for i in range(deep))
     first, second = got[:, :width], got[:, width : 2 * width]
     units = (8.0, 2.0**-6, 2.0**-15, 2.0**-15)
     total = sum(u * got[:, 2 * width + 32 * i :][:, :1] for i, u in enumerate(units))

time: 176 us -> 175 us (level)
  no operation moved by 1% of the time
where the time goes in v11:
time: 175 us; the launch traced here: 174 us
  blocking collectives  163 us (93%)
  Pallas kernels  7.38 us (4%)
  other arithmetic  2.14 us (1%)
    all_to_all x3, blocking collectives, on_device(): got = everyone(sent)  66.2 us
    all_to_all x1, blocking collectives, on_device(): lax.all_to_all(ordered.reshape(groups, block, width), 'narrow', split_axi...  26.1 us
    all_to_all x1, blocking collectives, on_device(): everyone(sent.reshape(deep, quarter // deep, sent.shape[1]), axis_index_g...  20.1 us
    all_to_all x1, blocking collectives, on_device(): everyone(jnp.broadcast_to(done[None], (deep,) + done.shape), axis_index_g...  18.8 us
    all_to_all x1, blocking collectives, on_device(): everyone(jnp.broadcast_to(here, (4,) + here.shape[1:]), axis_index_groups...  16.3 us
    all_to_all x1, blocking collectives, on_device(): got = everyone(sent, axis_index_groups=blocks)  15.7 us

profile of v11, /device:TPU:24, one launch (start us, length us, event | category | flops | bytes accessed | tf_op | source)
XLA Modules:
  0.0 173.7 jit_solution(17332191164779715161)
XLA Ops:
  0.6 3.1 %shard_map.59 = (bf16[768,1024]{1,0:T(8,128)(2,1)S(1)}, bf16[256,1024]{1,0:T(8,128)(2,1)S(1)}, bf16[256,1024]{1,0:T(8,128)(2,1)S(1)}, f32[1,256]{1,0:T(1,128)S(1)}) custom-call(s32[768]{0:T(1024)} %dest_hbm.1, bf16[256,1024]{1,0:T(8,128)(2,1)} %var_hbm.1, bf16[256,1024]{1,0:T(8,128)(2,1)} %mean_hbm.1, bf16[768,1024]{1,0:T(8,128)(2,1)} %embed_hbm.1), custom_call_target="tpu_custom_call" | custom-call | flops 1207959552 | bytes 3145728 | tf_op jit(solution)/shard_map/pallas_call | solution.py:201
  3.8 26.1 %all_to_all.40 = bf16[16,48,1024]{2,1,0:T(8,128)(2,1)S(1)} all-to-all(bf16[16,48,1024]{2,1,0:T(8,128)(2,1)S(1)} %bitcast.11), channel_id=1, replica_groups=mesh['wide'=32,'narrow'=16] {'narrow'}, dimensions={0} | all-to-all | bytes 3145728 | tf_op jit(solution)/shard_map/all_to_all | solution.py:213
  29.9 1.3 shard_map.60
  31.2 30.5 %all_to_all.41.got_ref = f32[32,2,128]{2,1,0:T(2,128)S(1)} all-to-all(f32[32,2,128]{2,1,0:T(2,128)S(1)} %get-tuple-element.18), channel_id=1, replica_groups=mesh['wide'=32,'narrow'=16] {'wide'}, dimensions={0} | all-to-all | bytes 65536 | tf_op jit(solution)/shard_map/all_to_all | solution.py:220
  61.7 0.3 shard_map.61
  62.0 17.8 %all_to_all.42.got_ref = f32[32,2,128]{2,1,0:T(2,128)S(1)} all-to-all(f32[32,2,128]{2,1,0:T(2,128)S(1)} %get-tuple-element.20), channel_id=1, replica_groups=mesh['wide'=32,'narrow'=16] {'wide'}, dimensions={0} | all-to-all | bytes 65536 | tf_op jit(solution)/shard_map/all_to_all | solution.py:226
  79.8 0.3 shard_map.62
  80.1 17.8 %all_to_all.43.got_ref = f32[32,2,128]{2,1,0:T(2,128)S(1)} all-to-all(f32[32,2,128]{2,1,0:T(2,128)S(1)} %get-tuple-element.22), channel_id=1, replica_groups=mesh['wide'=32,'narrow'=16] {'wide'}, dimensions={0} | all-to-all | bytes 65536 | tf_op jit(solution)/shard_map/all_to_all | solution.py:226
  97.9 2.4 %shard_map.63 = f32[256,2176]{1,0:T(8,128)S(1)} custom-call(f32[32,2,128]{2,1,0:T(2,128)S(1)} %all_to_all.43.got_ref, f32[768,256]{1,0:T(8,128)S(1)} %get-tuple-element.23.resp_ref, bf16[768,1024]{1,0:T(8,128)(2,1)S(1)} %bitcast.10, bf16[768,1024]{1,0:T(8,128)(2,1)S(1)} %get-tuple-element.24.high_ref, bf16[768,1024]{1,0:T(8,128)(2,1)S(1)} %get-tuple-element.25.low_ref), custom_call_target="tpu_custom_call" | custom-call | flops 2013265920 | bytes 6291456 | tf_op jit(solution)/shard_map/pallas_call | solution.py:227
  100.3 0.1 convert_element_type.78
  100.5 15.7 %all_to_all.44 = f16[4,64,2176]{2,1,0:T(8,128)(2,1)S(1)} all-to-all(f16[4,64,2176]{2,1,0:T(8,128)(2,1)S(1)} %bitcast.12), channel_id=1, replica_groups={{0,16,32,48},{64,80,96,112},{128,144,160,176},{192,208,224,240},{256,27..., dimensions={0} | all-to-all | bytes 2228224 | tf_op jit(solution)/shard_map/all_to_all | solution.py:233
  116.2 0.2 fusion
  116.4 20.1 %all_to_all.45 = f16[8,8,2176]{2,1,0:T(8,128)(2,1)S(1)} all-to-all(f16[8,8,2176]{2,1,0:T(8,128)(2,1)S(1)} %fusion), channel_id=1, replica_groups={{0,64,128,192,256,320,384,448},{16,80,144,208,272,336,400,464},{32,96,1..., dimensions={0} | all-to-all | bytes 557056 | tf_op jit(solution)/shard_map/all_to_all | solution.py:235
  136.5 0.2 fusion.5
  136.7 0.1 fusion.8
  136.9 18.8 %all_to_all.46 = f16[8,8,2048]{2,1,0:T(8,128)(2,1)S(1)} all-to-all(f16[8,8,2048]{2,1,0:T(8,128)(2,1)S(1)} %broadcast_in_dim.6), channel_id=1, replica_groups={{0,64,128,192,256,320,384,448},{16,80,144,208,272,336,400,464},{32,96,1..., dimensions={0} | all-to-all | bytes 524288 | tf_op jit(solution)/shard_map/all_to_all | solution.py:243
  155.7 0.1 broadcast_in_dim.15
  155.8 16.3 %all_to_all.47 = f16[4,64,2048]{2,1,0:T(8,128)(2,1)S(1)} all-to-all(f16[4,64,2048]{2,1,0:T(8,128)(2,1)S(1)} %broadcast_in_dim.15), channel_id=1, replica_groups={{0,16,32,48},{64,80,96,112},{128,144,160,176},{192,208,224,240},{256,27..., dimensions={0} | all-to-all | bytes 2097152 | tf_op jit(solution)/shard_map/all_to_all | solution.py:245
  172.2 1.5 slice_convert_fusion
  (3 shorter events, 0.1 us)

commit v12 on v9

--- a/solution.py
+++ b/solution.py
@@ -236,9 +236,9 @@
     )(got, resp, mine, high, low)
     sent = sums.astype(jnp.float16).reshape(4, quarter, sums.shape[1])
     got = everyone(sent, axis_index_groups=blocks)
-    sent = (SAFE * jnp.sum(got.astype(F32), axis=0)).astype(jnp.float16)
+    sent = (SAFE * sum(got[i].astype(F32) for i in range(4))).astype(jnp.float16)
     got = everyone(sent.reshape(deep, quarter // deep, sent.shape[1]), axis_index_groups=lines)
-    got = jnp.sum(got.astype(F32), axis=0)
+    got = sum(got[i].astype(F32) for i in range(deep))
     first, second = got[:, :width], got[:, width : 2 * width]
     units = (8.0, 2.0**-6, 2.0**-15, 2.0**-15)
     total = sum(u * got[:, 2 * width + 32 * i :][:, :1] for i, u in enumerate(units))

time: 176 us -> 176 us (level)
  no operation moved by 1% of the time
where the time goes in v12:
time: 176 us; the launch traced here: 174 us
  blocking collectives  163 us (93%)
  Pallas kernels  7.55 us (4%)
  other arithmetic  2.14 us (1%)
    all_to_all x3, blocking collectives, on_device(): got = everyone(sent)  66.2 us
    all_to_all x1, blocking collectives, on_device(): lax.all_to_all(ordered.reshape(groups, block, width), 'narrow', split_axi...  26.1 us
    all_to_all x1, blocking collectives, on_device(): everyone(jnp.broadcast_to(done[None], (deep,) + done.shape), axis_index_g...  21.4 us
    all_to_all x1, blocking collectives, on_device(): everyone(sent.reshape(deep, quarter // deep, sent.shape[1]), axis_index_g...  20.1 us
    all_to_all x1, blocking collectives, on_device(): got = everyone(sent, axis_index_groups=blocks)  15.7 us
    all_to_all x1, blocking collectives, on_device(): everyone(jnp.broadcast_to(here, (4,) + here.shape[1:]), axis_index_groups...  13.8 us

profile of v12, /device:TPU:24, one launch (start us, length us, event | category | flops | bytes accessed | tf_op | source)
XLA Modules:
  0.0 173.9 jit_solution(9550331387358887233)
XLA Ops:
  0.6 3.1 %shard_map.59 = (bf16[768,1024]{1,0:T(8,128)(2,1)S(1)}, bf16[256,1024]{1,0:T(8,128)(2,1)S(1)}, bf16[256,1024]{1,0:T(8,128)(2,1)S(1)}, f32[1,256]{1,0:T(1,128)S(1)}) custom-call(s32[768]{0:T(1024)} %dest_hbm.1, bf16[256,1024]{1,0:T(8,128)(2,1)} %var_hbm.1, bf16[256,1024]{1,0:T(8,128)(2,1)} %mean_hbm.1, bf16[768,1024]{1,0:T(8,128)(2,1)} %embed_hbm.1), custom_call_target="tpu_custom_call" | custom-call | flops 1207959552 | bytes 3145728 | tf_op jit(solution)/shard_map/pallas_call | solution.py:206
  3.8 26.1 %all_to_all.40 = bf16[16,48,1024]{2,1,0:T(8,128)(2,1)S(1)} all-to-all(bf16[16,48,1024]{2,1,0:T(8,128)(2,1)S(1)} %bitcast.11), channel_id=1, replica_groups=mesh['wide'=32,'narrow'=16] {'narrow'}, dimensions={0} | all-to-all | bytes 3145728 | tf_op jit(solution)/shard_map/all_to_all | solution.py:218
  29.9 1.3 shard_map.60
  31.2 30.5 %all_to_all.41.got_ref = f32[32,2,128]{2,1,0:T(2,128)S(1)} all-to-all(f32[32,2,128]{2,1,0:T(2,128)S(1)} %get-tuple-element.18), channel_id=1, replica_groups=mesh['wide'=32,'narrow'=16] {'wide'}, dimensions={0} | all-to-all | bytes 65536 | tf_op jit(solution)/shard_map/all_to_all | solution.py:225
  61.7 0.3 shard_map.61
  62.0 17.8 %all_to_all.42.got_ref = f32[32,2,128]{2,1,0:T(2,128)S(1)} all-to-all(f32[32,2,128]{2,1,0:T(2,128)S(1)} %get-tuple-element.20), channel_id=1, replica_groups=mesh['wide'=32,'narrow'=16] {'wide'}, dimensions={0} | all-to-all | bytes 65536 | tf_op jit(solution)/shard_map/all_to_all | solution.py:231
  79.8 0.3 shard_map.62
  80.1 17.8 %all_to_all.43.got_ref = f32[32,2,128]{2,1,0:T(2,128)S(1)} all-to-all(f32[32,2,128]{2,1,0:T(2,128)S(1)} %get-tuple-element.22), channel_id=1, replica_groups=mesh['wide'=32,'narrow'=16] {'wide'}, dimensions={0} | all-to-all | bytes 65536 | tf_op jit(solution)/shard_map/all_to_all | solution.py:231
  97.9 2.6 %shard_map.63 = f32[256,2176]{1,0:T(8,128)S(1)} custom-call(f32[32,2,128]{2,1,0:T(2,128)S(1)} %all_to_all.43.got_ref, f32[768,256]{1,0:T(8,128)S(1)} %get-tuple-element.23.resp_ref, bf16[768,1024]{1,0:T(8,128)(2,1)S(1)} %bitcast.10, bf16[768,1024]{1,0:T(8,128)(2,1)S(1)} %get-tuple-element.24.high_ref, bf16[768,1024]{1,0:T(8,128)(2,1)S(1)} %get-tuple-element.25.low_ref), custom_call_target="tpu_custom_call" | custom-call | flops 2013265920 | bytes 6291456 | tf_op jit(solution)/shard_map/pallas_call | solution.py:232
  100.5 0.1 convert_element_type.78
  100.6 15.7 %all_to_all.44 = f16[4,64,2176]{2,1,0:T(8,128)(2,1)S(1)} all-to-all(f16[4,64,2176]{2,1,0:T(8,128)(2,1)S(1)} %bitcast.12), channel_id=1, replica_groups={{0,16,32,48},{64,80,96,112},{128,144,160,176},{192,208,224,240},{256,27..., dimensions={0} | all-to-all | bytes 2228224 | tf_op jit(solution)/shard_map/all_to_all | solution.py:238
  116.4 0.2 fusion
  116.5 20.1 %all_to_all.45 = f16[8,8,2176]{2,1,0:T(8,128)(2,1)S(1)} all-to-all(f16[8,8,2176]{2,1,0:T(8,128)(2,1)S(1)} %fusion), channel_id=1, replica_groups={{0,64,128,192,256,320,384,448},{16,80,144,208,272,336,400,464},{32,96,1..., dimensions={0} | all-to-all | bytes 557056 | tf_op jit(solution)/shard_map/all_to_all | solution.py:240
  136.7 0.2 fusion.5
  136.9 0.1 fusion.8
  137.0 21.4 %all_to_all.46 = f16[8,8,2048]{2,1,0:T(8,128)(2,1)S(1)} all-to-all(f16[8,8,2048]{2,1,0:T(8,128)(2,1)S(1)} %broadcast_in_dim.6), channel_id=1, replica_groups={{0,64,128,192,256,320,384,448},{16,80,144,208,272,336,400,464},{32,96,1..., dimensions={0} | all-to-all | bytes 524288 | tf_op jit(solution)/shard_map/all_to_all | solution.py:248
  158.4 0.1 broadcast_in_dim.15
  158.6 13.8 %all_to_all.47 = f16[4,64,2048]{2,1,0:T(8,128)(2,1)S(1)} all-to-all(f16[4,64,2048]{2,1,0:T(8,128)(2,1)S(1)} %broadcast_in_dim.15), channel_id=1, replica_groups={{0,16,32,48},{64,80,96,112},{128,144,160,176},{192,208,224,240},{256,27..., dimensions={0} | all-to-all | bytes 2097152 | tf_op jit(solution)/shard_map/all_to_all | solution.py:250
  172.3 1.5 slice_convert_fusion
  (3 shorter events, 0.1 us)

commit v13 on v9

--- a/solution.py
+++ b/solution.py
@@ -9,7 +9,7 @@
 
 SINK = 3
 LANES = 128
-ROW_STEP = 256
+ROW_STEP = 384
 SAFE = 0.25
 F32 = jnp.float32
 BF16 = jnp.bfloat16

time: 176 us -> 176 us (level)
    all_to_all x1, blocking collectives: 21.4 us -> 19 us  [on_device(): everyone(jnp.broadcast_to(done[None], (deep,) + done.shape), axis_index_g...]
    all_to_all x1, blocking collectives: 13.8 us -> 16.2 us  [on_device(): everyone(jnp.broadcast_to(here, (4,) + here.shape[1:]), axis_index_groups...]
where the time goes in v13:
time: 176 us; the launch traced here: 174 us
  blocking collectives  163 us (93%)
  Pallas kernels  7.59 us (4%)
  other arithmetic  2.16 us (1%)
    all_to_all x3, blocking collectives, on_device(): got = everyone(sent)  66.2 us
    all_to_all x1, blocking collectives, on_device(): lax.all_to_all(ordered.reshape(groups, block, width), 'narrow', split_axi...  26.1 us
    all_to_all x1, blocking collectives, on_device(): everyone(sent.reshape(deep, quarter // deep, sent.shape[1]), axis_index_g...  20.1 us
    all_to_all x1, blocking collectives, on_device(): everyone(jnp.broadcast_to(done[None], (deep,) + done.shape), axis_index_g...  19 us
    all_to_all x1, blocking collectives, on_device(): everyone(jnp.broadcast_to(here, (4,) + here.shape[1:]), axis_index_groups...  16.2 us
    all_to_all x1, blocking collectives, on_device(): got = everyone(sent, axis_index_groups=blocks)  15.7 us

profile of v13, /device:TPU:24, one launch (start us, length us, event | category | flops | bytes accessed | tf_op | source)
XLA Modules:
  0.0 173.9 jit_solution(9527768769763049387)
XLA Ops:
  0.6 3.1 %shard_map.59 = (bf16[768,1024]{1,0:T(8,128)(2,1)S(1)}, bf16[256,1024]{1,0:T(8,128)(2,1)S(1)}, bf16[256,1024]{1,0:T(8,128)(2,1)S(1)}, f32[1,256]{1,0:T(1,128)S(1)}) custom-call(s32[768]{0:T(1024)} %dest_hbm.1, bf16[256,1024]{1,0:T(8,128)(2,1)} %var_hbm.1, bf16[256,1024]{1,0:T(8,128)(2,1)} %mean_hbm.1, bf16[768,1024]{1,0:T(8,128)(2,1)} %embed_hbm.1), custom_call_target="tpu_custom_call" | custom-call | flops 1207959552 | bytes 3145728 | tf_op jit(solution)/shard_map/pallas_call | solution.py:206
  3.8 26.1 %all_to_all.40 = bf16[16,48,1024]{2,1,0:T(8,128)(2,1)S(1)} all-to-all(bf16[16,48,1024]{2,1,0:T(8,128)(2,1)S(1)} %bitcast.9), channel_id=1, replica_groups=mesh['wide'=32,'narrow'=16] {'narrow'}, dimensions={0} | all-to-all | bytes 3145728 | tf_op jit(solution)/shard_map/all_to_all | solution.py:218
  29.9 1.4 shard_map.60
  31.2 30.5 %all_to_all.41.got_ref = f32[32,2,128]{2,1,0:T(2,128)S(1)} all-to-all(f32[32,2,128]{2,1,0:T(2,128)S(1)} %get-tuple-element.18), channel_id=1, replica_groups=mesh['wide'=32,'narrow'=16] {'wide'}, dimensions={0} | all-to-all | bytes 65536 | tf_op jit(solution)/shard_map/all_to_all | solution.py:225
  61.8 0.3 shard_map.61
  62.0 17.8 %all_to_all.42.got_ref = f32[32,2,128]{2,1,0:T(2,128)S(1)} all-to-all(f32[32,2,128]{2,1,0:T(2,128)S(1)} %get-tuple-element.20), channel_id=1, replica_groups=mesh['wide'=32,'narrow'=16] {'wide'}, dimensions={0} | all-to-all | bytes 65536 | tf_op jit(solution)/shard_map/all_to_all | solution.py:231
  79.8 0.3 shard_map.62
  80.1 17.8 %all_to_all.43.got_ref = f32[32,2,128]{2,1,0:T(2,128)S(1)} all-to-all(f32[32,2,128]{2,1,0:T(2,128)S(1)} %get-tuple-element.22), channel_id=1, replica_groups=mesh['wide'=32,'narrow'=16] {'wide'}, dimensions={0} | all-to-all | bytes 65536 | tf_op jit(solution)/shard_map/all_to_all | solution.py:231
  97.9 2.6 %shard_map.63 = f32[256,2176]{1,0:T(8,128)S(1)} custom-call(f32[32,2,128]{2,1,0:T(2,128)S(1)} %all_to_all.43.got_ref, f32[768,256]{1,0:T(8,128)S(1)} %get-tuple-element.23.resp_ref, bf16[768,1024]{1,0:T(8,128)(2,1)S(1)} %bitcast.8, bf16[768,1024]{1,0:T(8,128)(2,1)S(1)} %get-tuple-element.24.high_ref, bf16[768,1024]{1,0:T(8,128)(2,1)S(1)} %get-tuple-element.25.low_ref), custom_call_target="tpu_custom_call" | custom-call | flops 2013265920 | bytes 6291456 | tf_op jit(solution)/shard_map/pallas_call | solution.py:232
  100.5 0.1 convert_element_type.27
  100.7 15.7 %all_to_all.44 = f16[4,64,2176]{2,1,0:T(8,128)(2,1)S(1)} all-to-all(f16[4,64,2176]{2,1,0:T(8,128)(2,1)S(1)} %bitcast.10), channel_id=1, replica_groups={{0,16,32,48},{64,80,96,112},{128,144,160,176},{192,208,224,240},{256,27..., dimensions={0} | all-to-all | bytes 2228224 | tf_op jit(solution)/shard_map/all_to_all | solution.py:238
  116.4 0.1 convert_reduce_fusion
  116.5 0.1 fusion
  116.6 20.1 %all_to_all.45 = f16[8,8,2176]{2,1,0:T(8,128)(2,1)S(1)} all-to-all(f16[8,8,2176]{2,1,0:T(8,128)(2,1)S(1)} %fusion), channel_id=1, replica_groups={{0,64,128,192,256,320,384,448},{16,80,144,208,272,336,400,464},{32,96,1..., dimensions={0} | all-to-all | bytes 557056 | tf_op jit(solution)/shard_map/all_to_all | solution.py:240
  136.8 0.2 fusion.5
  137.0 0.1 fusion.8
  137.1 19.0 %all_to_all.46 = f16[8,8,2048]{2,1,0:T(8,128)(2,1)S(1)} all-to-all(f16[8,8,2048]{2,1,0:T(8,128)(2,1)S(1)} %broadcast_in_dim.6), channel_id=1, replica_groups={{0,64,128,192,256,320,384,448},{16,80,144,208,272,336,400,464},{32,96,1..., dimensions={0} | all-to-all | bytes 524288 | tf_op jit(solution)/shard_map/all_to_all | solution.py:248
  156.1 0.1 broadcast_in_dim.15
  156.2 16.2 %all_to_all.47 = f16[4,64,2048]{2,1,0:T(8,128)(2,1)S(1)} all-to-all(f16[4,64,2048]{2,1,0:T(8,128)(2,1)S(1)} %broadcast_in_dim.15), channel_id=1, replica_groups={{0,16,32,48},{64,80,96,112},{128,144,160,176},{192,208,224,240},{256,27..., dimensions={0} | all-to-all | bytes 2097152 | tf_op jit(solution)/shard_map/all_to_all | solution.py:250
  172.4 1.5 slice_convert_fusion
  (3 shorter events, 0.1 us)
